TPU v7x, 32 devices: a whole 2x2x4 slice. The times are simulated.
32 devices in a mesh: row: 4 (over y, x), col: 8 (over z, core).
Axes of the slice: x: 2, y: 2, z: 4, core: 2. Of those that a mesh axis runs over, the one named last changes fastest.
Arguments:
- factor: bfloat16 [7168, 7168], P('row', 'col'), may hold values from -2 to 2, as said below
- gradient: float32 [7168, 512], P(('row', 'col')), may hold values from -6 to 6
- starts: int32 [4], replicated, may hold values from 0 to 3, each once
Outputs:
- solved: float32 [7168, 512], P(('row', 'col'))
Inputs may be any that keep to these rules, and one draw needn't show every extreme that they name: `factor`: tiles above the block diagonal are zero, and every diagonal tile is upper triangular. `starts`: every block column is the start of exactly one panel.
All inputs are finite; a program needn't handle non-finite values.
Results may differ from a plain program's by a relative error of at most 0.0046.
Values may be sent and summed in bfloat16 or wider, within the bound.
No kernel may reach another device: no remote copies, remote signals or barrier semaphores. Data moves between devices by JAX's collectives and lax.ppermute only.
A program may use at most 64 MiB of HBM per device.

v0:
```python
import jax
import jax.numpy as jnp
from jax import lax
from jax.sharding import PartitionSpec as P

TICKS = 6


def partner(array, axis, bit):
    return lax.ppermute(array, axis, [(i, i ^ 1 << bit) for i in range(lax.axis_size(axis))])


def broadcast(value, axis, source):
    kept = jnp.where(lax.axis_index(axis) == source, value, 0).astype(value.dtype)
    return lax.psum(kept, axis)


def shifted(block, axis, distance):
    devices = range(lax.axis_size(axis))
    route = [((i - distance) % len(devices), i) for i in devices]
    return lax.ppermute(block, axis, route)


def pair_share(partial_value, half_idx, half_rows):
    keep = lax.dynamic_slice_in_dim(partial_value, half_idx * half_rows, half_rows, 0)
    give = lax.dynamic_slice_in_dim(partial_value, (1 - half_idx) * half_rows, half_rows, 0)
    return keep + partner(give, "col", 0)


def body(factor, gradient, starts):
    row_count = gradient.shape[0]
    block_count = starts.shape[0]
    panel_width = gradient.shape[1] // block_count
    tile_rows = factor.shape[0]
    half_rows = factor.shape[1]
    col_count = lax.axis_size("col")
    row_idx = lax.axis_index("row")
    col_idx = lax.axis_index("col")
    block_col = col_idx // 2
    half_idx = col_idx % 2
    slots = jnp.arange(block_count, dtype=jnp.int32)
    start_hot = (starts[None, :] == slots[:, None]).astype(jnp.float32)
    pieces = gradient.reshape(2, row_count // 2, block_count, panel_width)
    ordered = jnp.einsum("jp,hrpw->jhrw", start_hot, pieces, precision=lax.Precision.HIGHEST)
    ordered = ordered.reshape(col_count * (row_count // 2), panel_width)
    received = lax.all_to_all(ordered, "col", split_axis=0, concat_axis=0, tiled=True)
    received = received.reshape(col_count, row_count // 2, panel_width)
    keep_first = (half_idx == 0).astype(jnp.float32)
    keep_second = 1.0 - keep_first
    buffer = jnp.stack([received * keep_first, received * keep_second], axis=1).reshape(
        tile_rows, panel_width
    )
    zeros_tile = jnp.zeros((tile_rows, panel_width), jnp.float32)
    share = pair_share(buffer, half_idx, half_rows)
    for tick_idx in range(TICKS):
        active = block_col >= tick_idx
        on_diag = active & (row_idx == block_col)
        below_diag = active & (row_idx > block_col)
        mine = share.astype(jnp.bfloat16)
        other = partner(mine, "col", 0)
        rounded = jnp.where(
            half_idx == 0,
            jnp.concatenate([mine, other], axis=0),
            jnp.concatenate([other, mine], axis=0),
        )
        solution = lax.dot_general(
            factor, rounded, (((0,), (0,)), ((), ())), preferred_element_type=jnp.float32
        )
        solution_bf = solution.astype(jnp.bfloat16)
        arrived = broadcast(solution_bf, "row", block_col)
        update = jnp.dot(factor, arrived, preferred_element_type=jnp.float32)
        own_update = pair_share(update, half_idx, half_rows)
        share = jnp.where(on_diag, solution, jnp.where(below_diag, share - own_update, share))
        if tick_idx + 1 < TICKS:
            share = shifted(share, "col", 2)
    buffer = lax.dynamic_update_slice_in_dim(zeros_tile, share, half_idx * half_rows, 0)
    end_hot = (((starts + (TICKS - 1)) % block_count)[None, :] == slots[:, None]).astype(
        jnp.float32
    )
    returned = lax.all_to_all(buffer, "col", split_axis=0, concat_axis=0, tiled=True)
    slot_rows = returned.reshape(block_count, 2, row_count, panel_width).sum(axis=1)
    result = jnp.einsum("jp,jrw->rpw", end_hot, slot_rows, precision=lax.Precision.HIGHEST)
    return result.reshape(row_count, block_count * panel_width)


def solution(mesh):
    in_specs = (P("row", "col"), P(("row", "col"), None), P())
    out_specs = P(("row", "col"), None)
    return jax.shard_map(body, mesh=mesh, in_specs=in_specs, out_specs=out_specs, check_vma=False)
```

profile of v0, /device:TPU:0, one launch (start us, length us, event | category | flops | bytes accessed | tf_op | source)
XLA Modules:
  0.0 470.8 jit_solution(8846670668747078767)
XLA Ops:
  6.5 2.1 reshape.28
  11.0 6.4 %all-to-all-start = ((f32[8,112,128]{2,1,0:T(8,128)}), f32[8,112,128]{2,1,0:T(8,128)}, u32[]{:S(2)}, u32[]{:S(2)}) async-start(f32[8,112,128]{2,1,0:T(8,128)} %bitcast.91), calls=%async_computation | async-start | bytes 917504 | tf_op jit(solution)/shard_map/all_to_all | solution.py:46
  17.4 14.0 %all-to-all-done = f32[8,112,128]{2,1,0:T(8,128)} async-done(((f32[8,112,128]{2,1,0:T(8,128)}), f32[8,112,128]{2,1,0:T(8,128)}, u32[]{:S(2)}, u32[]{:S(2)}) %all-to-all-start) | async-done | bytes 458784 | tf_op jit(solution)/shard_map/all_to_all | solution.py:46
  33.6 2.0 copy.18
  35.6 2.0 copy.17
  37.7 2.0 fusion.58
  41.3 2.6 convert_select_fusion.5
  44.0 41.9 %all-reduce.7.cloned.1.call-done = bf16[896,128]{0,1:T(8,128)(2,1)} async-done(((bf16[896,128]{0,1:T(8,128)(2,1)}), bf16[896,128]{0,1:T(8,128)(2,1)}) %all-reduce.7.cloned.1.call-update) | async-done | bytes 229392 | tf_op jit(solution)/shard_map/psum | solution.py:15
  85.9 1.9 fusion.59
  89.6 2.2 collective-permute-done.2
  94.7 13.0 %collective-permute-done.3 = f32[896,128]{0,1:T(8,128)S(1)} collective-permute-done((f32[896,128]{0,1:T(8,128)S(1)}, f32[896,128]{0,1:T(8,128)S(1)}, u32[]{:S(2)}, u32[]{:S(2)}) %collective-permute-start.3) | collective-permute-done | bytes 458784 | tf_op jit(solution)/shard_map/ppermute | solution.py:21
  111.7 41.1 %all-reduce.9.cloned.1.call-done = bf16[896,128]{0,1:T(8,128)(2,1)} async-done(((bf16[896,128]{0,1:T(8,128)(2,1)}), bf16[896,128]{0,1:T(8,128)(2,1)}) %all-reduce.9.cloned.1.call-update) | async-done | bytes 229392 | tf_op jit(solution)/shard_map/psum | solution.py:15
  152.8 1.9 fusion.60
  156.5 2.2 collective-permute-done.5
  161.6 12.9 %collective-permute-done.6 = f32[896,128]{0,1:T(8,128)S(1)} collective-permute-done((f32[896,128]{0,1:T(8,128)S(1)}, f32[896,128]{0,1:T(8,128)S(1)}, u32[]{:S(2)}, u32[]{:S(2)}) %collective-permute-start.6) | collective-permute-done | bytes 458784 | tf_op jit(solution)/shard_map/ppermute | solution.py:21
  178.4 41.3 %all-reduce.11.cloned.1.call-done = bf16[896,128]{0,1:T(8,128)(2,1)} async-done(((bf16[896,128]{0,1:T(8,128)(2,1)}), bf16[896,128]{0,1:T(8,128)(2,1)}) %all-reduce.11.cloned.1.call-update) | async-done | bytes 229392 | tf_op jit(solution)/shard_map/psum | solution.py:15
  223.4 2.2 collective-permute-done.8
  228.5 12.9 %collective-permute-done.9 = f32[896,128]{0,1:T(8,128)S(1)} collective-permute-done((f32[896,128]{0,1:T(8,128)S(1)}, f32[896,128]{0,1:T(8,128)S(1)}, u32[]{:S(2)}, u32[]{:S(2)}) %collective-permute-start.9) | collective-permute-done | bytes 458784 | tf_op jit(solution)/shard_map/ppermute | solution.py:21
  245.4 41.3 %all-reduce.13.cloned.1.call-done = bf16[896,128]{0,1:T(8,128)(2,1)} async-done(((bf16[896,128]{0,1:T(8,128)(2,1)}), bf16[896,128]{0,1:T(8,128)(2,1)}) %all-reduce.13.cloned.1.call-update) | async-done | bytes 229392 | tf_op jit(solution)/shard_map/psum | solution.py:15
  286.6 1.9 fusion.62
  290.3 2.2 collective-permute-done.11
  295.4 12.9 %collective-permute-done.12 = f32[896,128]{0,1:T(8,128)S(1)} collective-permute-done((f32[896,128]{0,1:T(8,128)S(1)}, f32[896,128]{0,1:T(8,128)S(1)}, u32[]{:S(2)}, u32[]{:S(2)}) %collective-permute-start.12) | collective-permute-done | bytes 458784 | tf_op jit(solution)/shard_map/ppermute | solution.py:21
  312.3 41.3 %all-reduce.15.cloned.1.call-done = bf16[896,128]{0,1:T(8,128)(2,1)} async-done(((bf16[896,128]{0,1:T(8,128)(2,1)}), bf16[896,128]{0,1:T(8,128)(2,1)}) %all-reduce.15.cloned.1.call-update) | async-done | bytes 229392 | tf_op jit(solution)/shard_map/psum | solution.py:15
  353.6 1.9 fusion.63
  357.3 2.2 collective-permute-done.14
  362.5 12.9 %collective-permute-done.15 = f32[896,128]{0,1:T(8,128)S(1)} collective-permute-done((f32[896,128]{0,1:T(8,128)S(1)}, f32[896,128]{0,1:T(8,128)S(1)}, u32[]{:S(2)}, u32[]{:S(2)}) %collective-permute-start.15) | collective-permute-done | bytes 458784 | tf_op jit(solution)/shard_map/ppermute | solution.py:21
  379.3 41.2 %all-reduce.17.cloned.1.call-done = bf16[896,128]{0,1:T(8,128)(2,1)} async-done(((bf16[896,128]{0,1:T(8,128)(2,1)}), bf16[896,128]{0,1:T(8,128)(2,1)}) %all-reduce.17.cloned.1.call-update) | async-done | bytes 229392 | tf_op jit(solution)/shard_map/psum | solution.py:15
  424.2 2.2 collective-permute-done.17
  426.4 2.2 fusion.5
  428.5 2.0 copy.14
  432.5 4.6 all-to-all-start.1
  437.2 23.8 %all-to-all-done.1 = f32[8,224,128]{2,1,0:T(8,128)} async-done(((f32[8,224,128]{2,1,0:T(8,128)}), f32[8,224,128]{2,1,0:T(8,128)}, u32[]{:S(2)}, u32[]{:S(2)}) %all-to-all-start.1) | async-done | bytes 917536 | tf_op jit(solution)/shard_map/all_to_all | solution.py:80
  (100 shorter events, 60.2 us)
Async XLA Ops:
  6.5 34.8 %copy-start = (bf16[1792,896]{1,0:T(8,128)(2,1)S(1)}, bf16[1792,896]{1,0:T(8,128)(2,1)}, u32[]{:S(2)}) copy-start(bf16[1792,896]{1,0:T(8,128)(2,1)} %param.3) | copy-start | bytes 9633796
  11.0 20.4 %all-to-all-start = ((f32[8,112,128]{2,1,0:T(8,128)}), f32[8,112,128]{2,1,0:T(8,128)}, u32[]{:S(2)}, u32[]{:S(2)}) async-start(f32[8,112,128]{2,1,0:T(8,128)} %bitcast.91), calls=%async_computation | async-start | bytes 917504 | tf_op jit(solution)/shard_map/all_to_all | solution.py:46
  17.3 68.5 %all-reduce.7.cloned.1.call-start = ((), (), s32[]{:S(2)}) async-start(), calls=%async_computation.2 | async-start | bytes 458752 | tf_op jit(solution)/shard_map/psum | solution.py:15
  35.6 2.2 collective-permute-start
  39.7 1.6 collective-permute-start.1
  43.9 108.9 %all-reduce.9.cloned.1.call-start = ((), (), s32[]{:S(2)}) async-start(), calls=%async_computation.3 | async-start | bytes 458752 | tf_op jit(solution)/shard_map/psum | solution.py:15
  87.8 0.9 copy-start.2
  89.6 2.2 collective-permute-start.2
  93.3 14.4 %collective-permute-start.3 = (f32[896,128]{0,1:T(8,128)S(1)}, f32[896,128]{0,1:T(8,128)S(1)}, u32[]{:S(2)}, u32[]{:S(2)}) collective-permute-start(f32[896,128]{0,1:T(8,128)S(1)} %fusion), channel_id=1, source_target_pairs={{6,0},{7,1},{0,2},{1,3},{2,4},{3,5},{4,6},{5,7},{14,8},{15,9},{8,1... | collective-permute-start | bytes 1376264 | tf_op jit(solution)/shard_map/ppermute | solution.py:21
  108.5 1.6 collective-permute-start.4
  111.6 108.1 %all-reduce.11.cloned.1.call-start = ((), (), s32[]{:S(2)}) async-start(), calls=%async_computation.4 | async-start | bytes 458752 | tf_op jit(solution)/shard_map/psum | solution.py:15
  156.5 2.2 collective-permute-start.5
  160.0 14.4 %collective-permute-start.6 = (f32[896,128]{0,1:T(8,128)S(1)}, f32[896,128]{0,1:T(8,128)S(1)}, u32[]{:S(2)}, u32[]{:S(2)}) collective-permute-start(f32[896,128]{0,1:T(8,128)S(1)} %fusion.1), channel_id=1, source_target_pairs={{6,0},{7,1},{0,2},{1,3},{2,4},{3,5},{4,6},{5,7},{14,8},{15,9},{8,1... | collective-permute-start | bytes 1376264 | tf_op jit(solution)/shard_map/ppermute | solution.py:21
  175.3 1.6 collective-permute-start.7
  178.4 108.3 %all-reduce.13.cloned.1.call-start = ((), (), s32[]{:S(2)}) async-start(), calls=%async_computation.5 | async-start | bytes 458752 | tf_op jit(solution)/shard_map/psum | solution.py:15
  223.4 2.2 collective-permute-start.8
  227.0 14.4 %collective-permute-start.9 = (f32[896,128]{0,1:T(8,128)S(1)}, f32[896,128]{0,1:T(8,128)S(1)}, u32[]{:S(2)}, u32[]{:S(2)}) collective-permute-start(f32[896,128]{0,1:T(8,128)S(1)} %fusion.2), channel_id=1, source_target_pairs={{6,0},{7,1},{0,2},{1,3},{2,4},{3,5},{4,6},{5,7},{14,8},{15,9},{8,1... | collective-permute-start | bytes 1376264 | tf_op jit(solution)/shard_map/ppermute | solution.py:21
  242.2 1.6 collective-permute-start.10
  245.3 108.3 %all-reduce.15.cloned.1.call-start = ((), (), s32[]{:S(2)}) async-start(), calls=%async_computation.6 | async-start | bytes 458752 | tf_op jit(solution)/shard_map/psum | solution.py:15
  288.6 0.9 copy-start.5
  290.3 2.2 collective-permute-start.11
  293.9 14.4 %collective-permute-start.12 = (f32[896,128]{0,1:T(8,128)S(1)}, f32[896,128]{0,1:T(8,128)S(1)}, u32[]{:S(2)}, u32[]{:S(2)}) collective-permute-start(f32[896,128]{0,1:T(8,128)S(1)} %fusion.3), channel_id=1, source_target_pairs={{6,0},{7,1},{0,2},{1,3},{2,4},{3,5},{4,6},{5,7},{14,8},{15,9},{8,1... | collective-permute-start | bytes 1376264 | tf_op jit(solution)/shard_map/ppermute | solution.py:21
  309.1 1.6 collective-permute-start.13
  312.2 108.3 %all-reduce.17.cloned.1.call-start = ((), (), s32[]{:S(2)}) async-start(), calls=%async_computation.7 | async-start | bytes 458752 | tf_op jit(solution)/shard_map/psum | solution.py:15
  355.5 0.9 copy-start.6
  357.3 2.2 collective-permute-start.14
  360.8 14.6 %collective-permute-start.15 = (f32[896,128]{0,1:T(8,128)S(1)}, f32[896,128]{0,1:T(8,128)S(1)}, u32[]{:S(2)}, u32[]{:S(2)}) collective-permute-start(f32[896,128]{0,1:T(8,128)S(1)} %fusion.4), channel_id=1, source_target_pairs={{6,0},{7,1},{0,2},{1,3},{2,4},{3,5},{4,6},{5,7},{14,8},{15,9},{8,1... | collective-permute-start | bytes 1376264 | tf_op jit(solution)/shard_map/ppermute | solution.py:21
  376.2 1.6 collective-permute-start.16
  422.5 0.9 copy-start.1
  424.2 2.2 collective-permute-start.17
  426.4 10.8 %copy-start.13 = (s32[4]{0:T(128)S(1)}, s32[4]{0:T(128)}, u32[]{:S(2)}) copy-start(s32[4]{0:T(128)} %param.5) | copy-start | bytes 52
  432.5 28.5 %all-to-all-start.1 = ((f32[8,224,128]{2,1,0:T(8,128)}), f32[8,224,128]{2,1,0:T(8,128)}, u32[]{:S(2)}, u32[]{:S(2)}) async-start(f32[8,224,128]{2,1,0:T(8,128)} %bitcast.90), calls=%async_computation.1 | async-start | bytes 1835008 | tf_op jit(solution)/shard_map/all_to_all | solution.py:80
  (8 other events, 6.8 us)
Sparse Core Ops, SparseCore 0:
  44.1 41.7 all-reduce.6
  111.7 41.0 all-reduce.8
  178.5 41.1 all-reduce.10
  245.4 41.1 all-reduce.12
  312.4 41.1 all-reduce.14
  379.5 41.0 all-reduce.16
where the time goes:
time: 472 us; the launch traced here: 471 us
  waiting for transfers between devices  372 us (79%)
  local copies, waits for them, and re-layouts  27.1 us (6%)
  matrix products  24.2 us (5%)
  starting transfers between devices  19.7 us (4%)
  between operations  13.8 us (3%)
  other arithmetic  13.7 us (3%)
    psum x6, waiting for transfers between devices, broadcast(): return lax.psum(kept, axis)  248 us
    ppermute x5, waiting for transfers between devices, shifted(): return lax.ppermute(block, axis, route)  64.5 us
    all_to_all x1, waiting for transfers between devices, body(): lax.all_to_all(buffer, 'col', split_axis=0, concat_axis=0, tiled=True)  23.8 us
    ppermute x13, waiting for transfers between devices, partner(): lax.ppermute(array, axis, [(i, i ^ 1 << bit) for i in range(lax.axis_size...  21.8 us
    unnamed x31, local copies, waits for them, and re-layouts  15.3 us
    all_to_all x1, waiting for transfers between devices, body(): lax.all_to_all(ordered, 'col', split_axis=0, concat_axis=0, tiled=True)  14 us
    dot_general x6, matrix products, body(): update = jnp.dot(factor, arrived, preferred_element_type=jnp.float32)  11.7 us
    dot_general x6, matrix products, body(): lax.dot_general(factor, rounded, (((0,), (0,)), ((), ())), preferred_elem...  10.2 us
  transfers between devices with their start and end apart: 26, of which 26 were waited for; matrix products, arithmetic and copies ran while one was open for 0% of the time, Pallas kernels for 0%

commit v1 on v0

v1 whole, which is shorter than its diff:
```python
import jax
import jax.numpy as jnp
from jax import lax
from jax.experimental import pallas as pl
from jax.experimental.pallas import tpu as pltpu
from jax.sharding import PartitionSpec as P

TICKS = 6
F32 = jnp.float32
BF16 = jnp.bfloat16
VM = pl.BlockSpec(memory_space=pltpu.VMEM)
SM = pl.BlockSpec(memory_space=pltpu.SMEM)


def call(kernel, outs, args, specs, scratch=(), flops=0, name=None):
    n_bytes = sum(o.size * o.dtype.itemsize for o in outs)
    return pl.pallas_call(
        kernel,
        out_shape=outs,
        in_specs=specs,
        out_specs=[VM] * len(outs),
        scratch_shapes=list(scratch),
        compiler_params=pltpu.CompilerParams(vmem_limit_bytes=24 << 20),
        cost_estimate=pl.CostEstimate(flops=flops, bytes_accessed=n_bytes, transcendentals=0),
        name=name,
    )(*args)


def shape(dims, dtype):
    return jax.ShapeDtypeStruct(dims, dtype)


def place():
    col = lax.axis_index("col")
    return lax.axis_index("row"), col // 2, col % 2


def panel_at(starts_ref, count, slot):
    found = jnp.int32(0)
    for p in range(count):
        found = jnp.where(starts_ref[p] == slot, jnp.int32(p), found)
    return found


def prep_kernel(count, width, starts_ref, grad_ref, out_ref):
    for slot in range(count):
        begin = pl.multiple_of(panel_at(starts_ref, count, slot) * width, width)
        out_ref[slot] = grad_ref[:, pl.ds(begin, width)].astype(out_ref.dtype)


def pack_kernel(count, width, mine_ref, other_ref, *out_refs):
    _, z, h = place()
    lanes = lax.broadcasted_iota(jnp.int32, mine_ref.shape[1:], 1)
    low = lanes < width // 2
    for k in range(count):
        slot = lax.rem(z + k, count)
        mine = mine_ref[slot].astype(F32)
        other = other_ref[slot].astype(F32)
        first = jnp.where(h == 0, mine, pltpu.roll(other, width // 2, 1))
        second = jnp.where(h == 0, pltpu.roll(other, width // 2, 1), mine)
        out_refs[k][...] = jnp.where(low, first, second).astype(out_refs[k].dtype)


def solve(x_ref, xb_ref, rhs, own_ref, other_ref):
    half = own_ref.shape[1]
    left = jnp.dot(rhs, own_ref[...], preferred_element_type=F32)
    right = jnp.dot(rhs, other_ref[...], preferred_element_type=F32)
    x_ref[:, :half] = left
    x_ref[:, half:] = right
    xb_ref[:, :half] = left.astype(BF16)
    xb_ref[:, half:] = right.astype(BF16)


def first_kernel(count, *refs):
    pieces = refs[:count]
    own_ref, other_ref, x_ref, xb_ref, acc_ref, natural = refs[count:]
    r, z, _ = place()
    rows, width = pieces[0].shape
    for k in range(count):
        source = lax.rem(z - k + count, count)
        piece = pieces[k][...].astype(F32)
        top = pl.multiple_of(source * (2 * rows), 8)
        natural[pl.ds(top, rows), :] = piece
        natural[pl.ds(pl.multiple_of(top + rows, 8), rows), :] = pltpu.roll(piece, width // 2, 1)
    acc_ref[...] = jnp.transpose(natural[...])[: width // 2]

    @pl.when(r == z)
    def _():
        solve(x_ref, xb_ref, acc_ref[...].astype(BF16), own_ref, other_ref)


def solve_kernel(tick, rhs_ref, own_ref, other_ref, x_ref, xb_ref):
    r, z, _ = place()

    @pl.when((r == z) & (z >= tick))
    def _():
        solve(x_ref, xb_ref, rhs_ref[...], own_ref, other_ref)


def product(x_ref, own_ref, other_ref):
    half = own_ref.shape[1]
    dims = (((1,), (1,)), ((), ()))
    left = lax.dot_general(x_ref[:, :half], own_ref[...], dims, preferred_element_type=F32)
    return left + lax.dot_general(x_ref[:, half:], other_ref[...], dims, preferred_element_type=F32)


def near_kernel(tick, x_ref, acc_ref, own_ref, other_ref, out_ref):
    r, z, _ = place()

    @pl.when((r == z + 1) & (z >= tick))
    def _():
        out_ref[...] = (acc_ref[...] - product(x_ref, own_ref, other_ref)).astype(out_ref.dtype)


def far_kernel(tick, acc_ref, own_ref, other_ref, *refs):
    x_refs, out_ref = refs[:-1], refs[-1]
    r, z, _ = place()
    for i, x_ref in enumerate(x_refs):

        @pl.when((r == z + 2 + i) & (z >= tick))
        def _():
            out_ref[...] = acc_ref[...] - product(x_ref, own_ref, other_ref)


def fold_kernel(count, x_ref, *refs):
    out_refs, natural = refs[:-1], refs[-1]
    _, z, h = place()
    rows, width = out_refs[0].shape
    half = x_ref.shape[1] // 2

    @pl.when(h == 0)
    def _():
        natural[: 2 * half, : width // 2] = jnp.transpose(x_ref[...])

    @pl.when(h == 1)
    def _():
        natural[half : 2 * half, : width // 2] = jnp.transpose(x_ref[:, :half])
        natural[:half, : width // 2] = jnp.transpose(x_ref[:, half:])

    lanes = lax.broadcasted_iota(jnp.int32, (rows, width), 1)
    for k in range(count):
        target = lax.rem(z + k, count)
        top = pl.multiple_of(target * (2 * rows), 8)
        upper = natural[pl.ds(top, rows), :]
        lower = natural[pl.ds(pl.multiple_of(top + rows, 8), rows), :]
        out_refs[k][...] = jnp.where(lanes < width // 2, upper, pltpu.roll(lower, width // 2, 1))


def pick_kernel(count, ticks, *refs):
    out_ref = refs[-1]
    early, last = refs[: (ticks - 1) * count], refs[(ticks - 1) * count : -1]
    r, z, _ = place()
    for t in range(ticks - 1):
        for k in range(count):

            @pl.when(lax.rem(z - r + count, count) == k)
            def _():
                out_ref[t] = early[t * count + k][...]

    for k in range(count):
        source = lax.rem(z - k + count, count)

        @pl.when((source >= ticks - 1) & (source <= r))
        def _():
            out_ref[source] = last[k][...]


def final_kernel(count, ticks, starts_ref, grad_ref, mine_ref, other_ref, out_ref):
    r, _, h = place()
    width = mine_ref.shape[2]
    lanes = lax.broadcasted_iota(jnp.int32, mine_ref.shape[1:], 1)
    for s in range(count):
        begin = pl.multiple_of(panel_at(starts_ref, count, s) * width, width)

        @pl.when(r < s)
        def _():
            out_ref[:, pl.ds(begin, width)] = grad_ref[:, pl.ds(begin, width)]

        @pl.when(r >= s)
        def _():
            slot = jnp.where(r - s <= ticks - 2, r - s, s + ticks - 1)
            mine = mine_ref[slot]
            other = pltpu.roll(other_ref[slot], width // 2, 1)
            low = jnp.where(h == 0, mine, other)
            high = jnp.where(h == 0, other, mine)
            out_ref[:, pl.ds(begin, width)] = jnp.where(lanes < width // 2, low, high)


def body(factor, gradient, starts):
    count = starts.shape[0]
    ticks = min(TICKS, count)
    rows = gradient.shape[0]
    width = gradient.shape[1] // count
    tile, half = factor.shape
    cols = width // 2
    devices = [(r, z, h) for r in range(count) for z in range(count) for h in range(2)]

    def move(array, target):
        pairs = []
        for r, z, h in devices:
            goal = target(r, z, h)
            if goal is not None:
                pairs.append(((r * count + z) * 2 + h, (goal[0] * count + goal[1]) * 2 + goal[2]))
        return lax.ppermute(array, ("row", "col"), pairs)

    def cores(array):
        return move(array, lambda r, z, h: (r, z, 1 - h))

    def along(array, k):
        return move(array, lambda r, z, h: (r, (z + k) % count, h))

    def across(array, d):
        return move(array, lambda r, z, h: ((r + d) % count, z, h))

    def to_next_row(array):
        def target(r, z, h):
            return (z % 2 + ((r - z % 2) % count ^ 1)) % count, z, h

        return move(array, target)

    def to_next_col(array):
        def target(r, z, h):
            if r % 2 == 1:
                return r, z ^ 1, h
            if z in (0, count - 1):
                return r ^ 2, z, h
            return r, ((z - 1) ^ 1) + 1, h

        return move(array, target)

    def far_to_next_col(array, tick):
        def target(r, z, h):
            return (r, z + 1, h) if r >= z + 2 and z >= tick else None

        return move(array, target)

    flops = 2 * cols * tile * tile
    other_tile = cores(factor)
    mine = call(
        lambda *a: prep_kernel(count, width, *a),
        [shape((count, rows, width), BF16)], (starts, gradient), [SM, VM], name="prep",
    )[0]
    theirs = cores(mine)
    pieces = call(
        lambda *a: pack_kernel(count, width, *a),
        [shape((rows, width), BF16)] * count, (mine, theirs), [VM, VM], name="pack",
    )
    arrived = [pieces[0]] + [along(pieces[k], k) for k in range(1, count)]
    wide = [shape((cols, tile), F32), shape((cols, tile), BF16)]
    x, xb, acc = call(
        lambda *a: first_kernel(count, *a),
        wide + [shape((cols, tile), F32)], (*arrived, factor, other_tile), [VM] * (count + 2),
        [pltpu.VMEM((tile, width), F32)], flops, "first",
    )
    early, last = [], None
    for tick in range(ticks):
        if tick:
            x, xb = call(
                lambda *a: solve_kernel(tick, *a),
                wide, (rhs, factor, other_tile), [VM] * 3, (), flops, "solve",
            )
        final = tick == ticks - 1
        result = x
        if count - 1 > tick:
            near = to_next_row(xb)
            far = [across(xb, d) for d in range(2, count - tick)]
            out = call(
                lambda *a: near_kernel(tick, *a),
                [shape((cols, tile), F32 if final else BF16)], (near, acc, factor, other_tile),
                [VM] * 4, (), flops, "near",
            )[0]
            if final:
                r, z, _ = place()
                result = jnp.where(r == z, x, out)
            else:
                rhs = to_next_col(out)
            if far:
                out = call(
                    lambda *a: far_kernel(tick, *a),
                    [shape((cols, tile), F32)], (acc, factor, other_tile, *far),
                    [VM] * (3 + len(far)), (), flops, "far",
                )[0]
                if final:
                    result = jnp.where(r >= z + 2, out, result)
                else:
                    acc = far_to_next_col(out, tick)
        parts = call(
            lambda *a: fold_kernel(count, *a),
            [shape((rows, width), F32)] * count, (result,), [VM],
            [pltpu.VMEM((tile, width), F32)], 0, "fold",
        )
        sent = [parts[0]] + [along(parts[k], k) for k in range(1, count)]
        if final:
            last = sent
        else:
            early += sent
    slots = max(count, ticks)
    mine = call(
        lambda *a: pick_kernel(count, ticks, *a),
        [shape((slots, rows, width), F32)], (*early, *last), [VM] * (count * ticks), name="pick",
    )[0]
    theirs = cores(mine)
    return call(
        lambda *a: final_kernel(count, ticks, *a),
        [shape(gradient.shape, F32)], (starts, gradient, mine, theirs), [SM, VM, VM, VM], name="final",
    )[0]


def solution(mesh):
    in_specs = (P("row", "col"), P(("row", "col"), None), P())
    out_specs = P(("row", "col"), None)
    return jax.shard_map(body, mesh=mesh, in_specs=in_specs, out_specs=out_specs, check_vma=False)
```

time: 472 us -> 116 us (0.25)
  waiting for transfers between devices: 372 us -> 45.3 us
  starting transfers between devices: 19.7 us -> 59.8 us
  matrix products: 24.2 us -> 0 us
  local copies, waits for them, and re-layouts: 27.1 us -> 3.6 us
  other arithmetic: 13.7 us -> 0 us
  between operations: 13.8 us -> 0.16 us
  Pallas kernels: 0 us -> 6.51 us
    psum x6 -> x0, waiting for transfers between devices: 248 us -> none  [broadcast(): return lax.psum(kept, axis)]
    ppermute x18 -> x29, starting transfers between devices: 8.45 us -> 59.8 us  [move(): return lax.ppermute(array, ('row', 'col'), pairs)]
    ppermute x18 -> x29, waiting for transfers between devices: 86.3 us -> 45.3 us  [move(): return lax.ppermute(array, ('row', 'col'), pairs)]
    all_to_all x2 -> x0, waiting for transfers between devices: 37.8 us -> none  [the longest x1 23.8 us: body(): lax.all_to_all(buffer, 'col', split_axis=0, concat_axis=0, tiled=True)]
    dot_general x14 -> x0, matrix products: 24.2 us -> none  [the longest x6 11.7 us: body(): update = jnp.dot(factor, arrived, preferred_element_type=jnp.float32)]
    unnamed x31 -> x12, local copies, waits for them, and re-layouts: 15.3 us -> 3.6 us
    all_to_all x2 -> x0, starting transfers between devices: 11 us -> none  [the longest x1 6.35 us: body(): lax.all_to_all(ordered, 'col', split_axis=0, concat_axis=0, tiled=True)]
    select_n x7 -> x0, other arithmetic: 9.21 us -> none  [the longest x6 9.2 us: body(): jnp.where(on_diag, solution, jnp.where(below_diag, share - own_update, sh...]
  transfers between devices with their start and end apart: 26 -> 29, of which waited for: 26 -> 15; matrix products, arithmetic and copies ran while one was open for 0% -> 0% of each run, Pallas kernels for 0% -> 3%
where the time goes in v1:
time: 116 us; the launch traced here: 115 us
  starting transfers between devices  59.8 us (52%)
  waiting for transfers between devices  45.3 us (39%)
  Pallas kernels  6.51 us (6%)
  local copies, waits for them, and re-layouts  3.6 us (3%)
    ppermute x29, starting transfers between devices, move(): return lax.ppermute(array, ('row', 'col'), pairs)  59.8 us
    ppermute x29, waiting for transfers between devices, move(): return lax.ppermute(array, ('row', 'col'), pairs)  45.3 us
    pallas_call x17, Pallas kernels, call(): pl.pallas_call(kernel, out_shape=outs, in_specs=specs, out_specs=[VM] * l...  6.51 us
    unnamed x12, local copies, waits for them, and re-layouts  3.6 us
  transfers between devices with their start and end apart: 29, of which 15 were waited for; matrix products, arithmetic and copies ran while one was open for 0% of the time, Pallas kernels for 3%

profile of v1, /device:TPU:0, one launch (start us, length us, event | category | flops | bytes accessed | tf_op | source)
XLA Modules:
  0.0 115.3 jit_solution(15797472848721710492)
XLA Ops:
  0.5 1.0 copy-done.2
  2.9 3.5 %collective-permute-done.a_1_ = bf16[4,224,128]{2,1,0:T(8,128)(2,1)S(1)} collective-permute-done((bf16[4,224,128]{2,1,0:T(8,128)(2,1)S(1)}, bf16[4,224,128]{2,1,0:T(8,128)(2,1)S(1)}, u32[]{:S(2)}, u32[]{:S(2)}) %collective-permute-start) | collective-permute-done | bytes 229408 | tf_op jit(solution)/shard_map/ppermute | solution.py:204
  6.6 3.0 %collective-permute-start.1 = (bf16[224,128]{1,0:T(8,128)(2,1)S(1)}, bf16[224,128]{1,0:T(8,128)(2,1)S(1)}, u32[]{:S(2)}, u32[]{:S(2)}) collective-permute-start(bf16[224,128]{1,0:T(8,128)(2,1)S(1)} %get-tuple-element.34), channel_id=1, source_target_pairs={{0,2},{1,3},{2,4},{3,5},{4,6},{5,7},{6,0},{7,1},{8,10},{9,11},{10,... | collective-permute-start | bytes 172040 | tf_op jit(solution)/shard_map/ppermute | solution.py:204
  9.6 2.6 %collective-permute-start.2 = (bf16[224,128]{1,0:T(8,128)(2,1)S(1)}, bf16[224,128]{1,0:T(8,128)(2,1)S(1)}, u32[]{:S(2)}, u32[]{:S(2)}) collective-permute-start(bf16[224,128]{1,0:T(8,128)(2,1)S(1)} %get-tuple-element.35), channel_id=1, source_target_pairs={{0,4},{1,5},{2,6},{3,7},{4,0},{5,1},{6,2},{7,3},{8,12},{9,13},{10,... | collective-permute-start | bytes 172040 | tf_op jit(solution)/shard_map/ppermute | solution.py:204
  12.2 1.3 %collective-permute-start.3 = (bf16[224,128]{1,0:T(8,128)(2,1)S(1)}, bf16[224,128]{1,0:T(8,128)(2,1)S(1)}, u32[]{:S(2)}, u32[]{:S(2)}) collective-permute-start(bf16[224,128]{1,0:T(8,128)(2,1)S(1)} %get-tuple-element.36), channel_id=1, source_target_pairs={{0,6},{1,7},{2,0},{3,1},{4,2},{5,3},{6,4},{7,5},{8,14},{9,15},{10,... | collective-permute-start | bytes 172040 | tf_op jit(solution)/shard_map/ppermute | solution.py:204
  13.9 2.5 %collective-permute-done.2.a_2_ = bf16[224,128]{1,0:T(8,128)(2,1)S(1)} collective-permute-done((bf16[224,128]{1,0:T(8,128)(2,1)S(1)}, bf16[224,128]{1,0:T(8,128)(2,1)S(1)}, u32[]{:S(2)}, u32[]{:S(2)}) %collective-permute-start.2) | collective-permute-done | bytes 57376 | tf_op jit(solution)/shard_map/ppermute | solution.py:204
  16.7 1.9 %copy-done = bf16[1792,896]{1,0:T(8,128)(2,1)S(1)} copy-done((bf16[1792,896]{1,0:T(8,128)(2,1)S(1)}, bf16[1792,896]{1,0:T(8,128)(2,1)}, u32[]{:S(2)}) %copy-start) | copy-done | bytes 3211288
  18.6 1.5 %first.1 = (f32[64,1792]{1,0:T(8,128)S(1)}, bf16[64,1792]{1,0:T(8,128)(2,1)S(1)}, f32[64,1792]{1,0:T(8,128)S(1)}) custom-call(bf16[224,128]{1,0:T(8,128)(2,1)S(1)} %get-tuple-element.33.a_0_, bf16[224,128]{1,0:T(8,128)(2,1)S(1)} %collective-permute-done.1.a_1_, bf16[224,128]{1,0:T(8,128)(2,1)S(1)} %collective-permute-done.2.a_2_, ...), custom_call_target="tpu_custom_call" | custom-call | flops 411041792 | bytes 1146880 | tf_op jit(solution)/shard_map/first/pallas_call | solution.py:17
  20.6 1.5 %collective-permute-start.15 = (bf16[64,1792]{1,0:T(8,128)(2,1)S(1)}, bf16[64,1792]{1,0:T(8,128)(2,1)S(1)}, u32[]{:S(2)}, u32[]{:S(2)}) collective-permute-start(bf16[64,1792]{1,0:T(8,128)(2,1)S(1)} %get-tuple-element.42), channel_id=1, source_target_pairs={{0,24},{1,25},{2,26},{3,27},{4,28},{5,29},{6,30},{7,31},{8,0},{9,1... | collective-permute-start | bytes 688136 | tf_op jit(solution)/shard_map/ppermute | solution.py:204
  22.1 1.6 %collective-permute-start.14 = (bf16[64,1792]{1,0:T(8,128)(2,1)S(1)}, bf16[64,1792]{1,0:T(8,128)(2,1)S(1)}, u32[]{:S(2)}, u32[]{:S(2)}) collective-permute-start(bf16[64,1792]{1,0:T(8,128)(2,1)S(1)} %get-tuple-element.42), channel_id=1, source_target_pairs={{0,16},{1,17},{2,18},{3,19},{4,20},{5,21},{6,22},{7,23},{8,24},{9,... | collective-permute-start | bytes 688136 | tf_op jit(solution)/shard_map/ppermute | solution.py:204
  23.7 5.0 %collective-permute-done.8.a_0_ = bf16[64,1792]{1,0:T(8,128)(2,1)S(1)} collective-permute-done((bf16[64,1792]{1,0:T(8,128)(2,1)S(1)}, bf16[64,1792]{1,0:T(8,128)(2,1)S(1)}, u32[]{:S(2)}, u32[]{:S(2)}) %collective-permute-start.8) | collective-permute-done | bytes 229408 | tf_op jit(solution)/shard_map/ppermute | solution.py:204
  29.1 3.1 %collective-permute-done.15.a_4_ = bf16[64,1792]{1,0:T(8,128)(2,1)S(1)} collective-permute-done((bf16[64,1792]{1,0:T(8,128)(2,1)S(1)}, bf16[64,1792]{1,0:T(8,128)(2,1)S(1)}, u32[]{:S(2)}, u32[]{:S(2)}) %collective-permute-start.15) | collective-permute-done | bytes 229408 | tf_op jit(solution)/shard_map/ppermute | solution.py:204
  32.9 1.8 %collective-permute-done.9.a_0_ = bf16[64,1792]{1,0:T(8,128)(2,1)S(1)} collective-permute-done((bf16[64,1792]{1,0:T(8,128)(2,1)S(1)}, bf16[64,1792]{1,0:T(8,128)(2,1)S(1)}, u32[]{:S(2)}, u32[]{:S(2)}) %collective-permute-start.9) | collective-permute-done | bytes 229408 | tf_op jit(solution)/shard_map/ppermute | solution.py:204
  34.7 2.5 %collective-permute-start.13 = (bf16[64,1792]{1,0:T(8,128)(2,1)S(1)}, bf16[64,1792]{1,0:T(8,128)(2,1)S(1)}, u32[]{:S(2)}, u32[]{:S(2)}) collective-permute-start(bf16[64,1792]{1,0:T(8,128)(2,1)S(1)} %get-tuple-element.49), channel_id=1, source_target_pairs={{0,8},{1,9},{2,26},{3,27},{4,12},{5,13},{6,30},{7,31},{8,0},{9,1},... | collective-permute-start | bytes 688136 | tf_op jit(solution)/shard_map/ppermute | solution.py:204
  37.2 8.6 %collective-permute-start.22 = (bf16[64,1792]{1,0:T(8,128)(2,1)S(1)}, bf16[64,1792]{1,0:T(8,128)(2,1)S(1)}, u32[]{:S(2)}, u32[]{:S(2)}) collective-permute-start(bf16[64,1792]{1,0:T(8,128)(2,1)S(1)} %get-tuple-element.49), channel_id=1, source_target_pairs={{0,16},{1,17},{2,18},{3,19},{4,20},{5,21},{6,22},{7,23},{8,24},{9,... | collective-permute-start | bytes 688136 | tf_op jit(solution)/shard_map/ppermute | solution.py:204
  45.8 5.5 %collective-permute-start.17 = (bf16[64,1792]{1,0:T(8,128)(2,1)S(1)}, bf16[64,1792]{1,0:T(8,128)(2,1)S(1)}, u32[]{:S(2)}, u32[]{:S(2)}) collective-permute-start(bf16[64,1792]{1,0:T(8,128)(2,1)S(1)} %near.4), channel_id=1, source_target_pairs={{0,16},{1,17},{2,4},{3,5},{4,2},{5,3},{6,22},{7,23},{8,10},{9,11},... | collective-permute-start | bytes 688136 | tf_op jit(solution)/shard_map/ppermute | solution.py:204
  52.0 4.2 %collective-permute-done.17.a_0_ = bf16[64,1792]{1,0:T(8,128)(2,1)S(1)} collective-permute-done((bf16[64,1792]{1,0:T(8,128)(2,1)S(1)}, bf16[64,1792]{1,0:T(8,128)(2,1)S(1)}, u32[]{:S(2)}, u32[]{:S(2)}) %collective-permute-start.17) | collective-permute-done | bytes 229408 | tf_op jit(solution)/shard_map/ppermute | solution.py:204
  56.5 5.8 %collective-permute-done.21.a_0_ = bf16[64,1792]{1,0:T(8,128)(2,1)S(1)} collective-permute-done((bf16[64,1792]{1,0:T(8,128)(2,1)S(1)}, bf16[64,1792]{1,0:T(8,128)(2,1)S(1)}, u32[]{:S(2)}, u32[]{:S(2)}) %collective-permute-start.21) | collective-permute-done | bytes 229408 | tf_op jit(solution)/shard_map/ppermute | solution.py:204
  62.3 5.0 %collective-permute-start.24 = (bf16[64,1792]{1,0:T(8,128)(2,1)S(1)}, bf16[64,1792]{1,0:T(8,128)(2,1)S(1)}, u32[]{:S(2)}, u32[]{:S(2)}) collective-permute-start(bf16[64,1792]{1,0:T(8,128)(2,1)S(1)} %near.5), channel_id=1, source_target_pairs={{0,16},{1,17},{2,4},{3,5},{4,2},{5,3},{6,22},{7,23},{8,10},{9,11},... | collective-permute-start | bytes 688136 | tf_op jit(solution)/shard_map/ppermute | solution.py:204
  67.9 1.0 collective-permute-start.5
  68.8 4.1 %collective-permute-start.6 = (f32[224,128]{1,0:T(8,128)S(1)}, f32[224,128]{1,0:T(8,128)S(1)}, u32[]{:S(2)}, u32[]{:S(2)}) collective-permute-start(f32[224,128]{1,0:T(8,128)S(1)} %get-tuple-element.40), channel_id=1, source_target_pairs={{0,4},{1,5},{2,6},{3,7},{4,0},{5,1},{6,2},{7,3},{8,12},{9,13},{10,... | collective-permute-start | bytes 344072 | tf_op jit(solution)/shard_map/ppermute | solution.py:204
  73.7 2.0 %collective-permute-start.10 = (f32[224,128]{1,0:T(8,128)S(1)}, f32[224,128]{1,0:T(8,128)S(1)}, u32[]{:S(2)}, u32[]{:S(2)}) collective-permute-start(f32[224,128]{1,0:T(8,128)S(1)} %get-tuple-element.46), channel_id=1, source_target_pairs={{0,2},{1,3},{2,4},{3,5},{4,6},{5,7},{6,0},{7,1},{8,10},{9,11},{10,... | collective-permute-start | bytes 344072 | tf_op jit(solution)/shard_map/ppermute | solution.py:204
  76.4 7.8 %collective-permute-start.11 = (f32[224,128]{1,0:T(8,128)S(1)}, f32[224,128]{1,0:T(8,128)S(1)}, u32[]{:S(2)}, u32[]{:S(2)}) collective-permute-start(f32[224,128]{1,0:T(8,128)S(1)} %get-tuple-element.47), channel_id=1, source_target_pairs={{0,4},{1,5},{2,6},{3,7},{4,0},{5,1},{6,2},{7,3},{8,12},{9,13},{10,... | collective-permute-start | bytes 344072 | tf_op jit(solution)/shard_map/ppermute | solution.py:204
  84.2 6.4 %collective-permute-done.6.a_2_ = f32[224,128]{1,0:T(8,128)S(1)} collective-permute-done((f32[224,128]{1,0:T(8,128)S(1)}, f32[224,128]{1,0:T(8,128)S(1)}, u32[]{:S(2)}, u32[]{:S(2)}) %collective-permute-start.6) | collective-permute-done | bytes 114720 | tf_op jit(solution)/shard_map/ppermute | solution.py:204
  90.6 2.0 %collective-permute-start.18 = (f32[224,128]{1,0:T(8,128)S(1)}, f32[224,128]{1,0:T(8,128)S(1)}, u32[]{:S(2)}, u32[]{:S(2)}) collective-permute-start(f32[224,128]{1,0:T(8,128)S(1)} %get-tuple-element.52), channel_id=1, source_target_pairs={{0,2},{1,3},{2,4},{3,5},{4,6},{5,7},{6,0},{7,1},{8,10},{9,11},{10,... | collective-permute-start | bytes 344072 | tf_op jit(solution)/shard_map/ppermute | solution.py:204
  93.9 2.4 %collective-permute-start.20 = (f32[224,128]{1,0:T(8,128)S(1)}, f32[224,128]{1,0:T(8,128)S(1)}, u32[]{:S(2)}, u32[]{:S(2)}) collective-permute-start(f32[224,128]{1,0:T(8,128)S(1)} %get-tuple-element.54), channel_id=1, source_target_pairs={{0,6},{1,7},{2,0},{3,1},{4,2},{5,3},{6,4},{7,5},{8,14},{9,15},{10,... | collective-permute-start | bytes 344072 | tf_op jit(solution)/shard_map/ppermute | solution.py:204
  96.4 4.1 %collective-permute-done.12.a_7_ = f32[224,128]{1,0:T(8,128)S(1)} collective-permute-done((f32[224,128]{1,0:T(8,128)S(1)}, f32[224,128]{1,0:T(8,128)S(1)}, u32[]{:S(2)}, u32[]{:S(2)}) %collective-permute-start.12) | collective-permute-done | bytes 114720 | tf_op jit(solution)/shard_map/ppermute | solution.py:204
  100.5 1.9 %collective-permute-start.26 = (f32[224,128]{1,0:T(8,128)S(1)}, f32[224,128]{1,0:T(8,128)S(1)}, u32[]{:S(2)}, u32[]{:S(2)}) collective-permute-start(f32[224,128]{1,0:T(8,128)S(1)} %get-tuple-element.59), channel_id=1, source_target_pairs={{0,4},{1,5},{2,6},{3,7},{4,0},{5,1},{6,2},{7,3},{8,12},{9,13},{10,... | collective-permute-start | bytes 344072 | tf_op jit(solution)/shard_map/ppermute | solution.py:204
  102.4 3.4 %collective-permute-start.27 = (f32[224,128]{1,0:T(8,128)S(1)}, f32[224,128]{1,0:T(8,128)S(1)}, u32[]{:S(2)}, u32[]{:S(2)}) collective-permute-start(f32[224,128]{1,0:T(8,128)S(1)} %get-tuple-element.60), channel_id=1, source_target_pairs={{0,6},{1,7},{2,0},{3,1},{4,2},{5,3},{6,4},{7,5},{8,14},{9,15},{10,... | collective-permute-start | bytes 344072 | tf_op jit(solution)/shard_map/ppermute | solution.py:204
  106.6 5.2 %collective-permute-done.26.a_14_ = f32[224,128]{1,0:T(8,128)S(1)} collective-permute-done((f32[224,128]{1,0:T(8,128)S(1)}, f32[224,128]{1,0:T(8,128)S(1)}, u32[]{:S(2)}, u32[]{:S(2)}) %collective-permute-start.26) | collective-permute-done | bytes 114720 | tf_op jit(solution)/shard_map/ppermute | solution.py:204
  112.0 1.8 %collective-permute-done.28.a_3_ = f32[4,224,128]{2,1,0:T(8,128)S(1)} collective-permute-done((f32[4,224,128]{2,1,0:T(8,128)S(1)}, f32[4,224,128]{2,1,0:T(8,128)S(1)}, u32[]{:S(2)}, u32[]{:S(2)}) %collective-permute-start.28) | collective-permute-done | bytes 458784 | tf_op jit(solution)/shard_map/ppermute | solution.py:204
  113.8 1.5 %final.1 = f32[224,512]{1,0:T(8,128)} custom-call(s32[4]{0:T(128)S(1)} %copy-done.5, f32[224,512]{1,0:T(8,128)S(1)} %copy-done.3, f32[4,224,128]{2,1,0:T(8,128)S(1)} %pick.1.a_2_, f32[4,224,128]{2,1,0:T(8,128)S(1)} %collective-permute-done.28.a_3_), custom_call_target="tpu_custom_call" | custom-call | bytes 458752 | tf_op jit(solution)/shard_map/final/pallas_call | solution.py:17
  (55 shorter events, 9.5 us)
Async XLA Ops:
  0.0 16.7 %collective-permute-start.4 = (bf16[1792,896]{1,0:T(8,128)(2,1)}, bf16[1792,896]{1,0:T(8,128)(2,1)S(1)}, u32[]{:S(2)}, u32[]{:S(2)}) collective-permute-start(bf16[1792,896]{1,0:T(8,128)(2,1)} %a_1_.12), channel_id=1, source_target_pairs={{0,1},{1,0},{2,3},{3,2},{4,5},{5,4},{6,7},{7,6},{8,9},{9,8},{10,11... | collective-permute-start | bytes 9633800 | tf_op jit(solution)/shard_map/ppermute | solution.py:204
  2.8 3.6 %collective-permute-start = (bf16[4,224,128]{2,1,0:T(8,128)(2,1)S(1)}, bf16[4,224,128]{2,1,0:T(8,128)(2,1)S(1)}, u32[]{:S(2)}, u32[]{:S(2)}) collective-permute-start(bf16[4,224,128]{2,1,0:T(8,128)(2,1)S(1)} %prep.1.a_0_), channel_id=1, source_target_pairs={{0,1},{1,0},{2,3},{3,2},{4,5},{5,4},{6,7},{7,6},{8,9},{9,8},{10,11... | collective-permute-start | bytes 688136 | tf_op jit(solution)/shard_map/ppermute | solution.py:204
  6.6 7.3 %collective-permute-start.1 = (bf16[224,128]{1,0:T(8,128)(2,1)S(1)}, bf16[224,128]{1,0:T(8,128)(2,1)S(1)}, u32[]{:S(2)}, u32[]{:S(2)}) collective-permute-start(bf16[224,128]{1,0:T(8,128)(2,1)S(1)} %get-tuple-element.34), channel_id=1, source_target_pairs={{0,2},{1,3},{2,4},{3,5},{4,6},{5,7},{6,0},{7,1},{8,10},{9,11},{10,... | collective-permute-start | bytes 172040 | tf_op jit(solution)/shard_map/ppermute | solution.py:204
  9.6 6.8 %collective-permute-start.2 = (bf16[224,128]{1,0:T(8,128)(2,1)S(1)}, bf16[224,128]{1,0:T(8,128)(2,1)S(1)}, u32[]{:S(2)}, u32[]{:S(2)}) collective-permute-start(bf16[224,128]{1,0:T(8,128)(2,1)S(1)} %get-tuple-element.35), channel_id=1, source_target_pairs={{0,4},{1,5},{2,6},{3,7},{4,0},{5,1},{6,2},{7,3},{8,12},{9,13},{10,... | collective-permute-start | bytes 172040 | tf_op jit(solution)/shard_map/ppermute | solution.py:204
  12.2 4.6 %collective-permute-start.3 = (bf16[224,128]{1,0:T(8,128)(2,1)S(1)}, bf16[224,128]{1,0:T(8,128)(2,1)S(1)}, u32[]{:S(2)}, u32[]{:S(2)}) collective-permute-start(bf16[224,128]{1,0:T(8,128)(2,1)S(1)} %get-tuple-element.36), channel_id=1, source_target_pairs={{0,6},{1,7},{2,0},{3,1},{4,2},{5,3},{6,4},{7,5},{8,14},{9,15},{10,... | collective-permute-start | bytes 172040 | tf_op jit(solution)/shard_map/ppermute | solution.py:204
  18.6 10.1 %copy-start.1 = (bf16[1792,896]{1,0:T(8,128)(2,1)S(1)}, bf16[1792,896]{1,0:T(8,128)(2,1)}, u32[]{:S(2)}) copy-start(bf16[1792,896]{1,0:T(8,128)(2,1)} %a_1_.12) | copy-start | bytes 9633796
  20.2 8.5 %collective-permute-start.8 = (bf16[64,1792]{1,0:T(8,128)(2,1)S(1)}, bf16[64,1792]{1,0:T(8,128)(2,1)S(1)}, u32[]{:S(2)}, u32[]{:S(2)}) collective-permute-start(bf16[64,1792]{1,0:T(8,128)(2,1)S(1)} %get-tuple-element.42), channel_id=1, source_target_pairs={{0,8},{1,9},{2,26},{3,27},{4,12},{5,13},{6,30},{7,31},{8,0},{9,1},... | collective-permute-start | bytes 688136 | tf_op jit(solution)/shard_map/ppermute | solution.py:204
  20.6 11.6 %collective-permute-start.15 = (bf16[64,1792]{1,0:T(8,128)(2,1)S(1)}, bf16[64,1792]{1,0:T(8,128)(2,1)S(1)}, u32[]{:S(2)}, u32[]{:S(2)}) collective-permute-start(bf16[64,1792]{1,0:T(8,128)(2,1)S(1)} %get-tuple-element.42), channel_id=1, source_target_pairs={{0,24},{1,25},{2,26},{3,27},{4,28},{5,29},{6,30},{7,31},{8,0},{9,1... | collective-permute-start | bytes 688136 | tf_op jit(solution)/shard_map/ppermute | solution.py:204
  22.1 10.1 %collective-permute-start.14 = (bf16[64,1792]{1,0:T(8,128)(2,1)S(1)}, bf16[64,1792]{1,0:T(8,128)(2,1)S(1)}, u32[]{:S(2)}, u32[]{:S(2)}) collective-permute-start(bf16[64,1792]{1,0:T(8,128)(2,1)S(1)} %get-tuple-element.42), channel_id=1, source_target_pairs={{0,16},{1,17},{2,18},{3,19},{4,20},{5,21},{6,22},{7,23},{8,24},{9,... | collective-permute-start | bytes 688136 | tf_op jit(solution)/shard_map/ppermute | solution.py:204
  28.7 6.0 %collective-permute-start.9 = (bf16[64,1792]{1,0:T(8,128)(2,1)S(1)}, bf16[64,1792]{1,0:T(8,128)(2,1)S(1)}, u32[]{:S(2)}, u32[]{:S(2)}) collective-permute-start(bf16[64,1792]{1,0:T(8,128)(2,1)S(1)} %near.3), channel_id=1, source_target_pairs={{0,16},{1,17},{2,4},{3,5},{4,2},{5,3},{6,22},{7,23},{8,10},{9,11},... | collective-permute-start | bytes 688136 | tf_op jit(solution)/shard_map/ppermute | solution.py:204
  32.2 13.6 %collective-permute-start.16 = (f32[64,1792]{1,0:T(8,128)S(1)}, f32[64,1792]{1,0:T(8,128)S(1)}, u32[]{:S(2)}, u32[]{:S(2)}) collective-permute-start(f32[64,1792]{1,0:T(8,128)S(1)} %far.2), channel_id=1, source_target_pairs={{16,18},{17,19},{24,26},{25,27},{26,28},{27,29}} | collective-permute-start | bytes 1376264 | tf_op jit(solution)/shard_map/ppermute | solution.py:204
  34.7 11.1 %collective-permute-start.13 = (bf16[64,1792]{1,0:T(8,128)(2,1)S(1)}, bf16[64,1792]{1,0:T(8,128)(2,1)S(1)}, u32[]{:S(2)}, u32[]{:S(2)}) collective-permute-start(bf16[64,1792]{1,0:T(8,128)(2,1)S(1)} %get-tuple-element.49), channel_id=1, source_target_pairs={{0,8},{1,9},{2,26},{3,27},{4,12},{5,13},{6,30},{7,31},{8,0},{9,1},... | collective-permute-start | bytes 688136 | tf_op jit(solution)/shard_map/ppermute | solution.py:204
  37.2 14.1 %collective-permute-start.22 = (bf16[64,1792]{1,0:T(8,128)(2,1)S(1)}, bf16[64,1792]{1,0:T(8,128)(2,1)S(1)}, u32[]{:S(2)}, u32[]{:S(2)}) collective-permute-start(bf16[64,1792]{1,0:T(8,128)(2,1)S(1)} %get-tuple-element.49), channel_id=1, source_target_pairs={{0,16},{1,17},{2,18},{3,19},{4,20},{5,21},{6,22},{7,23},{8,24},{9,... | collective-permute-start | bytes 688136 | tf_op jit(solution)/shard_map/ppermute | solution.py:204
  45.8 10.4 %collective-permute-start.17 = (bf16[64,1792]{1,0:T(8,128)(2,1)S(1)}, bf16[64,1792]{1,0:T(8,128)(2,1)S(1)}, u32[]{:S(2)}, u32[]{:S(2)}) collective-permute-start(bf16[64,1792]{1,0:T(8,128)(2,1)S(1)} %near.4), channel_id=1, source_target_pairs={{0,16},{1,17},{2,4},{3,5},{4,2},{5,3},{6,22},{7,23},{8,10},{9,11},... | collective-permute-start | bytes 688136 | tf_op jit(solution)/shard_map/ppermute | solution.py:204
  51.3 5.2 %collective-permute-start.23 = (f32[64,1792]{1,0:T(8,128)S(1)}, f32[64,1792]{1,0:T(8,128)S(1)}, u32[]{:S(2)}, u32[]{:S(2)}) collective-permute-start(f32[64,1792]{1,0:T(8,128)S(1)} %far.3), channel_id=1, source_target_pairs={{26,28},{27,29}} | collective-permute-start | bytes 1376264 | tf_op jit(solution)/shard_map/ppermute | solution.py:204
  56.2 6.1 %collective-permute-start.21 = (bf16[64,1792]{1,0:T(8,128)(2,1)S(1)}, bf16[64,1792]{1,0:T(8,128)(2,1)S(1)}, u32[]{:S(2)}, u32[]{:S(2)}) collective-permute-start(bf16[64,1792]{1,0:T(8,128)(2,1)S(1)} %get-tuple-element.55), channel_id=1, source_target_pairs={{0,8},{1,9},{2,26},{3,27},{4,12},{5,13},{6,30},{7,31},{8,0},{9,1},... | collective-permute-start | bytes 688136 | tf_op jit(solution)/shard_map/ppermute | solution.py:204
  62.3 28.3 %collective-permute-start.24 = (bf16[64,1792]{1,0:T(8,128)(2,1)S(1)}, bf16[64,1792]{1,0:T(8,128)(2,1)S(1)}, u32[]{:S(2)}, u32[]{:S(2)}) collective-permute-start(bf16[64,1792]{1,0:T(8,128)(2,1)S(1)} %near.5), channel_id=1, source_target_pairs={{0,16},{1,17},{2,4},{3,5},{4,2},{5,3},{6,22},{7,23},{8,10},{9,11},... | collective-permute-start | bytes 688136 | tf_op jit(solution)/shard_map/ppermute | solution.py:204
  67.9 8.5 %collective-permute-start.5 = (f32[224,128]{1,0:T(8,128)S(1)}, f32[224,128]{1,0:T(8,128)S(1)}, u32[]{:S(2)}, u32[]{:S(2)}) collective-permute-start(f32[224,128]{1,0:T(8,128)S(1)} %get-tuple-element.39), channel_id=1, source_target_pairs={{0,2},{1,3},{2,4},{3,5},{4,6},{5,7},{6,0},{7,1},{8,10},{9,11},{10,... | collective-permute-start | bytes 344072 | tf_op jit(solution)/shard_map/ppermute | solution.py:204
  68.8 21.8 %collective-permute-start.6 = (f32[224,128]{1,0:T(8,128)S(1)}, f32[224,128]{1,0:T(8,128)S(1)}, u32[]{:S(2)}, u32[]{:S(2)}) collective-permute-start(f32[224,128]{1,0:T(8,128)S(1)} %get-tuple-element.40), channel_id=1, source_target_pairs={{0,4},{1,5},{2,6},{3,7},{4,0},{5,1},{6,2},{7,3},{8,12},{9,13},{10,... | collective-permute-start | bytes 344072 | tf_op jit(solution)/shard_map/ppermute | solution.py:204
  73.0 20.8 %collective-permute-start.7 = (f32[224,128]{1,0:T(8,128)S(1)}, f32[224,128]{1,0:T(8,128)S(1)}, u32[]{:S(2)}, u32[]{:S(2)}) collective-permute-start(f32[224,128]{1,0:T(8,128)S(1)} %get-tuple-element.41), channel_id=1, source_target_pairs={{0,6},{1,7},{2,0},{3,1},{4,2},{5,3},{6,4},{7,5},{8,14},{9,15},{10,... | collective-permute-start | bytes 344072 | tf_op jit(solution)/shard_map/ppermute | solution.py:204
  73.7 20.2 %collective-permute-start.10 = (f32[224,128]{1,0:T(8,128)S(1)}, f32[224,128]{1,0:T(8,128)S(1)}, u32[]{:S(2)}, u32[]{:S(2)}) collective-permute-start(f32[224,128]{1,0:T(8,128)S(1)} %get-tuple-element.46), channel_id=1, source_target_pairs={{0,2},{1,3},{2,4},{3,5},{4,6},{5,7},{6,0},{7,1},{8,10},{9,11},{10,... | collective-permute-start | bytes 344072 | tf_op jit(solution)/shard_map/ppermute | solution.py:204
  76.4 19.9 %collective-permute-start.11 = (f32[224,128]{1,0:T(8,128)S(1)}, f32[224,128]{1,0:T(8,128)S(1)}, u32[]{:S(2)}, u32[]{:S(2)}) collective-permute-start(f32[224,128]{1,0:T(8,128)S(1)} %get-tuple-element.47), channel_id=1, source_target_pairs={{0,4},{1,5},{2,6},{3,7},{4,0},{5,1},{6,2},{7,3},{8,12},{9,13},{10,... | collective-permute-start | bytes 344072 | tf_op jit(solution)/shard_map/ppermute | solution.py:204
  90.6 9.9 %collective-permute-start.12 = (f32[224,128]{1,0:T(8,128)S(1)}, f32[224,128]{1,0:T(8,128)S(1)}, u32[]{:S(2)}, u32[]{:S(2)}) collective-permute-start(f32[224,128]{1,0:T(8,128)S(1)} %get-tuple-element.48), channel_id=1, source_target_pairs={{0,6},{1,7},{2,0},{3,1},{4,2},{5,3},{6,4},{7,5},{8,14},{9,15},{10,... | collective-permute-start | bytes 344072 | tf_op jit(solution)/shard_map/ppermute | solution.py:204
  90.6 23.2 %copy-start.3 = (f32[224,512]{1,0:T(8,128)S(1)}, f32[224,512]{1,0:T(8,128)}, u32[]{:S(2)}) copy-start(f32[224,512]{1,0:T(8,128)} %a_1_.13) | copy-start | bytes 1376260
  90.6 23.2 %copy-start.5 = (s32[4]{0:T(128)S(1)}, s32[4]{0:T(128)}, u32[]{:S(2)}) copy-start(s32[4]{0:T(128)} %a_0_.3) | copy-start | bytes 52
  90.6 11.8 %collective-permute-start.18 = (f32[224,128]{1,0:T(8,128)S(1)}, f32[224,128]{1,0:T(8,128)S(1)}, u32[]{:S(2)}, u32[]{:S(2)}) collective-permute-start(f32[224,128]{1,0:T(8,128)S(1)} %get-tuple-element.52), channel_id=1, source_target_pairs={{0,2},{1,3},{2,4},{3,5},{4,6},{5,7},{6,0},{7,1},{8,10},{9,11},{10,... | collective-permute-start | bytes 344072 | tf_op jit(solution)/shard_map/ppermute | solution.py:204
  93.8 12.8 %collective-permute-start.19 = (f32[224,128]{1,0:T(8,128)S(1)}, f32[224,128]{1,0:T(8,128)S(1)}, u32[]{:S(2)}, u32[]{:S(2)}) collective-permute-start(f32[224,128]{1,0:T(8,128)S(1)} %get-tuple-element.53), channel_id=1, source_target_pairs={{0,4},{1,5},{2,6},{3,7},{4,0},{5,1},{6,2},{7,3},{8,12},{9,13},{10,... | collective-permute-start | bytes 344072 | tf_op jit(solution)/shard_map/ppermute | solution.py:204
  93.9 12.7 %collective-permute-start.20 = (f32[224,128]{1,0:T(8,128)S(1)}, f32[224,128]{1,0:T(8,128)S(1)}, u32[]{:S(2)}, u32[]{:S(2)}) collective-permute-start(f32[224,128]{1,0:T(8,128)S(1)} %get-tuple-element.54), channel_id=1, source_target_pairs={{0,6},{1,7},{2,0},{3,1},{4,2},{5,3},{6,4},{7,5},{8,14},{9,15},{10,... | collective-permute-start | bytes 344072 | tf_op jit(solution)/shard_map/ppermute | solution.py:204
  96.3 10.3 %collective-permute-start.25 = (f32[224,128]{1,0:T(8,128)S(1)}, f32[224,128]{1,0:T(8,128)S(1)}, u32[]{:S(2)}, u32[]{:S(2)}) collective-permute-start(f32[224,128]{1,0:T(8,128)S(1)} %get-tuple-element.58), channel_id=1, source_target_pairs={{0,2},{1,3},{2,4},{3,5},{4,6},{5,7},{6,0},{7,1},{8,10},{9,11},{10,... | collective-permute-start | bytes 344072 | tf_op jit(solution)/shard_map/ppermute | solution.py:204
  100.5 11.4 %collective-permute-start.26 = (f32[224,128]{1,0:T(8,128)S(1)}, f32[224,128]{1,0:T(8,128)S(1)}, u32[]{:S(2)}, u32[]{:S(2)}) collective-permute-start(f32[224,128]{1,0:T(8,128)S(1)} %get-tuple-element.59), channel_id=1, source_target_pairs={{0,4},{1,5},{2,6},{3,7},{4,0},{5,1},{6,2},{7,3},{8,12},{9,13},{10,... | collective-permute-start | bytes 344072 | tf_op jit(solution)/shard_map/ppermute | solution.py:204
  102.4 9.4 %collective-permute-start.27 = (f32[224,128]{1,0:T(8,128)S(1)}, f32[224,128]{1,0:T(8,128)S(1)}, u32[]{:S(2)}, u32[]{:S(2)}) collective-permute-start(f32[224,128]{1,0:T(8,128)S(1)} %get-tuple-element.60), channel_id=1, source_target_pairs={{0,6},{1,7},{2,0},{3,1},{4,2},{5,3},{6,4},{7,5},{8,14},{9,15},{10,... | collective-permute-start | bytes 344072 | tf_op jit(solution)/shard_map/ppermute | solution.py:204
  111.9 1.9 %collective-permute-start.28 = (f32[4,224,128]{2,1,0:T(8,128)S(1)}, f32[4,224,128]{2,1,0:T(8,128)S(1)}, u32[]{:S(2)}, u32[]{:S(2)}) collective-permute-start(f32[4,224,128]{2,1,0:T(8,128)S(1)} %pick.1.a_2_), channel_id=1, source_target_pairs={{0,1},{1,0},{2,3},{3,2},{4,5},{5,4},{6,7},{7,6},{8,9},{9,8},{10,11... | collective-permute-start | bytes 1376264 | tf_op jit(solution)/shard_map/ppermute | solution.py:204
  (3 other events, 3.6 us)

commit v2 on v1

v2 whole, which is shorter than its diff:
```python
import jax
import jax.numpy as jnp
from jax import lax
from jax.experimental import pallas as pl
from jax.experimental.pallas import tpu as pltpu
from jax.sharding import PartitionSpec as P


TICKS = 6
F32 = jnp.float32
BF16 = jnp.bfloat16
VM = pl.BlockSpec(memory_space=pltpu.VMEM)
SM = pl.BlockSpec(memory_space=pltpu.SMEM)


def call(kernel, outs, args, specs, scratch=(), flops=0):
    n_bytes = sum(o.size * o.dtype.itemsize for o in outs)
    return pl.pallas_call(
        kernel,
        out_shape=outs,
        in_specs=specs,
        out_specs=[VM] * len(outs),
        scratch_shapes=list(scratch),
        compiler_params=pltpu.CompilerParams(vmem_limit_bytes=24 << 20),
        cost_estimate=pl.CostEstimate(flops=flops, bytes_accessed=n_bytes, transcendentals=0),
    )(*args)


def shape(dims, dtype):
    return jax.ShapeDtypeStruct(dims, dtype)


def place():
    col = lax.axis_index("col")
    return lax.axis_index("row"), col // 2, col % 2


def panel_at(starts_ref, count, slot):
    found = jnp.int32(0)
    for p in range(count):
        found = jnp.where(starts_ref[p] == slot, jnp.int32(p), found)
    return found


def prep_kernel(count, width, starts_ref, grad_ref, out_ref):
    for slot in range(count):
        begin = pl.multiple_of(panel_at(starts_ref, count, slot) * width, width)
        out_ref[slot] = grad_ref[:, pl.ds(begin, width)].astype(out_ref.dtype)


def pack_kernel(count, width, mine_ref, other_ref, *out_refs):
    _, z, h = place()
    lanes = lax.broadcasted_iota(jnp.int32, mine_ref.shape[1:], 1)
    low = lanes < width // 2
    for k in range(count):
        slot = z ^ k
        mine = mine_ref[slot].astype(F32)
        other = other_ref[slot].astype(F32)
        first = jnp.where(h == 0, mine, pltpu.roll(other, width // 2, 1))
        second = jnp.where(h == 0, pltpu.roll(other, width // 2, 1), mine)
        out_refs[k][...] = jnp.where(low, first, second).astype(out_refs[k].dtype)


def solve(x_ref, xb_ref, rhs, own_ref, other_ref):
    half = own_ref.shape[1]
    left = jnp.dot(rhs, own_ref[...], preferred_element_type=F32)
    right = jnp.dot(rhs, other_ref[...], preferred_element_type=F32)
    x_ref[:, :half] = left
    x_ref[:, half:] = right
    xb_ref[:, :half] = left.astype(BF16)
    xb_ref[:, half:] = right.astype(BF16)


def solve(rhs, own_ref, other_ref, x_ref, xb_ref):
    half = own_ref.shape[1]
    left = jnp.dot(rhs, own_ref[...], preferred_element_type=F32)
    right = jnp.dot(rhs, other_ref[...], preferred_element_type=F32)
    xb_ref[:, :half] = left.astype(BF16)
    xb_ref[:, half:] = right.astype(BF16)
    x_ref[:, :half] = left
    x_ref[:, half:] = right


def load_kernel(tile_ref, _, out_ref, sem):
    copy = pltpu.make_async_copy(tile_ref, out_ref, sem)
    copy.start()
    copy.wait()


def first_kernel(count, *refs):
    pieces = refs[:count]
    own_ref, other_ref, x_ref, xb_ref, grad_ref, natural = refs[count:]
    r, z, _ = place()
    rows, width = pieces[0].shape
    for k in range(count):
        source = z ^ k
        piece = pieces[k][...].astype(F32)
        top = pl.multiple_of(source * (2 * rows), 8)
        natural[pl.ds(top, rows), :] = piece
        natural[pl.ds(pl.multiple_of(top + rows, 8), rows), :] = pltpu.roll(piece, width // 2, 1)
    grad_ref[...] = jnp.transpose(natural[...])[: width // 2].astype(BF16)

    @pl.when(r == z)
    def _():
        solve(grad_ref[...], own_ref, other_ref, x_ref, xb_ref)


def solve_kernel(tick, rhs_ref, own_ref, other_ref, x_ref, xb_ref):
    r, z, _ = place()

    @pl.when((r == z) & (z >= tick))
    def _():
        solve(rhs_ref[...], own_ref, other_ref, x_ref, xb_ref)


def turn_kernel(own_ref, other_ref, _, out_ref):
    r, z, _ = place()
    half = own_ref.shape[1]

    @pl.when(r > z)
    def _():
        out_ref[:half] = jnp.transpose(own_ref[...])
        out_ref[half:] = jnp.transpose(other_ref[...])


def near_kernel(tick, x_ref, grad_ref, turned_ref, *refs):
    out_ref = refs[-1]
    r, z, _ = place()

    @pl.when((r == z + 1) & (z >= tick))
    def _():
        value = grad_ref[...].astype(F32)
        if tick:
            value = value - refs[0][...].astype(F32)
        value = value - jnp.dot(x_ref[...], turned_ref[...], preferred_element_type=F32)
        out_ref[...] = value.astype(out_ref.dtype)


def far_kernel(tick, final, turned_ref, *refs):
    out_ref = refs[-1]
    before = refs[0] if tick else None
    grad_ref = refs[1] if final else None
    x_refs = refs[(1 if tick else 0) + (1 if final else 0) : -1]
    r, z, _ = place()
    for i, x_ref in enumerate(x_refs):

        @pl.when((r == z + 2 + i) & (z >= tick))
        def _():
            value = jnp.dot(x_ref[...], turned_ref[...], preferred_element_type=F32)
            if before is not None:
                value = value + before[...].astype(F32)
            if grad_ref is not None:
                value = grad_ref[...].astype(F32) - value
            out_ref[...] = value.astype(out_ref.dtype)


def fold(x_ref, natural):
    _, _, h = place()
    half, width = x_ref.shape[1] // 2, natural.shape[1]

    @pl.when(h == 0)
    def _():
        natural[: 2 * half, : width // 2] = jnp.transpose(x_ref[...])

    @pl.when(h == 1)
    def _():
        natural[half : 2 * half, : width // 2] = jnp.transpose(x_ref[:, :half])
        natural[:half, : width // 2] = jnp.transpose(x_ref[:, half:])


def folded(natural, rows, target):
    width = natural.shape[1]
    lanes = lax.broadcasted_iota(jnp.int32, (rows, width), 1)
    top = pl.multiple_of(target * (2 * rows), 8)
    upper = natural[pl.ds(top, rows), :]
    lower = natural[pl.ds(pl.multiple_of(top + rows, 8), rows), :]
    return jnp.where(lanes < width // 2, upper, pltpu.roll(lower, width // 2, 1))


def early_kernel(count, n_parts, *refs):
    x_refs, out_refs, natural = refs[:n_parts], refs[n_parts:-1], refs[-1]
    r, z, _ = place()
    rows = out_refs[0].shape[1]

    @pl.when(r == z)
    def _():
        for t in range(n_parts):
            fold(x_refs[t], natural)
            for k in range(count):
                out_refs[k][t] = folded(natural, rows, z ^ k)


def last_kernel(count, x_ref, *refs):
    out_refs, natural = refs[:-1], refs[-1]
    _, z, _ = place()
    rows = out_refs[0].shape[0]
    fold(x_ref, natural)
    for k in range(count):
        out_refs[k][...] = folded(natural, rows, z ^ k).astype(out_refs[k].dtype)


def pick_early_kernel(count, *refs):
    out_ref = refs[-1]
    r, z, _ = place()
    first = 0
    for group in range(0, len(refs) - 1, count):
        parts = refs[group].shape[0]
        for k in range(count):

            @pl.when((z ^ r) == k)
            def _():
                out_ref[first : first + parts] = refs[group + k][...]

        first += parts


def pick_last_kernel(count, ticks, *refs):
    out_ref = refs[-1]
    r, z, _ = place()
    for k in range(count):
        source = z ^ k

        @pl.when((source >= ticks - 1) & (source <= r))
        def _():
            out_ref[source - (ticks - 1)] = refs[k][...]


def join(mine, other, h):
    width = mine.shape[1]
    lanes = lax.broadcasted_iota(jnp.int32, mine.shape, 1)
    other = pltpu.roll(other.astype(F32), width // 2, 1)
    mine = mine.astype(F32)
    low = jnp.where(h == 0, mine, other)
    high = jnp.where(h == 0, other, mine)
    return jnp.where(lanes < width // 2, low, high)


def put_early_kernel(count, ticks, starts_ref, grad_ref, mine_ref, other_ref, out_ref):
    r, _, h = place()
    width = mine_ref.shape[2]
    for s in range(count):
        begin = pl.multiple_of(panel_at(starts_ref, count, s) * width, width)

        @pl.when(r < s)
        def _():
            out_ref[:, pl.ds(begin, width)] = grad_ref[:, pl.ds(begin, width)]

        @pl.when((r >= s) & (r - s <= ticks - 2))
        def _():
            t = r - s
            out_ref[:, pl.ds(begin, width)] = join(mine_ref[t], other_ref[t], h)


def put_last_kernel(count, ticks, starts_ref, early_ref, mine_ref, other_ref, out_ref):
    r, _, h = place()
    width = mine_ref.shape[2]
    out_ref[...] = early_ref[...]
    for s in range(count - ticks + 1):
        begin = pl.multiple_of(panel_at(starts_ref, count, s) * width, width)

        @pl.when(r - s >= ticks - 1)
        def _():
            out_ref[:, pl.ds(begin, width)] = join(mine_ref[s], other_ref[s], h)


def early_groups(ticks):
    if ticks < 3:
        return {ticks - 2: list(range(ticks - 1))}
    groups = {t: [t - 1] for t in range(1, ticks - 1)}
    groups[ticks - 2].append(ticks - 2)
    return groups


def body(factor, gradient, starts):
    count = starts.shape[0]
    ticks = min(TICKS, count)
    rows = gradient.shape[0]
    width = gradient.shape[1] // count
    tile, _ = factor.shape
    cols = width // 2
    devices = [(r, z, h) for r in range(count) for z in range(count) for h in range(2)]

    def move(array, target):
        pairs = []
        for r, z, h in devices:
            goal = target(r, z, h)
            if goal is not None:
                pairs.append(((r * count + z) * 2 + h, (goal[0] * count + goal[1]) * 2 + goal[2]))
        return lax.ppermute(array, ("row", "col"), pairs)

    def cores(array):
        return move(array, lambda r, z, h: (r, z, 1 - h))

    def along(array, k):
        return move(array, lambda r, z, h: (r, z ^ k, h))

    def from_diagonal(array, k):
        return move(array, lambda r, z, h: (r, z ^ k, h) if r == z else None)

    def to_far_row(array, tick, d):
        def target(r, z, h):
            return (r + d, z, h) if r == z and z >= tick and r + d < count else None

        return move(array, target)

    def to_next_row(array):
        def target(r, z, h):
            return (z % 2 + ((r - z % 2) % count ^ 1)) % count, z, h

        return move(array, target)

    def to_next_col(array):
        def target(r, z, h):
            base = z - z % 2 if r % 2 else z - 1 + z % 2
            if base < 0 or base + 1 >= count:
                return r ^ 2, z, h
            lead = (r ^ 2) == base + 1 or (r != base + 1 and r & 2)
            if (z == base) == (not lead):
                return r, base + 1 if z == base else base, h
            return r ^ 2, z, h

        return move(array, target)

    def far_to_next_col(array, tick):
        def target(r, z, h):
            return (r, z + 1, h) if r >= z + 2 and z >= tick else None

        return move(array, target)

    flops = 2 * cols * tile * tile
    mine = call(
        lambda *a: prep_kernel(count, width, *a),
        [shape((count, rows, width), BF16)], (starts, gradient), [SM, VM],
    )[0]
    theirs = cores(mine)
    pieces = call(
        lambda *a: pack_kernel(count, width, *a),
        [shape((rows, width), BF16)] * count, (mine, theirs), [VM, VM],
    )
    arrived = [pieces[0]] + [along(pieces[k], k) for k in range(1, count)]
    other_tile = cores(factor)
    own_tile = call(
        load_kernel, [shape(factor.shape, BF16)], (factor, pieces[0]),
        [pl.BlockSpec(memory_space=pl.ANY), VM], [pltpu.SemaphoreType.DMA],
    )[0]
    wide = [shape((cols, tile), F32), shape((cols, tile), BF16)]
    x, xb, grad = call(
        lambda *a: first_kernel(count, *a),
        wide + [shape((cols, tile), BF16)], (*arrived, own_tile, other_tile), [VM] * (count + 2),
        [pltpu.VMEM((tile, width), F32)], flops,
    )
    turned = call(turn_kernel, [shape((tile, tile), BF16)], (own_tile, other_tile, xb), [VM] * 3)[0]
    groups = early_groups(ticks) if ticks > 1 else {}
    xs, before, sent_early = [], None, []
    for tick in range(ticks):
        final = tick == ticks - 1
        if tick:
            x, xb = call(
                lambda *a: solve_kernel(tick, *a),
                wide, (rhs, own_tile, other_tile), [VM] * 3, (), flops,
            )
        result = x
        xs.append(x)
        if count - 1 > tick:
            dtype = F32 if final else BF16
            near = to_next_row(xb)
            far = [to_far_row(xb, tick, d) for d in range(2, count - tick)]
            carried = [before] if tick else []
            out = call(
                lambda *a: near_kernel(tick, *a),
                [shape((cols, tile), dtype)], (near, grad, turned, *carried),
                [VM] * (3 + len(carried)), (), flops,
            )[0]
            if final:
                r, z, _ = place()
                result = jnp.where(r == z, x, out)
                carried = carried + [grad]
            else:
                rhs = to_next_col(out)
            if far:
                if not final:
                    grad = far_to_next_col(grad, tick)
                out = call(
                    lambda *a: far_kernel(tick, final, *a),
                    [shape((cols, tile), dtype)], (turned, *carried, *far),
                    [VM] * (1 + len(carried) + len(far)), (), flops,
                )[0]
                if final:
                    result = jnp.where(r >= z + 2, out, result)
                else:
                    before = far_to_next_col(out, tick)
        if tick in groups:
            members = groups[tick]
            parts = call(
                lambda *a: early_kernel(count, len(members), *a),
                [shape((len(members), rows, width), F32)] * count, tuple(xs[t] for t in members),
                [VM] * len(members), [pltpu.VMEM((tile, width), F32)],
            )
            sent_early += [parts[0]]
            sent_early += [from_diagonal(parts[k], k) for k in range(1, count)]
    parts = call(
        lambda *a: last_kernel(count, *a),
        [shape((rows, width), BF16)] * count, (result,), [VM],
        [pltpu.VMEM((tile, width), F32)],
    )
    sent = [parts[0]] + [along(parts[k], k) for k in range(1, count)]
    mine = call(
        lambda *a: pick_early_kernel(count, *a),
        [shape((ticks - 1, rows, width), F32)], sent_early, [VM] * len(sent_early),
    )[0]
    theirs = cores(mine)
    early = call(
        lambda *a: put_early_kernel(count, ticks, *a),
        [shape(gradient.shape, F32)], (starts, gradient, mine, theirs), [SM, VM, VM, VM],
    )[0]
    mine = call(
        lambda *a: pick_last_kernel(count, ticks, *a),
        [shape((count - ticks + 1, rows, width), BF16)], sent, [VM] * count,
    )[0]
    theirs = cores(mine)
    return call(
        lambda *a: put_last_kernel(count, ticks, *a),
        [shape(gradient.shape, F32)], (starts, early, mine, theirs), [SM, VM, VM, VM],
    )[0]


def solution(mesh):
    in_specs = (P("row", "col"), P(("row", "col"), None), P())
    out_specs = P(("row", "col"), None)

    return jax.shard_map(body, mesh=mesh, in_specs=in_specs, out_specs=out_specs, check_vma=False)
```

time: 116 us -> 96.1 us (0.83)
  starting transfers between devices: 59.8 us -> 44.7 us
  waiting for transfers between devices: 45.3 us -> 39.6 us
    ppermute x29, starting transfers between devices: 59.8 us -> 44.7 us  [move(): return lax.ppermute(array, ('row', 'col'), pairs)]
    ppermute x29, waiting for transfers between devices: 45.3 us -> 39.6 us  [move(): return lax.ppermute(array, ('row', 'col'), pairs)]
    pallas_call x17 -> x20, Pallas kernels: 6.51 us -> 7.44 us  [call(): pl.pallas_call(kernel, out_shape=outs, in_specs=specs, out_specs=[VM] * l...]
    unnamed x12 -> x10, local copies, waits for them, and re-layouts: 3.6 us -> 3.59 us
  transfers between devices with their start and end apart: 29 -> 29, of which waited for: 15 -> 13; matrix products, arithmetic and copies ran while one was open for 0% -> 0% of each run, Pallas kernels for 3% -> 5%
where the time goes in v2:
time: 96.1 us; the launch traced here: 95.7 us
  starting transfers between devices  44.7 us (47%)
  waiting for transfers between devices  39.6 us (41%)
  Pallas kernels  7.44 us (8%)
  local copies, waits for them, and re-layouts  3.59 us (4%)
    ppermute x29, starting transfers between devices, move(): return lax.ppermute(array, ('row', 'col'), pairs)  44.7 us
    ppermute x29, waiting for transfers between devices, move(): return lax.ppermute(array, ('row', 'col'), pairs)  39.6 us
    pallas_call x20, Pallas kernels, call(): pl.pallas_call(kernel, out_shape=outs, in_specs=specs, out_specs=[VM] * l...  7.44 us
    unnamed x10, local copies, waits for them, and re-layouts  3.59 us
  transfers between devices with their start and end apart: 29, of which 13 were waited for; matrix products, arithmetic and copies ran while one was open for 0% of the time, Pallas kernels for 5%

profile of v2, /device:TPU:0, one launch (start us, length us, event | category | flops | bytes accessed | tf_op | source)
XLA Modules:
  0.0 95.7 jit_solution(9794229003898681547)
XLA Ops:
  0.5 1.0 %copy-done.1 = f32[224,512]{1,0:T(8,128)S(1)} copy-done((f32[224,512]{1,0:T(8,128)S(1)}, f32[224,512]{1,0:T(8,128)}, u32[]{:S(2)}) %copy-start.1) | copy-done | bytes 458776
  2.9 3.5 %collective-permute-done.a_1_ = bf16[4,224,128]{2,1,0:T(8,128)(2,1)S(1)} collective-permute-done((bf16[4,224,128]{2,1,0:T(8,128)(2,1)S(1)}, bf16[4,224,128]{2,1,0:T(8,128)(2,1)S(1)}, u32[]{:S(2)}, u32[]{:S(2)}) %collective-permute-start) | collective-permute-done | bytes 229408 | tf_op jit(solution)/shard_map/ppermute | solution.py:289
  6.6 3.0 %collective-permute-start.1 = (bf16[224,128]{1,0:T(8,128)(2,1)S(1)}, bf16[224,128]{1,0:T(8,128)(2,1)S(1)}, u32[]{:S(2)}, u32[]{:S(2)}) collective-permute-start(bf16[224,128]{1,0:T(8,128)(2,1)S(1)} %get-tuple-element.30), channel_id=1, source_target_pairs={{0,2},{1,3},{2,0},{3,1},{4,6},{5,7},{6,4},{7,5},{8,10},{9,11},{10,... | collective-permute-start | bytes 172040 | tf_op jit(solution)/shard_map/ppermute | solution.py:289
  9.6 2.6 %collective-permute-start.2 = (bf16[224,128]{1,0:T(8,128)(2,1)S(1)}, bf16[224,128]{1,0:T(8,128)(2,1)S(1)}, u32[]{:S(2)}, u32[]{:S(2)}) collective-permute-start(bf16[224,128]{1,0:T(8,128)(2,1)S(1)} %get-tuple-element.31), channel_id=1, source_target_pairs={{0,4},{1,5},{2,6},{3,7},{4,0},{5,1},{6,2},{7,3},{8,12},{9,13},{10,... | collective-permute-start | bytes 172040 | tf_op jit(solution)/shard_map/ppermute | solution.py:289
  12.2 1.9 %copy-done = bf16[1792,896]{1,0:T(8,128)(2,1)S(1)} copy-done((bf16[1792,896]{1,0:T(8,128)(2,1)S(1)}, bf16[1792,896]{1,0:T(8,128)(2,1)}, u32[]{:S(2)}) %copy-start) | copy-done | bytes 3211288
  14.4 1.6 %collective-permute-done.2.a_2_ = bf16[224,128]{1,0:T(8,128)(2,1)S(1)} collective-permute-done((bf16[224,128]{1,0:T(8,128)(2,1)S(1)}, bf16[224,128]{1,0:T(8,128)(2,1)S(1)}, u32[]{:S(2)}, u32[]{:S(2)}) %collective-permute-start.2) | collective-permute-done | bytes 57376 | tf_op jit(solution)/shard_map/ppermute | solution.py:289
  16.0 2.2 %collective-permute-done.3.a_3_ = bf16[224,128]{1,0:T(8,128)(2,1)S(1)} collective-permute-done((bf16[224,128]{1,0:T(8,128)(2,1)S(1)}, bf16[224,128]{1,0:T(8,128)(2,1)S(1)}, u32[]{:S(2)}, u32[]{:S(2)}) %collective-permute-start.3) | collective-permute-done | bytes 57376 | tf_op jit(solution)/shard_map/ppermute | solution.py:289
  18.2 1.4 %shard_map.40 = (f32[64,1792]{1,0:T(8,128)S(1)}, bf16[64,1792]{1,0:T(8,128)(2,1)S(1)}, bf16[64,1792]{1,0:T(8,128)(2,1)S(1)}) custom-call(bf16[224,128]{1,0:T(8,128)(2,1)S(1)} %get-tuple-element.29._.a_0_, bf16[224,128]{1,0:T(8,128)(2,1)S(1)} %collective-permute-done.1.a_1_, bf16[224,128]{1,0:T(8,128)(2,1)S(1)} %collective-permute-done.2.a_2_, ...), custom_call_target="tpu_custom_call" | custom-call | flops 411041792 | bytes 917504 | tf_op jit(solution)/shard_map/pallas_call | solution.py:18
  20.0 3.4 %collective-permute-start.12 = (bf16[64,1792]{1,0:T(8,128)(2,1)S(1)}, bf16[64,1792]{1,0:T(8,128)(2,1)S(1)}, u32[]{:S(2)}, u32[]{:S(2)}) collective-permute-start(bf16[64,1792]{1,0:T(8,128)(2,1)S(1)} %get-tuple-element.38._), channel_id=1, source_target_pairs={{0,16},{1,17},{10,26},{11,27}} | collective-permute-start | bytes 688136 | tf_op jit(solution)/shard_map/ppermute | solution.py:289
  23.5 1.3 %collective-permute-start.13 = (bf16[64,1792]{1,0:T(8,128)(2,1)S(1)}, bf16[64,1792]{1,0:T(8,128)(2,1)S(1)}, u32[]{:S(2)}, u32[]{:S(2)}) collective-permute-start(bf16[64,1792]{1,0:T(8,128)(2,1)S(1)} %get-tuple-element.38._), channel_id=1, source_target_pairs={{0,24},{1,25}} | collective-permute-start | bytes 688136 | tf_op jit(solution)/shard_map/ppermute | solution.py:289
  24.8 0.8 collective-permute-done.8.a_0_
  26.8 2.4 %collective-permute-done.12.a_1_ = bf16[64,1792]{1,0:T(8,128)(2,1)S(1)} collective-permute-done((bf16[64,1792]{1,0:T(8,128)(2,1)S(1)}, bf16[64,1792]{1,0:T(8,128)(2,1)S(1)}, u32[]{:S(2)}, u32[]{:S(2)}) %collective-permute-start.12) | collective-permute-done | bytes 229408 | tf_op jit(solution)/shard_map/ppermute | solution.py:289
  29.8 1.8 %collective-permute-done.9.a_0_ = bf16[64,1792]{1,0:T(8,128)(2,1)S(1)} collective-permute-done((bf16[64,1792]{1,0:T(8,128)(2,1)S(1)}, bf16[64,1792]{1,0:T(8,128)(2,1)S(1)}, u32[]{:S(2)}, u32[]{:S(2)}) %collective-permute-start.9) | collective-permute-done | bytes 229408 | tf_op jit(solution)/shard_map/ppermute | solution.py:289
  31.6 2.2 %collective-permute-start.10 = (bf16[64,1792]{1,0:T(8,128)(2,1)S(1)}, bf16[64,1792]{1,0:T(8,128)(2,1)S(1)}, u32[]{:S(2)}, u32[]{:S(2)}) collective-permute-start(bf16[64,1792]{1,0:T(8,128)(2,1)S(1)} %get-tuple-element.41), channel_id=1, source_target_pairs={{0,8},{1,9},{2,26},{3,27},{4,12},{5,13},{6,30},{7,31},{8,0},{9,1},... | collective-permute-start | bytes 688136 | tf_op jit(solution)/shard_map/ppermute | solution.py:289
  34.5 3.3 %collective-permute-done.10.a_0_ = bf16[64,1792]{1,0:T(8,128)(2,1)S(1)} collective-permute-done((bf16[64,1792]{1,0:T(8,128)(2,1)S(1)}, bf16[64,1792]{1,0:T(8,128)(2,1)S(1)}, u32[]{:S(2)}, u32[]{:S(2)}) %collective-permute-start.10) | collective-permute-done | bytes 229408 | tf_op jit(solution)/shard_map/ppermute | solution.py:289
  37.9 4.5 %collective-permute-start.15 = (bf16[64,1792]{1,0:T(8,128)(2,1)S(1)}, bf16[64,1792]{1,0:T(8,128)(2,1)S(1)}, u32[]{:S(2)}, u32[]{:S(2)}) collective-permute-start(bf16[64,1792]{1,0:T(8,128)(2,1)S(1)} %shard_map.46), channel_id=1, source_target_pairs={{0,16},{1,17},{2,18},{3,19},{4,2},{5,3},{6,22},{7,23},{8,10},{9,11... | collective-permute-start | bytes 688136 | tf_op jit(solution)/shard_map/ppermute | solution.py:289
  43.5 4.8 %collective-permute-start.5 = (f32[1,224,128]{2,1,0:T(8,128)S(1)}, f32[1,224,128]{2,1,0:T(8,128)S(1)}, u32[]{:S(2)}, u32[]{:S(2)}) collective-permute-start(f32[1,224,128]{2,1,0:T(8,128)S(1)} %get-tuple-element.35), channel_id=1, source_target_pairs={{0,2},{1,3},{10,8},{11,9},{20,22},{21,23},{30,28},{31,29}} | collective-permute-start | bytes 344072 | tf_op jit(solution)/shard_map/ppermute | solution.py:289
  49.8 1.1 %shard_map.48 = (f32[2,224,128]{2,1,0:T(8,128)S(1)}, f32[2,224,128]{2,1,0:T(8,128)S(1)}, f32[2,224,128]{2,1,0:T(8,128)S(1)}, f32[2,224,128]{2,1,0:T(8,128)S(1)}) custom-call(f32[64,1792]{1,0:T(8,128)S(1)} %get-tuple-element.40.a_0_, f32[64,1792]{1,0:T(8,128)S(1)} %get-tuple-element.42.a_1_), custom_call_target="tpu_custom_call" | custom-call | bytes 917504 | tf_op jit(solution)/shard_map/pallas_call | solution.py:18
  50.9 7.2 %collective-permute-start.16 = (f32[2,224,128]{2,1,0:T(8,128)S(1)}, f32[2,224,128]{2,1,0:T(8,128)S(1)}, u32[]{:S(2)}, u32[]{:S(2)}) collective-permute-start(f32[2,224,128]{2,1,0:T(8,128)S(1)} %get-tuple-element.44), channel_id=1, source_target_pairs={{0,2},{1,3},{10,8},{11,9},{20,22},{21,23},{30,28},{31,29}} | collective-permute-start | bytes 688136 | tf_op jit(solution)/shard_map/ppermute | solution.py:289
  58.1 1.3 %collective-permute-start.17 = (f32[2,224,128]{2,1,0:T(8,128)S(1)}, f32[2,224,128]{2,1,0:T(8,128)S(1)}, u32[]{:S(2)}, u32[]{:S(2)}) collective-permute-start(f32[2,224,128]{2,1,0:T(8,128)S(1)} %get-tuple-element.45), channel_id=1, source_target_pairs={{0,4},{1,5},{10,14},{11,15},{20,16},{21,17},{30,26},{31,27}} | collective-permute-start | bytes 688136 | tf_op jit(solution)/shard_map/ppermute | solution.py:289
  59.4 1.3 %collective-permute-start.18 = (f32[2,224,128]{2,1,0:T(8,128)S(1)}, f32[2,224,128]{2,1,0:T(8,128)S(1)}, u32[]{:S(2)}, u32[]{:S(2)}) collective-permute-start(f32[2,224,128]{2,1,0:T(8,128)S(1)} %get-tuple-element.46), channel_id=1, source_target_pairs={{0,6},{1,7},{10,12},{11,13},{20,18},{21,19},{30,24},{31,25}} | collective-permute-start | bytes 688136 | tf_op jit(solution)/shard_map/ppermute | solution.py:289
  60.7 1.3 %collective-permute-start.6 = (f32[1,224,128]{2,1,0:T(8,128)S(1)}, f32[1,224,128]{2,1,0:T(8,128)S(1)}, u32[]{:S(2)}, u32[]{:S(2)}) collective-permute-start(f32[1,224,128]{2,1,0:T(8,128)S(1)} %get-tuple-element.36), channel_id=1, source_target_pairs={{0,4},{1,5},{10,14},{11,15},{20,16},{21,17},{30,26},{31,27}} | collective-permute-start | bytes 344072 | tf_op jit(solution)/shard_map/ppermute | solution.py:289
  62.1 1.3 %collective-permute-start.7 = (f32[1,224,128]{2,1,0:T(8,128)S(1)}, f32[1,224,128]{2,1,0:T(8,128)S(1)}, u32[]{:S(2)}, u32[]{:S(2)}) collective-permute-start(f32[1,224,128]{2,1,0:T(8,128)S(1)} %get-tuple-element.37), channel_id=1, source_target_pairs={{0,6},{1,7},{10,12},{11,13},{20,18},{21,19},{30,24},{31,25}} | collective-permute-start | bytes 344072 | tf_op jit(solution)/shard_map/ppermute | solution.py:289
  63.4 12.9 %collective-permute-done.6.a_2_ = f32[1,224,128]{2,1,0:T(8,128)S(1)} collective-permute-done((f32[1,224,128]{2,1,0:T(8,128)S(1)}, f32[1,224,128]{2,1,0:T(8,128)S(1)}, u32[]{:S(2)}, u32[]{:S(2)}) %collective-permute-start.6) | collective-permute-done | bytes 114720 | tf_op jit(solution)/shard_map/ppermute | solution.py:289
  76.3 1.2 %collective-permute-done.7.a_3_ = f32[1,224,128]{2,1,0:T(8,128)S(1)} collective-permute-done((f32[1,224,128]{2,1,0:T(8,128)S(1)}, f32[1,224,128]{2,1,0:T(8,128)S(1)}, u32[]{:S(2)}, u32[]{:S(2)}) %collective-permute-start.7) | collective-permute-done | bytes 114720 | tf_op jit(solution)/shard_map/ppermute | solution.py:289
  77.8 4.6 %collective-permute-done.24.a_0_ = bf16[64,1792]{1,0:T(8,128)(2,1)S(1)} collective-permute-done((bf16[64,1792]{1,0:T(8,128)(2,1)S(1)}, bf16[64,1792]{1,0:T(8,128)(2,1)S(1)}, u32[]{:S(2)}, u32[]{:S(2)}) %collective-permute-start.24) | collective-permute-done | bytes 229408 | tf_op jit(solution)/shard_map/ppermute | solution.py:289
  83.5 2.0 %collective-permute-start.25 = (bf16[224,128]{1,0:T(8,128)(2,1)S(1)}, bf16[224,128]{1,0:T(8,128)(2,1)S(1)}, u32[]{:S(2)}, u32[]{:S(2)}) collective-permute-start(bf16[224,128]{1,0:T(8,128)(2,1)S(1)} %get-tuple-element.50), channel_id=1, source_target_pairs={{0,2},{1,3},{2,0},{3,1},{4,6},{5,7},{6,4},{7,5},{8,10},{9,11},{10,... | collective-permute-start | bytes 172040 | tf_op jit(solution)/shard_map/ppermute | solution.py:289
  85.5 1.5 %collective-permute-start.26 = (bf16[224,128]{1,0:T(8,128)(2,1)S(1)}, bf16[224,128]{1,0:T(8,128)(2,1)S(1)}, u32[]{:S(2)}, u32[]{:S(2)}) collective-permute-start(bf16[224,128]{1,0:T(8,128)(2,1)S(1)} %get-tuple-element.51), channel_id=1, source_target_pairs={{0,4},{1,5},{2,6},{3,7},{4,0},{5,1},{6,2},{7,3},{8,12},{9,13},{10,... | collective-permute-start | bytes 172040 | tf_op jit(solution)/shard_map/ppermute | solution.py:289
  87.0 1.4 %collective-permute-start.27 = (bf16[224,128]{1,0:T(8,128)(2,1)S(1)}, bf16[224,128]{1,0:T(8,128)(2,1)S(1)}, u32[]{:S(2)}, u32[]{:S(2)}) collective-permute-start(bf16[224,128]{1,0:T(8,128)(2,1)S(1)} %get-tuple-element.52), channel_id=1, source_target_pairs={{0,6},{1,7},{2,4},{3,5},{4,2},{5,3},{6,0},{7,1},{8,14},{9,15},{10,... | collective-permute-start | bytes 172040 | tf_op jit(solution)/shard_map/ppermute | solution.py:289
  88.4 2.1 %collective-permute-done.26.a_2_ = bf16[224,128]{1,0:T(8,128)(2,1)S(1)} collective-permute-done((bf16[224,128]{1,0:T(8,128)(2,1)S(1)}, bf16[224,128]{1,0:T(8,128)(2,1)S(1)}, u32[]{:S(2)}, u32[]{:S(2)}) %collective-permute-start.26) | collective-permute-done | bytes 57376 | tf_op jit(solution)/shard_map/ppermute | solution.py:289
  90.6 2.5 %collective-permute-done.27.a_3_ = bf16[224,128]{1,0:T(8,128)(2,1)S(1)} collective-permute-done((bf16[224,128]{1,0:T(8,128)(2,1)S(1)}, bf16[224,128]{1,0:T(8,128)(2,1)S(1)}, u32[]{:S(2)}, u32[]{:S(2)}) %collective-permute-start.27) | collective-permute-done | bytes 57376 | tf_op jit(solution)/shard_map/ppermute | solution.py:289
  94.3 1.3 %shard_map.56 = f32[224,512]{1,0:T(8,128)} custom-call(s32[4]{0:T(128)S(1)} %copy-done.4, f32[224,512]{1,0:T(8,128)S(1)} %shard_map.50.a_1_, bf16[1,224,128]{2,1,0:T(8,128)(2,1)S(1)} %shard_map.55.a_2_, bf16[1,224,128]{2,1,0:T(8,128)(2,1)S(1)} %collective-permute-done.28.a_3_), custom_call_target="tpu_custom_call" | custom-call | bytes 458752 | tf_op jit(solution)/shard_map/pallas_call | solution.py:18
  (56 shorter events, 10.4 us)
Async XLA Ops:
  0.0 18.2 %collective-permute-start.4 = (bf16[1792,896]{1,0:T(8,128)(2,1)}, bf16[1792,896]{1,0:T(8,128)(2,1)S(1)}, u32[]{:S(2)}, u32[]{:S(2)}) collective-permute-start(bf16[1792,896]{1,0:T(8,128)(2,1)} %tile_ref.1), channel_id=1, source_target_pairs={{0,1},{1,0},{2,3},{3,2},{4,5},{5,4},{6,7},{7,6},{8,9},{9,8},{10,11... | collective-permute-start | bytes 9633800 | tf_op jit(solution)/shard_map/ppermute | solution.py:289
  2.8 3.6 %collective-permute-start = (bf16[4,224,128]{2,1,0:T(8,128)(2,1)S(1)}, bf16[4,224,128]{2,1,0:T(8,128)(2,1)S(1)}, u32[]{:S(2)}, u32[]{:S(2)}) collective-permute-start(bf16[4,224,128]{2,1,0:T(8,128)(2,1)S(1)} %shard_map.37.a_0_), channel_id=1, source_target_pairs={{0,1},{1,0},{2,3},{3,2},{4,5},{5,4},{6,7},{7,6},{8,9},{9,8},{10,11... | collective-permute-start | bytes 688136 | tf_op jit(solution)/shard_map/ppermute | solution.py:289
  6.6 7.8 %collective-permute-start.1 = (bf16[224,128]{1,0:T(8,128)(2,1)S(1)}, bf16[224,128]{1,0:T(8,128)(2,1)S(1)}, u32[]{:S(2)}, u32[]{:S(2)}) collective-permute-start(bf16[224,128]{1,0:T(8,128)(2,1)S(1)} %get-tuple-element.30), channel_id=1, source_target_pairs={{0,2},{1,3},{2,0},{3,1},{4,6},{5,7},{6,4},{7,5},{8,10},{9,11},{10,... | collective-permute-start | bytes 172040 | tf_op jit(solution)/shard_map/ppermute | solution.py:289
  9.6 6.4 %collective-permute-start.2 = (bf16[224,128]{1,0:T(8,128)(2,1)S(1)}, bf16[224,128]{1,0:T(8,128)(2,1)S(1)}, u32[]{:S(2)}, u32[]{:S(2)}) collective-permute-start(bf16[224,128]{1,0:T(8,128)(2,1)S(1)} %get-tuple-element.31), channel_id=1, source_target_pairs={{0,4},{1,5},{2,6},{3,7},{4,0},{5,1},{6,2},{7,3},{8,12},{9,13},{10,... | collective-permute-start | bytes 172040 | tf_op jit(solution)/shard_map/ppermute | solution.py:289
  12.2 6.0 %collective-permute-start.3 = (bf16[224,128]{1,0:T(8,128)(2,1)S(1)}, bf16[224,128]{1,0:T(8,128)(2,1)S(1)}, u32[]{:S(2)}, u32[]{:S(2)}) collective-permute-start(bf16[224,128]{1,0:T(8,128)(2,1)S(1)} %get-tuple-element.32), channel_id=1, source_target_pairs={{0,6},{1,7},{2,4},{3,5},{4,2},{5,3},{6,0},{7,1},{8,14},{9,15},{10,... | collective-permute-start | bytes 172040 | tf_op jit(solution)/shard_map/ppermute | solution.py:289
  12.2 1.9 %copy-start = (bf16[1792,896]{1,0:T(8,128)(2,1)S(1)}, bf16[1792,896]{1,0:T(8,128)(2,1)}, u32[]{:S(2)}) copy-start(bf16[1792,896]{1,0:T(8,128)(2,1)} %tile_ref.1) | copy-start | bytes 9633796
  19.5 6.1 %collective-permute-start.8 = (bf16[64,1792]{1,0:T(8,128)(2,1)S(1)}, bf16[64,1792]{1,0:T(8,128)(2,1)S(1)}, u32[]{:S(2)}, u32[]{:S(2)}) collective-permute-start(bf16[64,1792]{1,0:T(8,128)(2,1)S(1)} %get-tuple-element.38._), channel_id=1, source_target_pairs={{0,8},{1,9},{2,26},{3,27},{4,12},{5,13},{6,30},{7,31},{8,0},{9,1},... | collective-permute-start | bytes 688136 | tf_op jit(solution)/shard_map/ppermute | solution.py:289
  20.0 9.1 %collective-permute-start.12 = (bf16[64,1792]{1,0:T(8,128)(2,1)S(1)}, bf16[64,1792]{1,0:T(8,128)(2,1)S(1)}, u32[]{:S(2)}, u32[]{:S(2)}) collective-permute-start(bf16[64,1792]{1,0:T(8,128)(2,1)S(1)} %get-tuple-element.38._), channel_id=1, source_target_pairs={{0,16},{1,17},{10,26},{11,27}} | collective-permute-start | bytes 688136 | tf_op jit(solution)/shard_map/ppermute | solution.py:289
  23.5 5.7 %collective-permute-start.13 = (bf16[64,1792]{1,0:T(8,128)(2,1)S(1)}, bf16[64,1792]{1,0:T(8,128)(2,1)S(1)}, u32[]{:S(2)}, u32[]{:S(2)}) collective-permute-start(bf16[64,1792]{1,0:T(8,128)(2,1)S(1)} %get-tuple-element.38._), channel_id=1, source_target_pairs={{0,24},{1,25}} | collective-permute-start | bytes 688136 | tf_op jit(solution)/shard_map/ppermute | solution.py:289
  25.6 6.0 %collective-permute-start.9 = (bf16[64,1792]{1,0:T(8,128)(2,1)S(1)}, bf16[64,1792]{1,0:T(8,128)(2,1)S(1)}, u32[]{:S(2)}, u32[]{:S(2)}) collective-permute-start(bf16[64,1792]{1,0:T(8,128)(2,1)S(1)} %shard_map.43), channel_id=1, source_target_pairs={{0,16},{1,17},{2,18},{3,19},{4,2},{5,3},{6,22},{7,23},{8,10},{9,11... | collective-permute-start | bytes 688136 | tf_op jit(solution)/shard_map/ppermute | solution.py:289
  26.1 8.4 %collective-permute-start.11 = (bf16[64,1792]{1,0:T(8,128)(2,1)S(1)}, bf16[64,1792]{1,0:T(8,128)(2,1)S(1)}, u32[]{:S(2)}, u32[]{:S(2)}) collective-permute-start(bf16[64,1792]{1,0:T(8,128)(2,1)S(1)} %get-tuple-element.39.a_1_), channel_id=1, source_target_pairs={{16,18},{17,19},{24,26},{25,27},{26,28},{27,29}} | collective-permute-start | bytes 688136 | tf_op jit(solution)/shard_map/ppermute | solution.py:289
  29.2 5.4 %collective-permute-start.14 = (bf16[64,1792]{1,0:T(8,128)(2,1)S(1)}, bf16[64,1792]{1,0:T(8,128)(2,1)S(1)}, u32[]{:S(2)}, u32[]{:S(2)}) collective-permute-start(bf16[64,1792]{1,0:T(8,128)(2,1)S(1)} %shard_map.45), channel_id=1, source_target_pairs={{16,18},{17,19},{24,26},{25,27},{26,28},{27,29}} | collective-permute-start | bytes 688136 | tf_op jit(solution)/shard_map/ppermute | solution.py:289
  31.6 6.2 %collective-permute-start.10 = (bf16[64,1792]{1,0:T(8,128)(2,1)S(1)}, bf16[64,1792]{1,0:T(8,128)(2,1)S(1)}, u32[]{:S(2)}, u32[]{:S(2)}) collective-permute-start(bf16[64,1792]{1,0:T(8,128)(2,1)S(1)} %get-tuple-element.41), channel_id=1, source_target_pairs={{0,8},{1,9},{2,26},{3,27},{4,12},{5,13},{6,30},{7,31},{8,0},{9,1},... | collective-permute-start | bytes 688136 | tf_op jit(solution)/shard_map/ppermute | solution.py:289
  33.9 14.4 %collective-permute-start.22 = (bf16[64,1792]{1,0:T(8,128)(2,1)S(1)}, bf16[64,1792]{1,0:T(8,128)(2,1)S(1)}, u32[]{:S(2)}, u32[]{:S(2)}) collective-permute-start(bf16[64,1792]{1,0:T(8,128)(2,1)S(1)} %get-tuple-element.41), channel_id=1, source_target_pairs={{10,26},{11,27}} | collective-permute-start | bytes 688136 | tf_op jit(solution)/shard_map/ppermute | solution.py:289
  37.9 11.2 %collective-permute-start.15 = (bf16[64,1792]{1,0:T(8,128)(2,1)S(1)}, bf16[64,1792]{1,0:T(8,128)(2,1)S(1)}, u32[]{:S(2)}, u32[]{:S(2)}) collective-permute-start(bf16[64,1792]{1,0:T(8,128)(2,1)S(1)} %shard_map.46), channel_id=1, source_target_pairs={{0,16},{1,17},{2,18},{3,19},{4,2},{5,3},{6,22},{7,23},{8,10},{9,11... | collective-permute-start | bytes 688136 | tf_op jit(solution)/shard_map/ppermute | solution.py:289
  42.3 17.1 %collective-permute-start.21 = (bf16[64,1792]{1,0:T(8,128)(2,1)S(1)}, bf16[64,1792]{1,0:T(8,128)(2,1)S(1)}, u32[]{:S(2)}, u32[]{:S(2)}) collective-permute-start(bf16[64,1792]{1,0:T(8,128)(2,1)S(1)} %collective-permute-done.11.a_1_), channel_id=1, source_target_pairs={{26,28},{27,29}} | collective-permute-start | bytes 688136 | tf_op jit(solution)/shard_map/ppermute | solution.py:289
  43.5 14.6 %collective-permute-start.5 = (f32[1,224,128]{2,1,0:T(8,128)S(1)}, f32[1,224,128]{2,1,0:T(8,128)S(1)}, u32[]{:S(2)}, u32[]{:S(2)}) collective-permute-start(f32[1,224,128]{2,1,0:T(8,128)S(1)} %get-tuple-element.35), channel_id=1, source_target_pairs={{0,2},{1,3},{10,8},{11,9},{20,22},{21,23},{30,28},{31,29}} | collective-permute-start | bytes 344072 | tf_op jit(solution)/shard_map/ppermute | solution.py:289
  48.3 12.4 %collective-permute-start.23 = (bf16[64,1792]{1,0:T(8,128)(2,1)S(1)}, bf16[64,1792]{1,0:T(8,128)(2,1)S(1)}, u32[]{:S(2)}, u32[]{:S(2)}) collective-permute-start(bf16[64,1792]{1,0:T(8,128)(2,1)S(1)} %shard_map.51), channel_id=1, source_target_pairs={{26,28},{27,29}} | collective-permute-start | bytes 688136 | tf_op jit(solution)/shard_map/ppermute | solution.py:289
  49.1 13.0 %collective-permute-start.20 = (bf16[64,1792]{1,0:T(8,128)(2,1)S(1)}, bf16[64,1792]{1,0:T(8,128)(2,1)S(1)}, u32[]{:S(2)}, u32[]{:S(2)}) collective-permute-start(bf16[64,1792]{1,0:T(8,128)(2,1)S(1)} %get-tuple-element.47), channel_id=1, source_target_pairs={{0,8},{1,9},{2,26},{3,27},{4,12},{5,13},{6,30},{7,31},{8,0},{9,1},... | collective-permute-start | bytes 688136 | tf_op jit(solution)/shard_map/ppermute | solution.py:289
  50.9 26.7 %collective-permute-start.16 = (f32[2,224,128]{2,1,0:T(8,128)S(1)}, f32[2,224,128]{2,1,0:T(8,128)S(1)}, u32[]{:S(2)}, u32[]{:S(2)}) collective-permute-start(f32[2,224,128]{2,1,0:T(8,128)S(1)} %get-tuple-element.44), channel_id=1, source_target_pairs={{0,2},{1,3},{10,8},{11,9},{20,22},{21,23},{30,28},{31,29}} | collective-permute-start | bytes 688136 | tf_op jit(solution)/shard_map/ppermute | solution.py:289
  58.1 19.5 %collective-permute-start.17 = (f32[2,224,128]{2,1,0:T(8,128)S(1)}, f32[2,224,128]{2,1,0:T(8,128)S(1)}, u32[]{:S(2)}, u32[]{:S(2)}) collective-permute-start(f32[2,224,128]{2,1,0:T(8,128)S(1)} %get-tuple-element.45), channel_id=1, source_target_pairs={{0,4},{1,5},{10,14},{11,15},{20,16},{21,17},{30,26},{31,27}} | collective-permute-start | bytes 688136 | tf_op jit(solution)/shard_map/ppermute | solution.py:289
  59.4 18.2 %collective-permute-start.18 = (f32[2,224,128]{2,1,0:T(8,128)S(1)}, f32[2,224,128]{2,1,0:T(8,128)S(1)}, u32[]{:S(2)}, u32[]{:S(2)}) collective-permute-start(f32[2,224,128]{2,1,0:T(8,128)S(1)} %get-tuple-element.46), channel_id=1, source_target_pairs={{0,6},{1,7},{10,12},{11,13},{20,18},{21,19},{30,24},{31,25}} | collective-permute-start | bytes 688136 | tf_op jit(solution)/shard_map/ppermute | solution.py:289
  60.7 15.6 %collective-permute-start.6 = (f32[1,224,128]{2,1,0:T(8,128)S(1)}, f32[1,224,128]{2,1,0:T(8,128)S(1)}, u32[]{:S(2)}, u32[]{:S(2)}) collective-permute-start(f32[1,224,128]{2,1,0:T(8,128)S(1)} %get-tuple-element.36), channel_id=1, source_target_pairs={{0,4},{1,5},{10,14},{11,15},{20,16},{21,17},{30,26},{31,27}} | collective-permute-start | bytes 344072 | tf_op jit(solution)/shard_map/ppermute | solution.py:289
  62.1 15.5 %collective-permute-start.7 = (f32[1,224,128]{2,1,0:T(8,128)S(1)}, f32[1,224,128]{2,1,0:T(8,128)S(1)}, u32[]{:S(2)}, u32[]{:S(2)}) collective-permute-start(f32[1,224,128]{2,1,0:T(8,128)S(1)} %get-tuple-element.37), channel_id=1, source_target_pairs={{0,6},{1,7},{10,12},{11,13},{20,18},{21,19},{30,24},{31,25}} | collective-permute-start | bytes 344072 | tf_op jit(solution)/shard_map/ppermute | solution.py:289
  76.3 6.0 %collective-permute-start.24 = (bf16[64,1792]{1,0:T(8,128)(2,1)S(1)}, bf16[64,1792]{1,0:T(8,128)(2,1)S(1)}, u32[]{:S(2)}, u32[]{:S(2)}) collective-permute-start(bf16[64,1792]{1,0:T(8,128)(2,1)S(1)} %shard_map.52), channel_id=1, source_target_pairs={{0,16},{1,17},{2,18},{3,19},{4,2},{5,3},{6,22},{7,23},{8,10},{9,11... | collective-permute-start | bytes 688136 | tf_op jit(solution)/shard_map/ppermute | solution.py:289
  77.7 15.4 %copy-start.2 = (f32[224,512]{1,0:T(8,128)S(1)}, f32[224,512]{1,0:T(8,128)}, u32[]{:S(2)}) copy-start(f32[224,512]{1,0:T(8,128)} %a_1_.3) | copy-start | bytes 1376260
  77.7 15.4 %copy-start.4 = (s32[4]{0:T(128)S(1)}, s32[4]{0:T(128)}, u32[]{:S(2)}) copy-start(s32[4]{0:T(128)} %a_0_.5) | copy-start | bytes 52
  77.7 15.4 %collective-permute-start.19 = (f32[3,224,128]{2,1,0:T(8,128)S(1)}, f32[3,224,128]{2,1,0:T(8,128)S(1)}, u32[]{:S(2)}, u32[]{:S(2)}) collective-permute-start(f32[3,224,128]{2,1,0:T(8,128)S(1)} %shard_map.49.a_2_), channel_id=1, source_target_pairs={{0,1},{1,0},{2,3},{3,2},{4,5},{5,4},{6,7},{7,6},{8,9},{9,8},{10,11... | collective-permute-start | bytes 1032200 | tf_op jit(solution)/shard_map/ppermute | solution.py:289
  83.5 4.9 %collective-permute-start.25 = (bf16[224,128]{1,0:T(8,128)(2,1)S(1)}, bf16[224,128]{1,0:T(8,128)(2,1)S(1)}, u32[]{:S(2)}, u32[]{:S(2)}) collective-permute-start(bf16[224,128]{1,0:T(8,128)(2,1)S(1)} %get-tuple-element.50), channel_id=1, source_target_pairs={{0,2},{1,3},{2,0},{3,1},{4,6},{5,7},{6,4},{7,5},{8,10},{9,11},{10,... | collective-permute-start | bytes 172040 | tf_op jit(solution)/shard_map/ppermute | solution.py:289
  85.5 5.1 %collective-permute-start.26 = (bf16[224,128]{1,0:T(8,128)(2,1)S(1)}, bf16[224,128]{1,0:T(8,128)(2,1)S(1)}, u32[]{:S(2)}, u32[]{:S(2)}) collective-permute-start(bf16[224,128]{1,0:T(8,128)(2,1)S(1)} %get-tuple-element.51), channel_id=1, source_target_pairs={{0,4},{1,5},{2,6},{3,7},{4,0},{5,1},{6,2},{7,3},{8,12},{9,13},{10,... | collective-permute-start | bytes 172040 | tf_op jit(solution)/shard_map/ppermute | solution.py:289
  87.0 6.1 %collective-permute-start.27 = (bf16[224,128]{1,0:T(8,128)(2,1)S(1)}, bf16[224,128]{1,0:T(8,128)(2,1)S(1)}, u32[]{:S(2)}, u32[]{:S(2)}) collective-permute-start(bf16[224,128]{1,0:T(8,128)(2,1)S(1)} %get-tuple-element.52), channel_id=1, source_target_pairs={{0,6},{1,7},{2,4},{3,5},{4,2},{5,3},{6,0},{7,1},{8,14},{9,15},{10,... | collective-permute-start | bytes 172040 | tf_op jit(solution)/shard_map/ppermute | solution.py:289
  93.1 1.2 %collective-permute-start.28 = (bf16[1,224,128]{2,1,0:T(8,128)(2,1)S(1)}, bf16[1,224,128]{2,1,0:T(8,128)(2,1)S(1)}, u32[]{:S(2)}, u32[]{:S(2)}) collective-permute-start(bf16[1,224,128]{2,1,0:T(8,128)(2,1)S(1)} %shard_map.55.a_2_), channel_id=1, source_target_pairs={{0,1},{1,0},{2,3},{3,2},{4,5},{5,4},{6,7},{7,6},{8,9},{9,8},{10,11... | collective-permute-start | bytes 172040 | tf_op jit(solution)/shard_map/ppermute | solution.py:289
  (2 other events, 1.7 us)

commit v3 on v2

--- a/solution.py
+++ b/solution.py
@@ -7,19 +7,21 @@
 
 
 TICKS = 6
+CHUNKS = 2
 F32 = jnp.float32
 BF16 = jnp.bfloat16
 VM = pl.BlockSpec(memory_space=pltpu.VMEM)
 SM = pl.BlockSpec(memory_space=pltpu.SMEM)
 
 
-def call(kernel, outs, args, specs, scratch=(), flops=0):
+def call(kernel, outs, args, specs, scratch=(), flops=0, out_spec=VM, aliases=()):
     n_bytes = sum(o.size * o.dtype.itemsize for o in outs)
     return pl.pallas_call(
         kernel,
         out_shape=outs,
         in_specs=specs,
-        out_specs=[VM] * len(outs),
+        out_specs=[out_spec] * len(outs),
+        input_output_aliases=dict(aliases),
         scratch_shapes=list(scratch),
         compiler_params=pltpu.CompilerParams(vmem_limit_bytes=24 << 20),
         cost_estimate=pl.CostEstimate(flops=flops, bytes_accessed=n_bytes, transcendentals=0),
@@ -73,12 +75,11 @@
 
 def solve(rhs, own_ref, other_ref, x_ref, xb_ref):
     half = own_ref.shape[1]
-    left = jnp.dot(rhs, own_ref[...], preferred_element_type=F32)
-    right = jnp.dot(rhs, other_ref[...], preferred_element_type=F32)
-    xb_ref[:, :half] = left.astype(BF16)
-    xb_ref[:, half:] = right.astype(BF16)
-    x_ref[:, :half] = left
-    x_ref[:, half:] = right
+    for side, tile_ref in ((slice(0, half), own_ref), (slice(half, 2 * half), other_ref)):
+        value = jnp.dot(rhs, tile_ref[...], preferred_element_type=F32)
+        x_ref[:, side] = value
+        if xb_ref is not None:
+            xb_ref[:, side] = value.astype(BF16)
 
 
 def load_kernel(tile_ref, _, out_ref, sem):
@@ -102,15 +103,22 @@
 
     @pl.when(r == z)
     def _():
-        solve(grad_ref[...], own_ref, other_ref, x_ref, xb_ref)
-
-
-def solve_kernel(tick, rhs_ref, own_ref, other_ref, x_ref, xb_ref):
-    r, z, _ = place()
+        solve(grad_ref[: x_ref.shape[0]], own_ref, other_ref, x_ref, xb_ref)
+
+
+def solve_kernel(tick, top, n_before, rhs_ref, own_ref, other_ref, *refs):
+    r, z, _ = place()
+    before, outs = refs[:n_before], refs[n_before:]
+    x_ref, xb_ref = outs[0], outs[1] if len(outs) > 1 else None
+    rows = x_ref.shape[0]
 
     @pl.when((r == z) & (z >= tick))
     def _():
-        solve(rhs_ref[...], own_ref, other_ref, x_ref, xb_ref)
+        solve(rhs_ref[top : top + rows], own_ref, other_ref, x_ref, xb_ref)
+        if len(outs) > 2:
+            for c, ref in enumerate(before):
+                outs[2][c * rows : (c + 1) * rows] = ref[...]
+            outs[2][n_before * rows :] = xb_ref[...]
 
 
 def turn_kernel(own_ref, other_ref, _, out_ref):
@@ -123,15 +131,17 @@
         out_ref[half:] = jnp.transpose(other_ref[...])
 
 
-def near_kernel(tick, x_ref, grad_ref, turned_ref, *refs):
+def near_kernel(tick, c, x_ref, grad_ref, turned_ref, *refs):
     out_ref = refs[-1]
+    rows = out_ref.shape[0]
+    mine = slice(c * rows, (c + 1) * rows)
     r, z, _ = place()
 
     @pl.when((r == z + 1) & (z >= tick))
     def _():
-        value = grad_ref[...].astype(F32)
+        value = grad_ref[mine].astype(F32)
         if tick:
-            value = value - refs[0][...].astype(F32)
+            value = value - refs[0][mine].astype(F32)
         value = value - jnp.dot(x_ref[...], turned_ref[...], preferred_element_type=F32)
         out_ref[...] = value.astype(out_ref.dtype)
 
@@ -154,18 +164,14 @@
             out_ref[...] = value.astype(out_ref.dtype)
 
 
-def fold(x_ref, natural):
+def fold(x_refs, natural):
     _, _, h = place()
-    half, width = x_ref.shape[1] // 2, natural.shape[1]
-
-    @pl.when(h == 0)
-    def _():
-        natural[: 2 * half, : width // 2] = jnp.transpose(x_ref[...])
-
-    @pl.when(h == 1)
-    def _():
-        natural[half : 2 * half, : width // 2] = jnp.transpose(x_ref[:, :half])
-        natural[:half, : width // 2] = jnp.transpose(x_ref[:, half:])
+    half, width = x_refs[0].shape[1] // 2, natural.shape[1]
+    own = jnp.concatenate([ref[:, :half] for ref in x_refs], axis=0)
+    other = jnp.concatenate([ref[:, half:] for ref in x_refs], axis=0)
+    top = pl.multiple_of(h * half, 8)
+    natural[pl.ds(top, half), : width // 2] = jnp.transpose(own)
+    natural[pl.ds(pl.multiple_of(half - top, 8), half), : width // 2] = jnp.transpose(other)
 
 
 def folded(natural, rows, target):
@@ -177,41 +183,48 @@
     return jnp.where(lanes < width // 2, upper, pltpu.roll(lower, width // 2, 1))
 
 
-def early_kernel(count, n_parts, *refs):
-    x_refs, out_refs, natural = refs[:n_parts], refs[n_parts:-1], refs[-1]
+def early_kernel(count, n_chunks, *refs):
+    x_refs, out_refs, natural = refs[: -count - 1], refs[-count - 1 : -1], refs[-1]
     r, z, _ = place()
     rows = out_refs[0].shape[1]
 
     @pl.when(r == z)
     def _():
-        for t in range(n_parts):
-            fold(x_refs[t], natural)
+        for t in range(len(x_refs) // n_chunks):
+            fold(x_refs[t * n_chunks : (t + 1) * n_chunks], natural)
             for k in range(count):
-                out_refs[k][t] = folded(natural, rows, z ^ k)
-
-
-def last_kernel(count, x_ref, *refs):
-    out_refs, natural = refs[:-1], refs[-1]
-    _, z, _ = place()
+                out_refs[k][t] = folded(natural, rows, z ^ k).astype(out_refs[k].dtype)
+
+
+def last_kernel(count, ticks, n_before, solves, *refs):
+    before, refs = refs[:n_before], refs[n_before:]
+    r, z, _ = place()
+    if solves:
+        rhs_ref, own_ref, other_ref = refs[:3]
+        out_refs, natural, x_ref = refs[3:-2], refs[-2], refs[-1]
+    else:
+        out_refs, natural = refs[:-1], refs[-1]
     rows = out_refs[0].shape[0]
-    fold(x_ref, natural)
-    for k in range(count):
-        out_refs[k][...] = folded(natural, rows, z ^ k).astype(out_refs[k].dtype)
+
+    @pl.when((z >= ticks - 1) & (z <= r))
+    def _():
+        x_refs = list(before)
+        if solves:
+            solve(rhs_ref[...], own_ref, other_ref, x_ref, None)
+            x_refs.append(x_ref)
+        fold(x_refs, natural)
+        for k in range(count):
+            out_refs[k][...] = folded(natural, rows, z ^ k).astype(out_refs[k].dtype)
 
 
 def pick_early_kernel(count, *refs):
     out_ref = refs[-1]
     r, z, _ = place()
-    first = 0
-    for group in range(0, len(refs) - 1, count):
-        parts = refs[group].shape[0]
-        for k in range(count):
-
-            @pl.when((z ^ r) == k)
-            def _():
-                out_ref[first : first + parts] = refs[group + k][...]
-
-        first += parts
+    for k in range(count):
+
+        @pl.when((z ^ r) == k)
+        def _():
+            out_ref[...] = refs[k][...]
 
 
 def pick_last_kernel(count, ticks, *refs):
@@ -251,24 +264,18 @@
             out_ref[:, pl.ds(begin, width)] = join(mine_ref[t], other_ref[t], h)
 
 
-def put_last_kernel(count, ticks, starts_ref, early_ref, mine_ref, other_ref, out_ref):
+def put_last_kernel(count, ticks, starts_ref, _, mine_ref, other_ref, out_ref, joined, sem):
     r, _, h = place()
     width = mine_ref.shape[2]
-    out_ref[...] = early_ref[...]
     for s in range(count - ticks + 1):
         begin = pl.multiple_of(panel_at(starts_ref, count, s) * width, width)
 
         @pl.when(r - s >= ticks - 1)
         def _():
-            out_ref[:, pl.ds(begin, width)] = join(mine_ref[s], other_ref[s], h)
-
-
-def early_groups(ticks):
-    if ticks < 3:
-        return {ticks - 2: list(range(ticks - 1))}
-    groups = {t: [t - 1] for t in range(1, ticks - 1)}
-    groups[ticks - 2].append(ticks - 2)
-    return groups
+            joined[...] = join(mine_ref[s], other_ref[s], h)
+            copy = pltpu.make_async_copy(joined, out_ref.at[:, pl.ds(begin, width)], sem)
+            copy.start()
+            copy.wait()
 
 
 def body(factor, gradient, starts):
@@ -303,9 +310,9 @@
 
         return move(array, target)
 
-    def to_next_row(array):
+    def to_next_row(array, tick):
         def target(r, z, h):
-            return (z % 2 + ((r - z % 2) % count ^ 1)) % count, z, h
+            return (r + 1, z, h) if r == z and z >= tick and r + 1 < count else None
 
         return move(array, target)
 
@@ -318,6 +325,12 @@
             if (z == base) == (not lead):
                 return r, base + 1 if z == base else base, h
             return r ^ 2, z, h
+
+        return move(array, target)
+
+    def from_last(array, k):
+        def target(r, z, h):
+            return (r, z ^ k, h) if ticks - 1 <= z <= r else None
 
         return move(array, target)
 
@@ -343,40 +356,62 @@
         load_kernel, [shape(factor.shape, BF16)], (factor, pieces[0]),
         [pl.BlockSpec(memory_space=pl.ANY), VM], [pltpu.SemaphoreType.DMA],
     )[0]
-    wide = [shape((cols, tile), F32), shape((cols, tile), BF16)]
+    part = cols // CHUNKS
+    pair = [shape((part, tile), F32), shape((part, tile), BF16)]
+    scratch = [pltpu.VMEM((tile, width), F32)]
     x, xb, grad = call(
         lambda *a: first_kernel(count, *a),
-        wide + [shape((cols, tile), BF16)], (*arrived, own_tile, other_tile), [VM] * (count + 2),
-        [pltpu.VMEM((tile, width), F32)], flops,
+        pair + [shape((cols, tile), BF16)], (*arrived, own_tile, other_tile), [VM] * (count + 2),
+        scratch, flops,
     )
-    turned = call(turn_kernel, [shape((tile, tile), BF16)], (own_tile, other_tile, xb), [VM] * 3)[0]
-    groups = early_groups(ticks) if ticks > 1 else {}
+    turned = call(
+        turn_kernel, [shape((tile, tile), BF16)], (own_tile, other_tile, grad), [VM] * 3,
+    )[0]
     xs, before, sent_early = [], None, []
     for tick in range(ticks):
         final = tick == ticks - 1
-        if tick:
-            x, xb = call(
-                lambda *a: solve_kernel(tick, *a),
-                wide, (rhs, own_tile, other_tile), [VM] * 3, (), flops,
-            )
-        result = x
-        xs.append(x)
-        if count - 1 > tick:
+        rest = count - 1 > tick
+        solved, solved_b, downs = [], [], []
+        for c in range(CHUNKS):
+            if tick or c:
+                if final and not rest and c == CHUNKS - 1:
+                    break
+                source, top = (rhs[c], 0) if tick else (grad, c * part)
+                joins = c == CHUNKS - 1 and CHUNKS > 1
+                outs = pair + ([shape((cols, tile), BF16)] if joins else [])
+                outs = outs if rest else outs[:1]
+                given = solved_b if joins else []
+                done = call(
+                    lambda *a: solve_kernel(tick, top, len(given), *a),
+                    outs, (source, own_tile, other_tile, *given), [VM] * (3 + len(given)), (), flops,
+                )
+                x, xb, whole = done[0], done[1 % len(done)], done[-1]
+            else:
+                whole = xb
+            solved.append(x)
+            solved_b.append(xb)
+            if rest:
+                downs.append(to_next_row(xb, tick))
+        xs.append(solved)
+        results = solved
+        if rest:
             dtype = F32 if final else BF16
-            near = to_next_row(xb)
-            far = [to_far_row(xb, tick, d) for d in range(2, count - tick)]
+            far = [to_far_row(whole, tick, d) for d in range(2, count - tick)]
             carried = [before] if tick else []
-            out = call(
-                lambda *a: near_kernel(tick, *a),
-                [shape((cols, tile), dtype)], (near, grad, turned, *carried),
-                [VM] * (3 + len(carried)), (), flops,
-            )[0]
+            outs, rhs = [], []
+            for c in range(CHUNKS):
+                out = call(
+                    lambda *a: near_kernel(tick, c, *a),
+                    [shape((part, tile), dtype)], (downs[c], grad, turned, *carried),
+                    [VM] * (3 + len(carried)), (), flops,
+                )[0]
+                outs.append(out)
+                if not final:
+                    rhs.append(to_next_col(out))
             if final:
                 r, z, _ = place()
-                result = jnp.where(r == z, x, out)
+                results = [jnp.where(r == z, a, b) for a, b in zip(solved, outs)]
                 carried = carried + [grad]
-            else:
-                rhs = to_next_col(out)
             if far:
                 if not final:
                     grad = far_to_next_col(grad, tick)
@@ -386,27 +421,33 @@
                     [VM] * (1 + len(carried) + len(far)), (), flops,
                 )[0]
                 if final:
-                    result = jnp.where(r >= z + 2, out, result)
+                    results = [
+                        jnp.where(r >= z + 2, out[c * part : (c + 1) * part], results[c])
+                        for c in range(CHUNKS)
+                    ]
                 else:
                     before = far_to_next_col(out, tick)
-        if tick in groups:
-            members = groups[tick]
+        if tick == ticks - 2:
+            given = [x for solved in xs for x in solved]
             parts = call(
-                lambda *a: early_kernel(count, len(members), *a),
-                [shape((len(members), rows, width), F32)] * count, tuple(xs[t] for t in members),
-                [VM] * len(members), [pltpu.VMEM((tile, width), F32)],
+                lambda *a: early_kernel(count, CHUNKS, *a),
+                [shape((ticks - 1, rows, width), BF16)] * count, given,
+                [VM] * len(given), scratch,
             )
-            sent_early += [parts[0]]
+            sent_early = [parts[0]]
             sent_early += [from_diagonal(parts[k], k) for k in range(1, count)]
+    given, more = list(results), []
+    if not rest:
+        given += [rhs[-1], own_tile, other_tile]
+        more = [pltpu.VMEM((part, tile), F32)]
     parts = call(
-        lambda *a: last_kernel(count, *a),
-        [shape((rows, width), BF16)] * count, (result,), [VM],
-        [pltpu.VMEM((tile, width), F32)],
+        lambda *a: last_kernel(count, ticks, len(results), not rest, *a),
+        [shape((rows, width), BF16)] * count, given, [VM] * len(given), scratch + more, flops,
     )
-    sent = [parts[0]] + [along(parts[k], k) for k in range(1, count)]
+    sent = [parts[0]] + [from_last(parts[k], k) for k in range(1, count)]
     mine = call(
         lambda *a: pick_early_kernel(count, *a),
-        [shape((ticks - 1, rows, width), F32)], sent_early, [VM] * len(sent_early),
+        [shape((ticks - 1, rows, width), BF16)], sent_early, [VM] * len(sent_early),
     )[0]
     theirs = cores(mine)
     early = call(
@@ -418,9 +459,11 @@
         [shape((count - ticks + 1, rows, width), BF16)], sent, [VM] * count,
     )[0]
     theirs = cores(mine)
+    hbm = pl.BlockSpec(memory_space=pltpu.HBM)
     return call(
         lambda *a: put_last_kernel(count, ticks, *a),
-        [shape(gradient.shape, F32)], (starts, early, mine, theirs), [SM, VM, VM, VM],
+        [shape(gradient.shape, F32)], (starts, early, mine, theirs), [SM, hbm, VM, VM],
+        [pltpu.VMEM((rows, width), F32), pltpu.SemaphoreType.DMA], 0, hbm, {1: 0},
     )[0]
 
 

time: 96.1 us -> 80.9 us (0.84)
  the two profiles are of different devices: /device:TPU:0 before, /device:TPU:7 now
where the time goes in v3:
time: 80.9 us; the launch traced here: 80.5 us
  starting transfers between devices  43.4 us (54%)
  waiting for transfers between devices  24.5 us (30%)
  Pallas kernels  8.37 us (10%)
  local copies, waits for them, and re-layouts  3.59 us (4%)
    ppermute x32, starting transfers between devices, move(): return lax.ppermute(array, ('row', 'col'), pairs)  43.4 us
    ppermute x32, waiting for transfers between devices, move(): return lax.ppermute(array, ('row', 'col'), pairs)  24.5 us
    pallas_call x25, Pallas kernels, call(): pl.pallas_call(kernel, out_shape=outs, in_specs=specs, out_specs=[out_spe...  8.37 us
    unnamed x10, local copies, waits for them, and re-layouts  3.59 us
  transfers between devices with their start and end apart: 32, of which 7 were waited for; matrix products, arithmetic and copies ran while one was open for 0% of the time, Pallas kernels for 8%

profile of v3, /device:TPU:7, one launch (start us, length us, event | category | flops | bytes accessed | tf_op | source)
XLA Modules:
  0.0 80.5 jit_solution(15020078668679720768)
XLA Ops:
  0.0 0.7 collective-permute-start.4
  0.7 1.0 %copy-done.1 = f32[224,512]{1,0:T(8,128)S(1)} copy-done((f32[224,512]{1,0:T(8,128)S(1)}, f32[224,512]{1,0:T(8,128)}, u32[]{:S(2)}) %copy-start.1) | copy-done | bytes 458776
  3.0 3.5 %collective-permute-done.a_1_ = bf16[4,224,128]{2,1,0:T(8,128)(2,1)S(1)} collective-permute-done((bf16[4,224,128]{2,1,0:T(8,128)(2,1)S(1)}, bf16[4,224,128]{2,1,0:T(8,128)(2,1)S(1)}, u32[]{:S(2)}, u32[]{:S(2)}) %collective-permute-start) | collective-permute-done | bytes 229408 | tf_op jit(solution)/shard_map/ppermute | solution.py:296
  6.8 1.4 %collective-permute-start.1 = (bf16[224,128]{1,0:T(8,128)(2,1)S(1)}, bf16[224,128]{1,0:T(8,128)(2,1)S(1)}, u32[]{:S(2)}, u32[]{:S(2)}) collective-permute-start(bf16[224,128]{1,0:T(8,128)(2,1)S(1)} %get-tuple-element.33), channel_id=1, source_target_pairs={{0,2},{1,3},{2,0},{3,1},{4,6},{5,7},{6,4},{7,5},{8,10},{9,11},{10,... | collective-permute-start | bytes 172040 | tf_op jit(solution)/shard_map/ppermute | solution.py:296
  8.1 2.3 %collective-permute-start.2 = (bf16[224,128]{1,0:T(8,128)(2,1)S(1)}, bf16[224,128]{1,0:T(8,128)(2,1)S(1)}, u32[]{:S(2)}, u32[]{:S(2)}) collective-permute-start(bf16[224,128]{1,0:T(8,128)(2,1)S(1)} %get-tuple-element.34), channel_id=1, source_target_pairs={{0,4},{1,5},{2,6},{3,7},{4,0},{5,1},{6,2},{7,3},{8,12},{9,13},{10,... | collective-permute-start | bytes 172040 | tf_op jit(solution)/shard_map/ppermute | solution.py:296
  10.4 1.9 %copy-done = bf16[1792,896]{1,0:T(8,128)(2,1)S(1)} copy-done((bf16[1792,896]{1,0:T(8,128)(2,1)S(1)}, bf16[1792,896]{1,0:T(8,128)(2,1)}, u32[]{:S(2)}) %copy-start) | copy-done | bytes 3211288
  12.7 2.7 %collective-permute-done.3.a_3_ = bf16[224,128]{1,0:T(8,128)(2,1)S(1)} collective-permute-done((bf16[224,128]{1,0:T(8,128)(2,1)S(1)}, bf16[224,128]{1,0:T(8,128)(2,1)S(1)}, u32[]{:S(2)}, u32[]{:S(2)}) %collective-permute-start.3) | collective-permute-done | bytes 57376 | tf_op jit(solution)/shard_map/ppermute | solution.py:296
  16.4 0.7 collective-permute-start.11
  17.1 1.3 %collective-permute-start.12 = (bf16[64,1792]{1,0:T(8,128)(2,1)S(1)}, bf16[64,1792]{1,0:T(8,128)(2,1)S(1)}, u32[]{:S(2)}, u32[]{:S(2)}) collective-permute-start(bf16[64,1792]{1,0:T(8,128)(2,1)S(1)} %get-tuple-element.44), channel_id=1, source_target_pairs={{0,24},{1,25}} | collective-permute-start | bytes 688136 | tf_op jit(solution)/shard_map/ppermute | solution.py:296
  19.1 1.7 %shard_map.42.a_2_.a_0_ = bf16[1792,1792]{1,0:T(8,128)(2,1)S(1)} custom-call(bf16[1792,896]{1,0:T(8,128)(2,1)S(1)} %shard_map.39.a_4_.a_1_.own_ref.a_2_, bf16[1792,896]{1,0:T(8,128)(2,1)S(1)} %collective-permute-done.4.a_5_.a_2_.other_ref.a_3_, bf16[64,1792]{1,0:T(8,128)(2,1)S(1)} %get-tuple-element.37.a_0_._.a_1_), custom_call_target="tpu_custom_call" | custom-call | bytes 6422528 | tf_op jit(solution)/shard_map/pallas_call | solution.py:19
  20.8 2.1 %collective-permute-start.6 = (bf16[32,1792]{1,0:T(8,128)(2,1)S(1)}, bf16[32,1792]{1,0:T(8,128)(2,1)S(1)}, u32[]{:S(2)}, u32[]{:S(2)}) collective-permute-start(bf16[32,1792]{1,0:T(8,128)(2,1)S(1)} %shard_map.43), channel_id=1, source_target_pairs={{0,16},{1,17},{2,18},{3,19},{4,2},{5,3},{6,22},{7,23},{8,10},{9,11... | collective-permute-start | bytes 344072 | tf_op jit(solution)/shard_map/ppermute | solution.py:296
  22.9 7.5 %collective-permute-start.8 = (bf16[32,1792]{1,0:T(8,128)(2,1)S(1)}, bf16[32,1792]{1,0:T(8,128)(2,1)S(1)}, u32[]{:S(2)}, u32[]{:S(2)}) collective-permute-start(bf16[32,1792]{1,0:T(8,128)(2,1)S(1)} %shard_map.45), channel_id=1, source_target_pairs={{0,16},{1,17},{2,18},{3,19},{4,2},{5,3},{6,22},{7,23},{8,10},{9,11... | collective-permute-start | bytes 344072 | tf_op jit(solution)/shard_map/ppermute | solution.py:296
  30.4 1.3 %collective-permute-start.10 = (bf16[64,1792]{1,0:T(8,128)(2,1)S(1)}, bf16[64,1792]{1,0:T(8,128)(2,1)S(1)}, u32[]{:S(2)}, u32[]{:S(2)}) collective-permute-start(bf16[64,1792]{1,0:T(8,128)(2,1)S(1)} %get-tuple-element.37.a_0_._.a_1_), channel_id=1, source_target_pairs={{16,18},{17,19},{24,26},{25,27},{26,28},{27,29}} | collective-permute-start | bytes 688136 | tf_op jit(solution)/shard_map/ppermute | solution.py:296
  31.7 1.3 %shard_map.47 = bf16[64,1792]{1,0:T(8,128)(2,1)S(1)} custom-call(bf16[1792,1792]{1,0:T(8,128)(2,1)S(1)} %shard_map.42.a_2_.a_0_, bf16[64,1792]{1,0:T(8,128)(2,1)S(1)} %collective-permute-done.11.a_1_, bf16[64,1792]{1,0:T(8,128)(2,1)S(1)} %collective-permute-done.12.a_2_), custom_call_target="tpu_custom_call" | custom-call | flops 411041792 | bytes 229376 | tf_op jit(solution)/shard_map/pallas_call | solution.py:19
  33.0 1.3 %collective-permute-start.13 = (bf16[64,1792]{1,0:T(8,128)(2,1)S(1)}, bf16[64,1792]{1,0:T(8,128)(2,1)S(1)}, u32[]{:S(2)}, u32[]{:S(2)}) collective-permute-start(bf16[64,1792]{1,0:T(8,128)(2,1)S(1)} %shard_map.47), channel_id=1, source_target_pairs={{16,18},{17,19},{24,26},{25,27},{26,28},{27,29}} | collective-permute-start | bytes 688136 | tf_op jit(solution)/shard_map/ppermute | solution.py:296
  34.3 0.7 collective-permute-start.23
  36.4 0.7 collective-permute-start.22
  37.1 1.9 %collective-permute-done.13.a_3_.a_1_ = bf16[64,1792]{1,0:T(8,128)(2,1)S(1)} collective-permute-done((bf16[64,1792]{1,0:T(8,128)(2,1)S(1)}, bf16[64,1792]{1,0:T(8,128)(2,1)S(1)}, u32[]{:S(2)}, u32[]{:S(2)}) %collective-permute-start.13) | collective-permute-done | bytes 229408 | tf_op jit(solution)/shard_map/ppermute | solution.py:296
  39.9 0.8 %collective-permute-start.16 = (bf16[32,1792]{1,0:T(8,128)(2,1)S(1)}, bf16[32,1792]{1,0:T(8,128)(2,1)S(1)}, u32[]{:S(2)}, u32[]{:S(2)}) collective-permute-start(bf16[32,1792]{1,0:T(8,128)(2,1)S(1)} %shard_map.50), channel_id=1, source_target_pairs={{0,16},{1,17},{2,18},{3,19},{4,2},{5,3},{6,22},{7,23},{8,10},{9,11... | collective-permute-start | bytes 344072 | tf_op jit(solution)/shard_map/ppermute | solution.py:296
  40.7 2.7 %collective-permute-done.14.a_0_ = bf16[32,1792]{1,0:T(8,128)(2,1)S(1)} collective-permute-done((bf16[32,1792]{1,0:T(8,128)(2,1)S(1)}, bf16[32,1792]{1,0:T(8,128)(2,1)S(1)}, u32[]{:S(2)}, u32[]{:S(2)}) %collective-permute-start.14) | collective-permute-done | bytes 114720 | tf_op jit(solution)/shard_map/ppermute | solution.py:296
  44.0 2.8 %collective-permute-done.16.a_0_ = bf16[32,1792]{1,0:T(8,128)(2,1)S(1)} collective-permute-done((bf16[32,1792]{1,0:T(8,128)(2,1)S(1)}, bf16[32,1792]{1,0:T(8,128)(2,1)S(1)}, u32[]{:S(2)}, u32[]{:S(2)}) %collective-permute-start.16) | collective-permute-done | bytes 114720 | tf_op jit(solution)/shard_map/ppermute | solution.py:296
  46.9 0.7 shard_map.51
  49.6 1.3 %collective-permute-start.19 = (bf16[3,224,128]{2,1,0:T(8,128)(2,1)S(1)}, bf16[3,224,128]{2,1,0:T(8,128)(2,1)S(1)}, u32[]{:S(2)}, u32[]{:S(2)}) collective-permute-start(bf16[3,224,128]{2,1,0:T(8,128)(2,1)S(1)} %get-tuple-element.52), channel_id=1, source_target_pairs={{0,6},{1,7},{10,12},{11,13},{20,18},{21,19},{30,24},{31,25}} | collective-permute-start | bytes 516104 | tf_op jit(solution)/shard_map/ppermute | solution.py:296
  51.1 3.6 %collective-permute-start.27 = (bf16[32,1792]{1,0:T(8,128)(2,1)S(1)}, bf16[32,1792]{1,0:T(8,128)(2,1)S(1)}, u32[]{:S(2)}, u32[]{:S(2)}) collective-permute-start(bf16[32,1792]{1,0:T(8,128)(2,1)S(1)} %shard_map.58), channel_id=1, source_target_pairs={{0,16},{1,17},{2,18},{3,19},{4,2},{5,3},{6,22},{7,23},{8,10},{9,11... | collective-permute-start | bytes 344072 | tf_op jit(solution)/shard_map/ppermute | solution.py:296
  54.7 4.9 %collective-permute-done.19.a_3_ = bf16[3,224,128]{2,1,0:T(8,128)(2,1)S(1)} collective-permute-done((bf16[3,224,128]{2,1,0:T(8,128)(2,1)S(1)}, bf16[3,224,128]{2,1,0:T(8,128)(2,1)S(1)}, u32[]{:S(2)}, u32[]{:S(2)}) %collective-permute-start.19) | collective-permute-done | bytes 172064 | tf_op jit(solution)/shard_map/ppermute | solution.py:296
  59.5 7.5 %collective-permute-start.20 = (bf16[3,224,128]{2,1,0:T(8,128)(2,1)S(1)}, bf16[3,224,128]{2,1,0:T(8,128)(2,1)S(1)}, u32[]{:S(2)}, u32[]{:S(2)}) collective-permute-start(bf16[3,224,128]{2,1,0:T(8,128)(2,1)S(1)} %shard_map.53.a_2_), channel_id=1, source_target_pairs={{0,1},{1,0},{2,3},{3,2},{4,5},{5,4},{6,7},{7,6},{8,9},{9,8},{10,11... | collective-permute-start | bytes 516104 | tf_op jit(solution)/shard_map/ppermute | solution.py:296
  67.1 0.8 collective-permute-start.28
  68.6 1.3 %collective-permute-start.30 = (bf16[224,128]{1,0:T(8,128)(2,1)S(1)}, bf16[224,128]{1,0:T(8,128)(2,1)S(1)}, u32[]{:S(2)}, u32[]{:S(2)}) collective-permute-start(bf16[224,128]{1,0:T(8,128)(2,1)S(1)} %get-tuple-element.58), channel_id=1, source_target_pairs={{30,24},{31,25}} | collective-permute-start | bytes 172040 | tf_op jit(solution)/shard_map/ppermute | solution.py:296
  69.9 5.9 %collective-permute-done.30.a_3_ = bf16[224,128]{1,0:T(8,128)(2,1)S(1)} collective-permute-done((bf16[224,128]{1,0:T(8,128)(2,1)S(1)}, bf16[224,128]{1,0:T(8,128)(2,1)S(1)}, u32[]{:S(2)}, u32[]{:S(2)}) %collective-permute-start.30) | collective-permute-done | bytes 57376 | tf_op jit(solution)/shard_map/ppermute | solution.py:296
  75.8 1.6 %collective-permute-start.31 = (bf16[1,224,128]{2,1,0:T(8,128)(2,1)S(1)}, bf16[1,224,128]{2,1,0:T(8,128)(2,1)S(1)}, u32[]{:S(2)}, u32[]{:S(2)}) collective-permute-start(bf16[1,224,128]{2,1,0:T(8,128)(2,1)S(1)} %shard_map.60.a_2_), channel_id=1, source_target_pairs={{0,1},{1,0},{2,3},{3,2},{4,5},{5,4},{6,7},{7,6},{8,9},{9,8},{10,11... | collective-permute-start | bytes 172040 | tf_op jit(solution)/shard_map/ppermute | solution.py:296
  77.4 1.6 %shard_map.54.a_1_ = f32[224,512]{1,0:T(8,128)} custom-call(s32[4]{0:T(128)S(1)} %copy-done.4, f32[224,512]{1,0:T(8,128)S(1)} %copy-done.2, bf16[3,224,128]{2,1,0:T(8,128)(2,1)S(1)} %shard_map.53.a_2_, bf16[3,224,128]{2,1,0:T(8,128)(2,1)S(1)} %collective-permute-done.20.a_3_), custom_call_target="tpu_custom_call" | custom-call | bytes 458752 | tf_op jit(solution)/shard_map/pallas_call | solution.py:19
  79.0 1.3 %shard_map.61 = f32[224,512]{1,0:T(8,128)} custom-call(s32[4]{0:T(128)S(1)} %copy-done.4, f32[224,512]{1,0:T(8,128)} %shard_map.54.a_1_, bf16[1,224,128]{2,1,0:T(8,128)(2,1)S(1)} %shard_map.60.a_2_, bf16[1,224,128]{2,1,0:T(8,128)(2,1)S(1)} %collective-permute-done.31.a_3_), custom_call_target="tpu_custom_call", output_to_operand_aliasing={{}: (1, {})} | custom-call | bytes 458752 | tf_op jit(solution)/shard_map/pallas_call | solution.py:19
  (67 shorter events, 9.3 us)
Async XLA Ops:
  0.0 15.4 %collective-permute-start.4 = (bf16[1792,896]{1,0:T(8,128)(2,1)}, bf16[1792,896]{1,0:T(8,128)(2,1)S(1)}, u32[]{:S(2)}, u32[]{:S(2)}) collective-permute-start(bf16[1792,896]{1,0:T(8,128)(2,1)} %tile_ref.1), channel_id=1, source_target_pairs={{0,1},{1,0},{2,3},{3,2},{4,5},{5,4},{6,7},{7,6},{8,9},{9,8},{10,11... | collective-permute-start | bytes 9633800 | tf_op jit(solution)/shard_map/ppermute | solution.py:296
  3.0 3.6 %collective-permute-start = (bf16[4,224,128]{2,1,0:T(8,128)(2,1)S(1)}, bf16[4,224,128]{2,1,0:T(8,128)(2,1)S(1)}, u32[]{:S(2)}, u32[]{:S(2)}) collective-permute-start(bf16[4,224,128]{2,1,0:T(8,128)(2,1)S(1)} %shard_map.37.a_0_), channel_id=1, source_target_pairs={{0,1},{1,0},{2,3},{3,2},{4,5},{5,4},{6,7},{7,6},{8,9},{9,8},{10,11... | collective-permute-start | bytes 688136 | tf_op jit(solution)/shard_map/ppermute | solution.py:296
  6.8 5.9 %collective-permute-start.1 = (bf16[224,128]{1,0:T(8,128)(2,1)S(1)}, bf16[224,128]{1,0:T(8,128)(2,1)S(1)}, u32[]{:S(2)}, u32[]{:S(2)}) collective-permute-start(bf16[224,128]{1,0:T(8,128)(2,1)S(1)} %get-tuple-element.33), channel_id=1, source_target_pairs={{0,2},{1,3},{2,0},{3,1},{4,6},{5,7},{6,4},{7,5},{8,10},{9,11},{10,... | collective-permute-start | bytes 172040 | tf_op jit(solution)/shard_map/ppermute | solution.py:296
  8.1 4.5 %collective-permute-start.2 = (bf16[224,128]{1,0:T(8,128)(2,1)S(1)}, bf16[224,128]{1,0:T(8,128)(2,1)S(1)}, u32[]{:S(2)}, u32[]{:S(2)}) collective-permute-start(bf16[224,128]{1,0:T(8,128)(2,1)S(1)} %get-tuple-element.34), channel_id=1, source_target_pairs={{0,4},{1,5},{2,6},{3,7},{4,0},{5,1},{6,2},{7,3},{8,12},{9,13},{10,... | collective-permute-start | bytes 172040 | tf_op jit(solution)/shard_map/ppermute | solution.py:296
  10.4 4.9 %collective-permute-start.3 = (bf16[224,128]{1,0:T(8,128)(2,1)S(1)}, bf16[224,128]{1,0:T(8,128)(2,1)S(1)}, u32[]{:S(2)}, u32[]{:S(2)}) collective-permute-start(bf16[224,128]{1,0:T(8,128)(2,1)S(1)} %get-tuple-element.35), channel_id=1, source_target_pairs={{0,6},{1,7},{2,4},{3,5},{4,2},{5,3},{6,0},{7,1},{8,14},{9,15},{10,... | collective-permute-start | bytes 172040 | tf_op jit(solution)/shard_map/ppermute | solution.py:296
  15.7 5.1 %collective-permute-start.5 = (bf16[32,1792]{1,0:T(8,128)(2,1)S(1)}, bf16[32,1792]{1,0:T(8,128)(2,1)S(1)}, u32[]{:S(2)}, u32[]{:S(2)}) collective-permute-start(bf16[32,1792]{1,0:T(8,128)(2,1)S(1)} %get-tuple-element.38.a_3_), channel_id=1, source_target_pairs={{0,8},{1,9},{10,18},{11,19},{20,28},{21,29}} | collective-permute-start | bytes 344072 | tf_op jit(solution)/shard_map/ppermute | solution.py:296
  16.4 15.3 %collective-permute-start.11 = (bf16[64,1792]{1,0:T(8,128)(2,1)S(1)}, bf16[64,1792]{1,0:T(8,128)(2,1)S(1)}, u32[]{:S(2)}, u32[]{:S(2)}) collective-permute-start(bf16[64,1792]{1,0:T(8,128)(2,1)S(1)} %get-tuple-element.44), channel_id=1, source_target_pairs={{0,16},{1,17},{10,26},{11,27}} | collective-permute-start | bytes 688136 | tf_op jit(solution)/shard_map/ppermute | solution.py:296
  17.1 14.6 %collective-permute-start.12 = (bf16[64,1792]{1,0:T(8,128)(2,1)S(1)}, bf16[64,1792]{1,0:T(8,128)(2,1)S(1)}, u32[]{:S(2)}, u32[]{:S(2)}) collective-permute-start(bf16[64,1792]{1,0:T(8,128)(2,1)S(1)} %get-tuple-element.44), channel_id=1, source_target_pairs={{0,24},{1,25}} | collective-permute-start | bytes 688136 | tf_op jit(solution)/shard_map/ppermute | solution.py:296
  18.4 4.5 %collective-permute-start.7 = (bf16[32,1792]{1,0:T(8,128)(2,1)S(1)}, bf16[32,1792]{1,0:T(8,128)(2,1)S(1)}, u32[]{:S(2)}, u32[]{:S(2)}) collective-permute-start(bf16[32,1792]{1,0:T(8,128)(2,1)S(1)} %get-tuple-element.41), channel_id=1, source_target_pairs={{0,8},{1,9},{10,18},{11,19},{20,28},{21,29}} | collective-permute-start | bytes 344072 | tf_op jit(solution)/shard_map/ppermute | solution.py:296
  20.8 10.8 %collective-permute-start.6 = (bf16[32,1792]{1,0:T(8,128)(2,1)S(1)}, bf16[32,1792]{1,0:T(8,128)(2,1)S(1)}, u32[]{:S(2)}, u32[]{:S(2)}) collective-permute-start(bf16[32,1792]{1,0:T(8,128)(2,1)S(1)} %shard_map.43), channel_id=1, source_target_pairs={{0,16},{1,17},{2,18},{3,19},{4,2},{5,3},{6,22},{7,23},{8,10},{9,11... | collective-permute-start | bytes 344072 | tf_op jit(solution)/shard_map/ppermute | solution.py:296
  22.9 11.4 %collective-permute-start.8 = (bf16[32,1792]{1,0:T(8,128)(2,1)S(1)}, bf16[32,1792]{1,0:T(8,128)(2,1)S(1)}, u32[]{:S(2)}, u32[]{:S(2)}) collective-permute-start(bf16[32,1792]{1,0:T(8,128)(2,1)S(1)} %shard_map.45), channel_id=1, source_target_pairs={{0,16},{1,17},{2,18},{3,19},{4,2},{5,3},{6,22},{7,23},{8,10},{9,11... | collective-permute-start | bytes 344072 | tf_op jit(solution)/shard_map/ppermute | solution.py:296
  30.4 6.0 %collective-permute-start.10 = (bf16[64,1792]{1,0:T(8,128)(2,1)S(1)}, bf16[64,1792]{1,0:T(8,128)(2,1)S(1)}, u32[]{:S(2)}, u32[]{:S(2)}) collective-permute-start(bf16[64,1792]{1,0:T(8,128)(2,1)S(1)} %get-tuple-element.37.a_0_._.a_1_), channel_id=1, source_target_pairs={{16,18},{17,19},{24,26},{25,27},{26,28},{27,29}} | collective-permute-start | bytes 688136 | tf_op jit(solution)/shard_map/ppermute | solution.py:296
  33.0 6.0 %collective-permute-start.13 = (bf16[64,1792]{1,0:T(8,128)(2,1)S(1)}, bf16[64,1792]{1,0:T(8,128)(2,1)S(1)}, u32[]{:S(2)}, u32[]{:S(2)}) collective-permute-start(bf16[64,1792]{1,0:T(8,128)(2,1)S(1)} %shard_map.47), channel_id=1, source_target_pairs={{16,18},{17,19},{24,26},{25,27},{26,28},{27,29}} | collective-permute-start | bytes 688136 | tf_op jit(solution)/shard_map/ppermute | solution.py:296
  34.3 4.7 %collective-permute-start.23 = (bf16[64,1792]{1,0:T(8,128)(2,1)S(1)}, bf16[64,1792]{1,0:T(8,128)(2,1)S(1)}, u32[]{:S(2)}, u32[]{:S(2)}) collective-permute-start(bf16[64,1792]{1,0:T(8,128)(2,1)S(1)} %get-tuple-element.53), channel_id=1, source_target_pairs={{10,26},{11,27}} | collective-permute-start | bytes 688136 | tf_op jit(solution)/shard_map/ppermute | solution.py:296
  35.0 2.0 %collective-permute-start.9 = (bf16[32,1792]{1,0:T(8,128)(2,1)S(1)}, bf16[32,1792]{1,0:T(8,128)(2,1)S(1)}, u32[]{:S(2)}, u32[]{:S(2)}) collective-permute-start(bf16[32,1792]{1,0:T(8,128)(2,1)S(1)} %get-tuple-element.42.a_3_), channel_id=1, source_target_pairs={{10,18},{11,19},{20,28},{21,29}} | collective-permute-start | bytes 344072 | tf_op jit(solution)/shard_map/ppermute | solution.py:296
  35.7 4.0 %collective-permute-start.15 = (bf16[32,1792]{1,0:T(8,128)(2,1)S(1)}, bf16[32,1792]{1,0:T(8,128)(2,1)S(1)}, u32[]{:S(2)}, u32[]{:S(2)}) collective-permute-start(bf16[32,1792]{1,0:T(8,128)(2,1)S(1)} %get-tuple-element.46), channel_id=1, source_target_pairs={{10,18},{11,19},{20,28},{21,29}} | collective-permute-start | bytes 344072 | tf_op jit(solution)/shard_map/ppermute | solution.py:296
  36.4 12.6 %collective-permute-start.22 = (bf16[64,1792]{1,0:T(8,128)(2,1)S(1)}, bf16[64,1792]{1,0:T(8,128)(2,1)S(1)}, u32[]{:S(2)}, u32[]{:S(2)}) collective-permute-start(bf16[64,1792]{1,0:T(8,128)(2,1)S(1)} %collective-permute-done.10.a_1_), channel_id=1, source_target_pairs={{26,28},{27,29}} | collective-permute-start | bytes 688136 | tf_op jit(solution)/shard_map/ppermute | solution.py:296
  39.0 4.4 %collective-permute-start.14 = (bf16[32,1792]{1,0:T(8,128)(2,1)S(1)}, bf16[32,1792]{1,0:T(8,128)(2,1)S(1)}, u32[]{:S(2)}, u32[]{:S(2)}) collective-permute-start(bf16[32,1792]{1,0:T(8,128)(2,1)S(1)} %shard_map.48), channel_id=1, source_target_pairs={{0,16},{1,17},{2,18},{3,19},{4,2},{5,3},{6,22},{7,23},{8,10},{9,11... | collective-permute-start | bytes 344072 | tf_op jit(solution)/shard_map/ppermute | solution.py:296
  39.0 11.9 %collective-permute-start.24 = (bf16[64,1792]{1,0:T(8,128)(2,1)S(1)}, bf16[64,1792]{1,0:T(8,128)(2,1)S(1)}, u32[]{:S(2)}, u32[]{:S(2)}) collective-permute-start(bf16[64,1792]{1,0:T(8,128)(2,1)S(1)} %shard_map.55), channel_id=1, source_target_pairs={{26,28},{27,29}} | collective-permute-start | bytes 688136 | tf_op jit(solution)/shard_map/ppermute | solution.py:296
  39.9 7.0 %collective-permute-start.16 = (bf16[32,1792]{1,0:T(8,128)(2,1)S(1)}, bf16[32,1792]{1,0:T(8,128)(2,1)S(1)}, u32[]{:S(2)}, u32[]{:S(2)}) collective-permute-start(bf16[32,1792]{1,0:T(8,128)(2,1)S(1)} %shard_map.50), channel_id=1, source_target_pairs={{0,16},{1,17},{2,18},{3,19},{4,2},{5,3},{6,22},{7,23},{8,10},{9,11... | collective-permute-start | bytes 344072 | tf_op jit(solution)/shard_map/ppermute | solution.py:296
  43.4 6.2 %collective-permute-start.21 = (bf16[32,1792]{1,0:T(8,128)(2,1)S(1)}, bf16[32,1792]{1,0:T(8,128)(2,1)S(1)}, u32[]{:S(2)}, u32[]{:S(2)}) collective-permute-start(bf16[32,1792]{1,0:T(8,128)(2,1)S(1)} %get-tuple-element.47.a_3_), channel_id=1, source_target_pairs={{20,28},{21,29}} | collective-permute-start | bytes 344072 | tf_op jit(solution)/shard_map/ppermute | solution.py:296
  47.6 3.5 %collective-permute-start.26 = (bf16[32,1792]{1,0:T(8,128)(2,1)S(1)}, bf16[32,1792]{1,0:T(8,128)(2,1)S(1)}, u32[]{:S(2)}, u32[]{:S(2)}) collective-permute-start(bf16[32,1792]{1,0:T(8,128)(2,1)S(1)} %get-tuple-element.54), channel_id=1, source_target_pairs={{20,28},{21,29}} | collective-permute-start | bytes 344072 | tf_op jit(solution)/shard_map/ppermute | solution.py:296
  48.2 6.4 %collective-permute-start.17 = (bf16[3,224,128]{2,1,0:T(8,128)(2,1)S(1)}, bf16[3,224,128]{2,1,0:T(8,128)(2,1)S(1)}, u32[]{:S(2)}, u32[]{:S(2)}) collective-permute-start(bf16[3,224,128]{2,1,0:T(8,128)(2,1)S(1)} %get-tuple-element.50), channel_id=1, source_target_pairs={{0,2},{1,3},{10,8},{11,9},{20,22},{21,23},{30,28},{31,29}} | collective-permute-start | bytes 516104 | tf_op jit(solution)/shard_map/ppermute | solution.py:296
  48.9 5.7 %collective-permute-start.18 = (bf16[3,224,128]{2,1,0:T(8,128)(2,1)S(1)}, bf16[3,224,128]{2,1,0:T(8,128)(2,1)S(1)}, u32[]{:S(2)}, u32[]{:S(2)}) collective-permute-start(bf16[3,224,128]{2,1,0:T(8,128)(2,1)S(1)} %get-tuple-element.51), channel_id=1, source_target_pairs={{0,4},{1,5},{10,14},{11,15},{20,16},{21,17},{30,26},{31,27}} | collective-permute-start | bytes 516104 | tf_op jit(solution)/shard_map/ppermute | solution.py:296
  49.6 9.9 %collective-permute-start.19 = (bf16[3,224,128]{2,1,0:T(8,128)(2,1)S(1)}, bf16[3,224,128]{2,1,0:T(8,128)(2,1)S(1)}, u32[]{:S(2)}, u32[]{:S(2)}) collective-permute-start(bf16[3,224,128]{2,1,0:T(8,128)(2,1)S(1)} %get-tuple-element.52), channel_id=1, source_target_pairs={{0,6},{1,7},{10,12},{11,13},{20,18},{21,19},{30,24},{31,25}} | collective-permute-start | bytes 516104 | tf_op jit(solution)/shard_map/ppermute | solution.py:296
  51.0 16.1 %collective-permute-start.25 = (bf16[32,1792]{1,0:T(8,128)(2,1)S(1)}, bf16[32,1792]{1,0:T(8,128)(2,1)S(1)}, u32[]{:S(2)}, u32[]{:S(2)}) collective-permute-start(bf16[32,1792]{1,0:T(8,128)(2,1)S(1)} %shard_map.56), channel_id=1, source_target_pairs={{0,16},{1,17},{2,18},{3,19},{4,2},{5,3},{6,22},{7,23},{8,10},{9,11... | collective-permute-start | bytes 344072 | tf_op jit(solution)/shard_map/ppermute | solution.py:296
  51.1 16.0 %collective-permute-start.27 = (bf16[32,1792]{1,0:T(8,128)(2,1)S(1)}, bf16[32,1792]{1,0:T(8,128)(2,1)S(1)}, u32[]{:S(2)}, u32[]{:S(2)}) collective-permute-start(bf16[32,1792]{1,0:T(8,128)(2,1)S(1)} %shard_map.58), channel_id=1, source_target_pairs={{0,16},{1,17},{2,18},{3,19},{4,2},{5,3},{6,22},{7,23},{8,10},{9,11... | collective-permute-start | bytes 344072 | tf_op jit(solution)/shard_map/ppermute | solution.py:296
  59.5 17.9 %collective-permute-start.20 = (bf16[3,224,128]{2,1,0:T(8,128)(2,1)S(1)}, bf16[3,224,128]{2,1,0:T(8,128)(2,1)S(1)}, u32[]{:S(2)}, u32[]{:S(2)}) collective-permute-start(bf16[3,224,128]{2,1,0:T(8,128)(2,1)S(1)} %shard_map.53.a_2_), channel_id=1, source_target_pairs={{0,1},{1,0},{2,3},{3,2},{4,5},{5,4},{6,7},{7,6},{8,9},{9,8},{10,11... | collective-permute-start | bytes 516104 | tf_op jit(solution)/shard_map/ppermute | solution.py:296
  67.1 2.8 %collective-permute-start.28 = (bf16[224,128]{1,0:T(8,128)(2,1)S(1)}, bf16[224,128]{1,0:T(8,128)(2,1)S(1)}, u32[]{:S(2)}, u32[]{:S(2)}) collective-permute-start(bf16[224,128]{1,0:T(8,128)(2,1)S(1)} %get-tuple-element.56), channel_id=1, source_target_pairs={{30,28},{31,29}} | collective-permute-start | bytes 172040 | tf_op jit(solution)/shard_map/ppermute | solution.py:296
  67.9 2.0 %collective-permute-start.29 = (bf16[224,128]{1,0:T(8,128)(2,1)S(1)}, bf16[224,128]{1,0:T(8,128)(2,1)S(1)}, u32[]{:S(2)}, u32[]{:S(2)}) collective-permute-start(bf16[224,128]{1,0:T(8,128)(2,1)S(1)} %get-tuple-element.57), channel_id=1, source_target_pairs={{30,26},{31,27}} | collective-permute-start | bytes 172040 | tf_op jit(solution)/shard_map/ppermute | solution.py:296
  68.6 7.3 %collective-permute-start.30 = (bf16[224,128]{1,0:T(8,128)(2,1)S(1)}, bf16[224,128]{1,0:T(8,128)(2,1)S(1)}, u32[]{:S(2)}, u32[]{:S(2)}) collective-permute-start(bf16[224,128]{1,0:T(8,128)(2,1)S(1)} %get-tuple-element.58), channel_id=1, source_target_pairs={{30,24},{31,25}} | collective-permute-start | bytes 172040 | tf_op jit(solution)/shard_map/ppermute | solution.py:296
  75.8 3.2 %collective-permute-start.31 = (bf16[1,224,128]{2,1,0:T(8,128)(2,1)S(1)}, bf16[1,224,128]{2,1,0:T(8,128)(2,1)S(1)}, u32[]{:S(2)}, u32[]{:S(2)}) collective-permute-start(bf16[1,224,128]{2,1,0:T(8,128)(2,1)S(1)} %shard_map.60.a_2_), channel_id=1, source_target_pairs={{0,1},{1,0},{2,3},{3,2},{4,5},{5,4},{6,7},{7,6},{8,9},{9,8},{10,11... | collective-permute-start | bytes 172040 | tf_op jit(solution)/shard_map/ppermute | solution.py:296
  (5 other events, 24.3 us)

commit v4 on v3

--- a/solution.py
+++ b/solution.py
@@ -248,11 +248,13 @@
     return jnp.where(lanes < width // 2, low, high)
 
 
-def put_early_kernel(count, ticks, starts_ref, grad_ref, mine_ref, other_ref, out_ref):
+def put_early_kernel(count, ticks, starts_ref, grad_ref, mine_ref, other_ref, out_ref, where_ref):
     r, _, h = place()
     width = mine_ref.shape[2]
     for s in range(count):
-        begin = pl.multiple_of(panel_at(starts_ref, count, s) * width, width)
+        panel = panel_at(starts_ref, count, s)
+        where_ref[s] = jnp.full(where_ref.shape[1:], panel.astype(F32))
+        begin = pl.multiple_of(panel * width, width)
 
         @pl.when(r < s)
         def _():
@@ -264,14 +266,15 @@
             out_ref[:, pl.ds(begin, width)] = join(mine_ref[t], other_ref[t], h)
 
 
-def put_last_kernel(count, ticks, starts_ref, _, mine_ref, other_ref, out_ref, joined, sem):
+def put_last_kernel(count, ticks, where_ref, _, mine_ref, other_ref, out_ref, joined, sem):
     r, _, h = place()
     width = mine_ref.shape[2]
     for s in range(count - ticks + 1):
-        begin = pl.multiple_of(panel_at(starts_ref, count, s) * width, width)
 
         @pl.when(r - s >= ticks - 1)
         def _():
+            panel = jnp.max(where_ref[s]).astype(jnp.int32)
+            begin = pl.multiple_of(panel * width, width)
             joined[...] = join(mine_ref[s], other_ref[s], h)
             copy = pltpu.make_async_copy(joined, out_ref.at[:, pl.ds(begin, width)], sem)
             copy.start()
@@ -310,9 +313,11 @@
 
         return move(array, target)
 
-    def to_next_row(array, tick):
+    def to_next_row(array):
         def target(r, z, h):
-            return (r + 1, z, h) if r == z and z >= tick and r + 1 < count else None
+            idle, far = range(z - 1, -1, -1), range(count - 1, z + 1, -1)
+            cycle = [z] + [z + 1] * (z + 1 < count) + [*far] + [*idle]
+            return cycle[(cycle.index(r) + 1) % count], z, h
 
         return move(array, target)
 
@@ -365,7 +370,7 @@
         scratch, flops,
     )
     turned = call(
-        turn_kernel, [shape((tile, tile), BF16)], (own_tile, other_tile, grad), [VM] * 3,
+        turn_kernel, [shape((tile, tile), BF16)], (own_tile, other_tile, pieces[0]), [VM] * 3,
     )[0]
     xs, before, sent_early = [], None, []
     for tick in range(ticks):
@@ -377,7 +382,7 @@
                 if final and not rest and c == CHUNKS - 1:
                     break
                 source, top = (rhs[c], 0) if tick else (grad, c * part)
-                joins = c == CHUNKS - 1 and CHUNKS > 1
+                joins = c == CHUNKS - 1 and CHUNKS > 1 and count - 2 > tick
                 outs = pair + ([shape((cols, tile), BF16)] if joins else [])
                 outs = outs if rest else outs[:1]
                 given = solved_b if joins else []
@@ -391,7 +396,7 @@
             solved.append(x)
             solved_b.append(xb)
             if rest:
-                downs.append(to_next_row(xb, tick))
+                downs.append(to_next_row(xb))
         xs.append(solved)
         results = solved
         if rest:
@@ -450,10 +455,11 @@
         [shape((ticks - 1, rows, width), BF16)], sent_early, [VM] * len(sent_early),
     )[0]
     theirs = cores(mine)
-    early = call(
+    early, where = call(
         lambda *a: put_early_kernel(count, ticks, *a),
-        [shape(gradient.shape, F32)], (starts, gradient, mine, theirs), [SM, VM, VM, VM],
-    )[0]
+        [shape(gradient.shape, F32), shape((count, 8, 128), F32)],
+        (starts, gradient, mine, theirs), [SM, VM, VM, VM],
+    )
     mine = call(
         lambda *a: pick_last_kernel(count, ticks, *a),
         [shape((count - ticks + 1, rows, width), BF16)], sent, [VM] * count,
@@ -462,7 +468,7 @@
     hbm = pl.BlockSpec(memory_space=pltpu.HBM)
     return call(
         lambda *a: put_last_kernel(count, ticks, *a),
-        [shape(gradient.shape, F32)], (starts, early, mine, theirs), [SM, hbm, VM, VM],
+        [shape(gradient.shape, F32)], (where, early, mine, theirs), [VM, hbm, VM, VM],
         [pltpu.VMEM((rows, width), F32), pltpu.SemaphoreType.DMA], 0, hbm, {1: 0},
     )[0]
 

time: 80.9 us -> 78.5 us (0.970)
  Pallas kernels: 8.37 us -> 6.9 us
    pallas_call x25, Pallas kernels: 8.37 us -> 6.9 us  [call(): pl.pallas_call(kernel, out_shape=outs, in_specs=specs, out_specs=[out_spe...]
  transfers between devices with their start and end apart: 32 -> 32, of which waited for: 7 -> 9; matrix products, arithmetic and copies ran while one was open for 0% -> 0% of each run, Pallas kernels for 8% -> 7%
where the time goes in v4:
time: 78.5 us; the launch traced here: 78.1 us
  starting transfers between devices  42.8 us (55%)
  waiting for transfers between devices  24.3 us (31%)
  Pallas kernels  6.9 us (9%)
  local copies, waits for them, and re-layouts  3.59 us (5%)
    ppermute x32, starting transfers between devices, move(): return lax.ppermute(array, ('row', 'col'), pairs)  42.8 us
    ppermute x32, waiting for transfers between devices, move(): return lax.ppermute(array, ('row', 'col'), pairs)  24.3 us
    pallas_call x25, Pallas kernels, call(): pl.pallas_call(kernel, out_shape=outs, in_specs=specs, out_specs=[out_spe...  6.9 us
    unnamed x10, local copies, waits for them, and re-layouts  3.59 us
  transfers between devices with their start and end apart: 32, of which 9 were waited for; matrix products, arithmetic and copies ran while one was open for 0% of the time, Pallas kernels for 7%

profile of v4, /device:TPU:7, one launch (start us, length us, event | category | flops | bytes accessed | tf_op | source)
XLA Modules:
  0.0 78.1 jit_solution(16796259996685008161)
XLA Ops:
  0.0 0.7 collective-permute-start.4
  0.7 1.0 %copy-done.1 = f32[224,512]{1,0:T(8,128)S(1)} copy-done((f32[224,512]{1,0:T(8,128)S(1)}, f32[224,512]{1,0:T(8,128)}, u32[]{:S(2)}) %copy-start.1) | copy-done | bytes 458776
  3.0 3.5 %collective-permute-done.a_1_ = bf16[4,224,128]{2,1,0:T(8,128)(2,1)S(1)} collective-permute-done((bf16[4,224,128]{2,1,0:T(8,128)(2,1)S(1)}, bf16[4,224,128]{2,1,0:T(8,128)(2,1)S(1)}, u32[]{:S(2)}, u32[]{:S(2)}) %collective-permute-start) | collective-permute-done | bytes 229408 | tf_op jit(solution)/shard_map/ppermute | solution.py:299
  6.8 1.4 %collective-permute-start.1 = (bf16[224,128]{1,0:T(8,128)(2,1)S(1)}, bf16[224,128]{1,0:T(8,128)(2,1)S(1)}, u32[]{:S(2)}, u32[]{:S(2)}) collective-permute-start(bf16[224,128]{1,0:T(8,128)(2,1)S(1)} %get-tuple-element.35), channel_id=1, source_target_pairs={{0,2},{1,3},{2,0},{3,1},{4,6},{5,7},{6,4},{7,5},{8,10},{9,11},{10,... | collective-permute-start | bytes 172040 | tf_op jit(solution)/shard_map/ppermute | solution.py:299
  8.1 2.3 %collective-permute-start.2 = (bf16[224,128]{1,0:T(8,128)(2,1)S(1)}, bf16[224,128]{1,0:T(8,128)(2,1)S(1)}, u32[]{:S(2)}, u32[]{:S(2)}) collective-permute-start(bf16[224,128]{1,0:T(8,128)(2,1)S(1)} %get-tuple-element.36), channel_id=1, source_target_pairs={{0,4},{1,5},{2,6},{3,7},{4,0},{5,1},{6,2},{7,3},{8,12},{9,13},{10,... | collective-permute-start | bytes 172040 | tf_op jit(solution)/shard_map/ppermute | solution.py:299
  10.4 1.9 %copy-done = bf16[1792,896]{1,0:T(8,128)(2,1)S(1)} copy-done((bf16[1792,896]{1,0:T(8,128)(2,1)S(1)}, bf16[1792,896]{1,0:T(8,128)(2,1)}, u32[]{:S(2)}) %copy-start) | copy-done | bytes 3211288
  12.7 2.7 %collective-permute-done.3.a_3_ = bf16[224,128]{1,0:T(8,128)(2,1)S(1)} collective-permute-done((bf16[224,128]{1,0:T(8,128)(2,1)S(1)}, bf16[224,128]{1,0:T(8,128)(2,1)S(1)}, u32[]{:S(2)}, u32[]{:S(2)}) %collective-permute-start.3) | collective-permute-done | bytes 57376 | tf_op jit(solution)/shard_map/ppermute | solution.py:299
  16.7 1.3 %collective-permute-start.12 = (bf16[64,1792]{1,0:T(8,128)(2,1)S(1)}, bf16[64,1792]{1,0:T(8,128)(2,1)S(1)}, u32[]{:S(2)}, u32[]{:S(2)}) collective-permute-start(bf16[64,1792]{1,0:T(8,128)(2,1)S(1)} %get-tuple-element.46), channel_id=1, source_target_pairs={{0,24},{1,25}} | collective-permute-start | bytes 688136 | tf_op jit(solution)/shard_map/ppermute | solution.py:299
  18.0 1.3 %collective-permute-start.7 = (bf16[32,1792]{1,0:T(8,128)(2,1)S(1)}, bf16[32,1792]{1,0:T(8,128)(2,1)S(1)}, u32[]{:S(2)}, u32[]{:S(2)}) collective-permute-start(bf16[32,1792]{1,0:T(8,128)(2,1)S(1)} %get-tuple-element.43), channel_id=1, source_target_pairs={{0,8},{1,9},{2,10},{3,11},{4,20},{5,21},{6,30},{7,31},{8,24},{9,25... | collective-permute-start | bytes 344072 | tf_op jit(solution)/shard_map/ppermute | solution.py:299
  19.2 1.7 %shard_map.42.a_2_.a_0_ = bf16[1792,1792]{1,0:T(8,128)(2,1)S(1)} custom-call(bf16[1792,896]{1,0:T(8,128)(2,1)S(1)} %shard_map.39.a_4_.a_1_.own_ref.a_2_, bf16[1792,896]{1,0:T(8,128)(2,1)S(1)} %collective-permute-done.4.a_5_.a_2_.other_ref.a_3_, bf16[224,128]{1,0:T(8,128)(2,1)S(1)} %get-tuple-element.34._.a_0_), custom_call_target="tpu_custom_call" | custom-call | bytes 6422528 | tf_op jit(solution)/shard_map/pallas_call | solution.py:19
  21.0 1.5 %collective-permute-start.6 = (bf16[32,1792]{1,0:T(8,128)(2,1)S(1)}, bf16[32,1792]{1,0:T(8,128)(2,1)S(1)}, u32[]{:S(2)}, u32[]{:S(2)}) collective-permute-start(bf16[32,1792]{1,0:T(8,128)(2,1)S(1)} %shard_map.43), channel_id=1, source_target_pairs={{0,16},{1,17},{2,18},{3,19},{4,2},{5,3},{6,22},{7,23},{8,10},{9,11... | collective-permute-start | bytes 344072 | tf_op jit(solution)/shard_map/ppermute | solution.py:299
  22.5 3.0 %collective-permute-done.7.a_0_ = bf16[32,1792]{1,0:T(8,128)(2,1)S(1)} collective-permute-done((bf16[32,1792]{1,0:T(8,128)(2,1)S(1)}, bf16[32,1792]{1,0:T(8,128)(2,1)S(1)}, u32[]{:S(2)}, u32[]{:S(2)}) %collective-permute-start.7) | collective-permute-done | bytes 114720 | tf_op jit(solution)/shard_map/ppermute | solution.py:299
  25.5 3.3 %collective-permute-start.8 = (bf16[32,1792]{1,0:T(8,128)(2,1)S(1)}, bf16[32,1792]{1,0:T(8,128)(2,1)S(1)}, u32[]{:S(2)}, u32[]{:S(2)}) collective-permute-start(bf16[32,1792]{1,0:T(8,128)(2,1)S(1)} %shard_map.45), channel_id=1, source_target_pairs={{0,16},{1,17},{2,18},{3,19},{4,2},{5,3},{6,22},{7,23},{8,10},{9,11... | collective-permute-start | bytes 344072 | tf_op jit(solution)/shard_map/ppermute | solution.py:299
  28.8 1.3 %collective-permute-start.10 = (bf16[64,1792]{1,0:T(8,128)(2,1)S(1)}, bf16[64,1792]{1,0:T(8,128)(2,1)S(1)}, u32[]{:S(2)}, u32[]{:S(2)}) collective-permute-start(bf16[64,1792]{1,0:T(8,128)(2,1)S(1)} %get-tuple-element.39.a_0_.a_1_), channel_id=1, source_target_pairs={{16,18},{17,19},{24,26},{25,27},{26,28},{27,29}} | collective-permute-start | bytes 688136 | tf_op jit(solution)/shard_map/ppermute | solution.py:299
  30.2 1.3 %shard_map.47 = bf16[64,1792]{1,0:T(8,128)(2,1)S(1)} custom-call(bf16[1792,1792]{1,0:T(8,128)(2,1)S(1)} %shard_map.42.a_2_.a_0_, bf16[64,1792]{1,0:T(8,128)(2,1)S(1)} %collective-permute-done.11.a_1_, bf16[64,1792]{1,0:T(8,128)(2,1)S(1)} %collective-permute-done.12.a_2_), custom_call_target="tpu_custom_call" | custom-call | flops 411041792 | bytes 229376 | tf_op jit(solution)/shard_map/pallas_call | solution.py:19
  31.4 1.3 %collective-permute-start.13 = (bf16[64,1792]{1,0:T(8,128)(2,1)S(1)}, bf16[64,1792]{1,0:T(8,128)(2,1)S(1)}, u32[]{:S(2)}, u32[]{:S(2)}) collective-permute-start(bf16[64,1792]{1,0:T(8,128)(2,1)S(1)} %shard_map.47), channel_id=1, source_target_pairs={{16,18},{17,19},{24,26},{25,27},{26,28},{27,29}} | collective-permute-start | bytes 688136 | tf_op jit(solution)/shard_map/ppermute | solution.py:299
  34.3 2.9 %collective-permute-done.9.a_0_ = bf16[32,1792]{1,0:T(8,128)(2,1)S(1)} collective-permute-done((bf16[32,1792]{1,0:T(8,128)(2,1)S(1)}, bf16[32,1792]{1,0:T(8,128)(2,1)S(1)}, u32[]{:S(2)}, u32[]{:S(2)}) %collective-permute-start.9) | collective-permute-done | bytes 114720 | tf_op jit(solution)/shard_map/ppermute | solution.py:299
  37.2 0.9 %collective-permute-start.24 = (bf16[64,1792]{1,0:T(8,128)(2,1)S(1)}, bf16[64,1792]{1,0:T(8,128)(2,1)S(1)}, u32[]{:S(2)}, u32[]{:S(2)}) collective-permute-start(bf16[64,1792]{1,0:T(8,128)(2,1)S(1)} %shard_map.55), channel_id=1, source_target_pairs={{26,28},{27,29}} | collective-permute-start | bytes 688136 | tf_op jit(solution)/shard_map/ppermute | solution.py:299
  38.4 1.8 %collective-permute-start.16 = (bf16[32,1792]{1,0:T(8,128)(2,1)S(1)}, bf16[32,1792]{1,0:T(8,128)(2,1)S(1)}, u32[]{:S(2)}, u32[]{:S(2)}) collective-permute-start(bf16[32,1792]{1,0:T(8,128)(2,1)S(1)} %shard_map.50), channel_id=1, source_target_pairs={{0,16},{1,17},{2,18},{3,19},{4,2},{5,3},{6,22},{7,23},{8,10},{9,11... | collective-permute-start | bytes 344072 | tf_op jit(solution)/shard_map/ppermute | solution.py:299
  40.2 1.4 %collective-permute-done.14.a_0_ = bf16[32,1792]{1,0:T(8,128)(2,1)S(1)} collective-permute-done((bf16[32,1792]{1,0:T(8,128)(2,1)S(1)}, bf16[32,1792]{1,0:T(8,128)(2,1)S(1)}, u32[]{:S(2)}, u32[]{:S(2)}) %collective-permute-start.14) | collective-permute-done | bytes 114720 | tf_op jit(solution)/shard_map/ppermute | solution.py:299
  41.6 2.6 %collective-permute-done.16.a_0_ = bf16[32,1792]{1,0:T(8,128)(2,1)S(1)} collective-permute-done((bf16[32,1792]{1,0:T(8,128)(2,1)S(1)}, bf16[32,1792]{1,0:T(8,128)(2,1)S(1)}, u32[]{:S(2)}, u32[]{:S(2)}) %collective-permute-start.16) | collective-permute-done | bytes 114720 | tf_op jit(solution)/shard_map/ppermute | solution.py:299
  45.6 1.3 %collective-permute-start.19 = (bf16[3,224,128]{2,1,0:T(8,128)(2,1)S(1)}, bf16[3,224,128]{2,1,0:T(8,128)(2,1)S(1)}, u32[]{:S(2)}, u32[]{:S(2)}) collective-permute-start(bf16[3,224,128]{2,1,0:T(8,128)(2,1)S(1)} %get-tuple-element.53), channel_id=1, source_target_pairs={{0,6},{1,7},{10,12},{11,13},{20,18},{21,19},{30,24},{31,25}} | collective-permute-start | bytes 516104 | tf_op jit(solution)/shard_map/ppermute | solution.py:299
  46.9 1.5 %collective-permute-start.25 = (bf16[32,1792]{1,0:T(8,128)(2,1)S(1)}, bf16[32,1792]{1,0:T(8,128)(2,1)S(1)}, u32[]{:S(2)}, u32[]{:S(2)}) collective-permute-start(bf16[32,1792]{1,0:T(8,128)(2,1)S(1)} %shard_map.56), channel_id=1, source_target_pairs={{0,16},{1,17},{2,18},{3,19},{4,2},{5,3},{6,22},{7,23},{8,10},{9,11... | collective-permute-start | bytes 344072 | tf_op jit(solution)/shard_map/ppermute | solution.py:299
  48.4 5.4 %collective-permute-start.27 = (bf16[32,1792]{1,0:T(8,128)(2,1)S(1)}, bf16[32,1792]{1,0:T(8,128)(2,1)S(1)}, u32[]{:S(2)}, u32[]{:S(2)}) collective-permute-start(bf16[32,1792]{1,0:T(8,128)(2,1)S(1)} %shard_map.58), channel_id=1, source_target_pairs={{0,16},{1,17},{2,18},{3,19},{4,2},{5,3},{6,22},{7,23},{8,10},{9,11... | collective-permute-start | bytes 344072 | tf_op jit(solution)/shard_map/ppermute | solution.py:299
  53.8 2.3 %collective-permute-done.19.a_3_ = bf16[3,224,128]{2,1,0:T(8,128)(2,1)S(1)} collective-permute-done((bf16[3,224,128]{2,1,0:T(8,128)(2,1)S(1)}, bf16[3,224,128]{2,1,0:T(8,128)(2,1)S(1)}, u32[]{:S(2)}, u32[]{:S(2)}) %collective-permute-start.19) | collective-permute-done | bytes 172064 | tf_op jit(solution)/shard_map/ppermute | solution.py:299
  56.1 8.6 %collective-permute-start.20 = (bf16[3,224,128]{2,1,0:T(8,128)(2,1)S(1)}, bf16[3,224,128]{2,1,0:T(8,128)(2,1)S(1)}, u32[]{:S(2)}, u32[]{:S(2)}) collective-permute-start(bf16[3,224,128]{2,1,0:T(8,128)(2,1)S(1)} %shard_map.53.a_2_), channel_id=1, source_target_pairs={{0,1},{1,0},{2,3},{3,2},{4,5},{5,4},{6,7},{7,6},{8,9},{9,8},{10,11... | collective-permute-start | bytes 516104 | tf_op jit(solution)/shard_map/ppermute | solution.py:299
  64.8 0.8 %collective-permute-start.28 = (bf16[224,128]{1,0:T(8,128)(2,1)S(1)}, bf16[224,128]{1,0:T(8,128)(2,1)S(1)}, u32[]{:S(2)}, u32[]{:S(2)}) collective-permute-start(bf16[224,128]{1,0:T(8,128)(2,1)S(1)} %get-tuple-element.60), channel_id=1, source_target_pairs={{30,28},{31,29}} | collective-permute-start | bytes 172040 | tf_op jit(solution)/shard_map/ppermute | solution.py:299
  66.3 1.3 %collective-permute-start.30 = (bf16[224,128]{1,0:T(8,128)(2,1)S(1)}, bf16[224,128]{1,0:T(8,128)(2,1)S(1)}, u32[]{:S(2)}, u32[]{:S(2)}) collective-permute-start(bf16[224,128]{1,0:T(8,128)(2,1)S(1)} %get-tuple-element.62), channel_id=1, source_target_pairs={{30,24},{31,25}} | collective-permute-start | bytes 172040 | tf_op jit(solution)/shard_map/ppermute | solution.py:299
  67.6 5.5 %collective-permute-done.30.a_3_ = bf16[224,128]{1,0:T(8,128)(2,1)S(1)} collective-permute-done((bf16[224,128]{1,0:T(8,128)(2,1)S(1)}, bf16[224,128]{1,0:T(8,128)(2,1)S(1)}, u32[]{:S(2)}, u32[]{:S(2)}) %collective-permute-start.30) | collective-permute-done | bytes 57376 | tf_op jit(solution)/shard_map/ppermute | solution.py:299
  73.1 2.4 %collective-permute-start.31 = (bf16[1,224,128]{2,1,0:T(8,128)(2,1)S(1)}, bf16[1,224,128]{2,1,0:T(8,128)(2,1)S(1)}, u32[]{:S(2)}, u32[]{:S(2)}) collective-permute-start(bf16[1,224,128]{2,1,0:T(8,128)(2,1)S(1)} %shard_map.60.a_2_), channel_id=1, source_target_pairs={{0,1},{1,0},{2,3},{3,2},{4,5},{5,4},{6,7},{7,6},{8,9},{9,8},{10,11... | collective-permute-start | bytes 172040 | tf_op jit(solution)/shard_map/ppermute | solution.py:299
  75.5 1.6 %shard_map.54 = (f32[224,512]{1,0:T(8,128)}, f32[4,8,128]{2,1,0:T(8,128)S(1)}) custom-call(s32[4]{0:T(128)S(1)} %copy-done.4, f32[224,512]{1,0:T(8,128)S(1)} %copy-done.2, bf16[3,224,128]{2,1,0:T(8,128)(2,1)S(1)} %shard_map.53.a_2_, bf16[3,224,128]{2,1,0:T(8,128)(2,1)S(1)} %collective-permute-done.20.a_3_), custom_call_target="tpu_custom_call" | custom-call | bytes 475136 | tf_op jit(solution)/shard_map/pallas_call | solution.py:19
  77.2 0.8 shard_map.61
  (67 shorter events, 7.1 us)
Async XLA Ops:
  0.0 15.4 %collective-permute-start.4 = (bf16[1792,896]{1,0:T(8,128)(2,1)}, bf16[1792,896]{1,0:T(8,128)(2,1)S(1)}, u32[]{:S(2)}, u32[]{:S(2)}) collective-permute-start(bf16[1792,896]{1,0:T(8,128)(2,1)} %tile_ref.1), channel_id=1, source_target_pairs={{0,1},{1,0},{2,3},{3,2},{4,5},{5,4},{6,7},{7,6},{8,9},{9,8},{10,11... | collective-permute-start | bytes 9633800 | tf_op jit(solution)/shard_map/ppermute | solution.py:299
  3.0 3.6 %collective-permute-start = (bf16[4,224,128]{2,1,0:T(8,128)(2,1)S(1)}, bf16[4,224,128]{2,1,0:T(8,128)(2,1)S(1)}, u32[]{:S(2)}, u32[]{:S(2)}) collective-permute-start(bf16[4,224,128]{2,1,0:T(8,128)(2,1)S(1)} %shard_map.37.a_0_), channel_id=1, source_target_pairs={{0,1},{1,0},{2,3},{3,2},{4,5},{5,4},{6,7},{7,6},{8,9},{9,8},{10,11... | collective-permute-start | bytes 688136 | tf_op jit(solution)/shard_map/ppermute | solution.py:299
  6.8 5.9 %collective-permute-start.1 = (bf16[224,128]{1,0:T(8,128)(2,1)S(1)}, bf16[224,128]{1,0:T(8,128)(2,1)S(1)}, u32[]{:S(2)}, u32[]{:S(2)}) collective-permute-start(bf16[224,128]{1,0:T(8,128)(2,1)S(1)} %get-tuple-element.35), channel_id=1, source_target_pairs={{0,2},{1,3},{2,0},{3,1},{4,6},{5,7},{6,4},{7,5},{8,10},{9,11},{10,... | collective-permute-start | bytes 172040 | tf_op jit(solution)/shard_map/ppermute | solution.py:299
  8.1 4.5 %collective-permute-start.2 = (bf16[224,128]{1,0:T(8,128)(2,1)S(1)}, bf16[224,128]{1,0:T(8,128)(2,1)S(1)}, u32[]{:S(2)}, u32[]{:S(2)}) collective-permute-start(bf16[224,128]{1,0:T(8,128)(2,1)S(1)} %get-tuple-element.36), channel_id=1, source_target_pairs={{0,4},{1,5},{2,6},{3,7},{4,0},{5,1},{6,2},{7,3},{8,12},{9,13},{10,... | collective-permute-start | bytes 172040 | tf_op jit(solution)/shard_map/ppermute | solution.py:299
  10.4 4.9 %collective-permute-start.3 = (bf16[224,128]{1,0:T(8,128)(2,1)S(1)}, bf16[224,128]{1,0:T(8,128)(2,1)S(1)}, u32[]{:S(2)}, u32[]{:S(2)}) collective-permute-start(bf16[224,128]{1,0:T(8,128)(2,1)S(1)} %get-tuple-element.37), channel_id=1, source_target_pairs={{0,6},{1,7},{2,4},{3,5},{4,2},{5,3},{6,0},{7,1},{8,14},{9,15},{10,... | collective-permute-start | bytes 172040 | tf_op jit(solution)/shard_map/ppermute | solution.py:299
  15.7 5.3 %collective-permute-start.5 = (bf16[32,1792]{1,0:T(8,128)(2,1)S(1)}, bf16[32,1792]{1,0:T(8,128)(2,1)S(1)}, u32[]{:S(2)}, u32[]{:S(2)}) collective-permute-start(bf16[32,1792]{1,0:T(8,128)(2,1)S(1)} %get-tuple-element.40.a_3_), channel_id=1, source_target_pairs={{0,8},{1,9},{2,10},{3,11},{4,20},{5,21},{6,30},{7,31},{8,24},{9,25... | collective-permute-start | bytes 344072 | tf_op jit(solution)/shard_map/ppermute | solution.py:299
  16.0 14.1 %collective-permute-start.11 = (bf16[64,1792]{1,0:T(8,128)(2,1)S(1)}, bf16[64,1792]{1,0:T(8,128)(2,1)S(1)}, u32[]{:S(2)}, u32[]{:S(2)}) collective-permute-start(bf16[64,1792]{1,0:T(8,128)(2,1)S(1)} %get-tuple-element.46), channel_id=1, source_target_pairs={{0,16},{1,17},{10,26},{11,27}} | collective-permute-start | bytes 688136 | tf_op jit(solution)/shard_map/ppermute | solution.py:299
  16.7 13.5 %collective-permute-start.12 = (bf16[64,1792]{1,0:T(8,128)(2,1)S(1)}, bf16[64,1792]{1,0:T(8,128)(2,1)S(1)}, u32[]{:S(2)}, u32[]{:S(2)}) collective-permute-start(bf16[64,1792]{1,0:T(8,128)(2,1)S(1)} %get-tuple-element.46), channel_id=1, source_target_pairs={{0,24},{1,25}} | collective-permute-start | bytes 688136 | tf_op jit(solution)/shard_map/ppermute | solution.py:299
  18.0 7.5 %collective-permute-start.7 = (bf16[32,1792]{1,0:T(8,128)(2,1)S(1)}, bf16[32,1792]{1,0:T(8,128)(2,1)S(1)}, u32[]{:S(2)}, u32[]{:S(2)}) collective-permute-start(bf16[32,1792]{1,0:T(8,128)(2,1)S(1)} %get-tuple-element.43), channel_id=1, source_target_pairs={{0,8},{1,9},{2,10},{3,11},{4,20},{5,21},{6,30},{7,31},{8,24},{9,25... | collective-permute-start | bytes 344072 | tf_op jit(solution)/shard_map/ppermute | solution.py:299
  21.0 9.1 %collective-permute-start.6 = (bf16[32,1792]{1,0:T(8,128)(2,1)S(1)}, bf16[32,1792]{1,0:T(8,128)(2,1)S(1)}, u32[]{:S(2)}, u32[]{:S(2)}) collective-permute-start(bf16[32,1792]{1,0:T(8,128)(2,1)S(1)} %shard_map.43), channel_id=1, source_target_pairs={{0,16},{1,17},{2,18},{3,19},{4,2},{5,3},{6,22},{7,23},{8,10},{9,11... | collective-permute-start | bytes 344072 | tf_op jit(solution)/shard_map/ppermute | solution.py:299
  25.5 7.2 %collective-permute-start.8 = (bf16[32,1792]{1,0:T(8,128)(2,1)S(1)}, bf16[32,1792]{1,0:T(8,128)(2,1)S(1)}, u32[]{:S(2)}, u32[]{:S(2)}) collective-permute-start(bf16[32,1792]{1,0:T(8,128)(2,1)S(1)} %shard_map.45), channel_id=1, source_target_pairs={{0,16},{1,17},{2,18},{3,19},{4,2},{5,3},{6,22},{7,23},{8,10},{9,11... | collective-permute-start | bytes 344072 | tf_op jit(solution)/shard_map/ppermute | solution.py:299
  28.8 4.8 %collective-permute-start.10 = (bf16[64,1792]{1,0:T(8,128)(2,1)S(1)}, bf16[64,1792]{1,0:T(8,128)(2,1)S(1)}, u32[]{:S(2)}, u32[]{:S(2)}) collective-permute-start(bf16[64,1792]{1,0:T(8,128)(2,1)S(1)} %get-tuple-element.39.a_0_.a_1_), channel_id=1, source_target_pairs={{16,18},{17,19},{24,26},{25,27},{26,28},{27,29}} | collective-permute-start | bytes 688136 | tf_op jit(solution)/shard_map/ppermute | solution.py:299
  31.4 5.7 %collective-permute-start.13 = (bf16[64,1792]{1,0:T(8,128)(2,1)S(1)}, bf16[64,1792]{1,0:T(8,128)(2,1)S(1)}, u32[]{:S(2)}, u32[]{:S(2)}) collective-permute-start(bf16[64,1792]{1,0:T(8,128)(2,1)S(1)} %shard_map.47), channel_id=1, source_target_pairs={{16,18},{17,19},{24,26},{25,27},{26,28},{27,29}} | collective-permute-start | bytes 688136 | tf_op jit(solution)/shard_map/ppermute | solution.py:299
  32.8 4.4 %collective-permute-start.23 = (bf16[64,1792]{1,0:T(8,128)(2,1)S(1)}, bf16[64,1792]{1,0:T(8,128)(2,1)S(1)}, u32[]{:S(2)}, u32[]{:S(2)}) collective-permute-start(bf16[64,1792]{1,0:T(8,128)(2,1)S(1)} %get-tuple-element.57), channel_id=1, source_target_pairs={{10,26},{11,27}} | collective-permute-start | bytes 688136 | tf_op jit(solution)/shard_map/ppermute | solution.py:299
  33.4 3.7 %collective-permute-start.9 = (bf16[32,1792]{1,0:T(8,128)(2,1)S(1)}, bf16[32,1792]{1,0:T(8,128)(2,1)S(1)}, u32[]{:S(2)}, u32[]{:S(2)}) collective-permute-start(bf16[32,1792]{1,0:T(8,128)(2,1)S(1)} %get-tuple-element.44.a_3_), channel_id=1, source_target_pairs={{0,8},{1,9},{2,10},{3,11},{4,20},{5,21},{6,30},{7,31},{8,24},{9,25... | collective-permute-start | bytes 344072 | tf_op jit(solution)/shard_map/ppermute | solution.py:299
  33.5 4.9 %collective-permute-start.15 = (bf16[32,1792]{1,0:T(8,128)(2,1)S(1)}, bf16[32,1792]{1,0:T(8,128)(2,1)S(1)}, u32[]{:S(2)}, u32[]{:S(2)}) collective-permute-start(bf16[32,1792]{1,0:T(8,128)(2,1)S(1)} %get-tuple-element.48), channel_id=1, source_target_pairs={{0,8},{1,9},{2,10},{3,11},{4,20},{5,21},{6,30},{7,31},{8,24},{9,25... | collective-permute-start | bytes 344072 | tf_op jit(solution)/shard_map/ppermute | solution.py:299
  33.6 11.3 %collective-permute-start.22 = (bf16[64,1792]{1,0:T(8,128)(2,1)S(1)}, bf16[64,1792]{1,0:T(8,128)(2,1)S(1)}, u32[]{:S(2)}, u32[]{:S(2)}) collective-permute-start(bf16[64,1792]{1,0:T(8,128)(2,1)S(1)} %collective-permute-done.10.a_1_), channel_id=1, source_target_pairs={{26,28},{27,29}} | collective-permute-start | bytes 688136 | tf_op jit(solution)/shard_map/ppermute | solution.py:299
  37.1 4.4 %collective-permute-start.14 = (bf16[32,1792]{1,0:T(8,128)(2,1)S(1)}, bf16[32,1792]{1,0:T(8,128)(2,1)S(1)}, u32[]{:S(2)}, u32[]{:S(2)}) collective-permute-start(bf16[32,1792]{1,0:T(8,128)(2,1)S(1)} %shard_map.48), channel_id=1, source_target_pairs={{0,16},{1,17},{2,18},{3,19},{4,2},{5,3},{6,22},{7,23},{8,10},{9,11... | collective-permute-start | bytes 344072 | tf_op jit(solution)/shard_map/ppermute | solution.py:299
  37.2 9.7 %collective-permute-start.24 = (bf16[64,1792]{1,0:T(8,128)(2,1)S(1)}, bf16[64,1792]{1,0:T(8,128)(2,1)S(1)}, u32[]{:S(2)}, u32[]{:S(2)}) collective-permute-start(bf16[64,1792]{1,0:T(8,128)(2,1)S(1)} %shard_map.55), channel_id=1, source_target_pairs={{26,28},{27,29}} | collective-permute-start | bytes 688136 | tf_op jit(solution)/shard_map/ppermute | solution.py:299
  38.4 5.8 %collective-permute-start.16 = (bf16[32,1792]{1,0:T(8,128)(2,1)S(1)}, bf16[32,1792]{1,0:T(8,128)(2,1)S(1)}, u32[]{:S(2)}, u32[]{:S(2)}) collective-permute-start(bf16[32,1792]{1,0:T(8,128)(2,1)S(1)} %shard_map.50), channel_id=1, source_target_pairs={{0,16},{1,17},{2,18},{3,19},{4,2},{5,3},{6,22},{7,23},{8,10},{9,11... | collective-permute-start | bytes 344072 | tf_op jit(solution)/shard_map/ppermute | solution.py:299
  41.6 4.0 %collective-permute-start.21 = (bf16[32,1792]{1,0:T(8,128)(2,1)S(1)}, bf16[32,1792]{1,0:T(8,128)(2,1)S(1)}, u32[]{:S(2)}, u32[]{:S(2)}) collective-permute-start(bf16[32,1792]{1,0:T(8,128)(2,1)S(1)} %get-tuple-element.56), channel_id=1, source_target_pairs={{0,8},{1,9},{2,10},{3,11},{4,20},{5,21},{6,30},{7,31},{8,24},{9,25... | collective-permute-start | bytes 344072 | tf_op jit(solution)/shard_map/ppermute | solution.py:299
  44.2 4.2 %collective-permute-start.26 = (bf16[32,1792]{1,0:T(8,128)(2,1)S(1)}, bf16[32,1792]{1,0:T(8,128)(2,1)S(1)}, u32[]{:S(2)}, u32[]{:S(2)}) collective-permute-start(bf16[32,1792]{1,0:T(8,128)(2,1)S(1)} %get-tuple-element.58), channel_id=1, source_target_pairs={{0,8},{1,9},{2,10},{3,11},{4,20},{5,21},{6,30},{7,31},{8,24},{9,25... | collective-permute-start | bytes 344072 | tf_op jit(solution)/shard_map/ppermute | solution.py:299
  44.2 9.6 %collective-permute-start.17 = (bf16[3,224,128]{2,1,0:T(8,128)(2,1)S(1)}, bf16[3,224,128]{2,1,0:T(8,128)(2,1)S(1)}, u32[]{:S(2)}, u32[]{:S(2)}) collective-permute-start(bf16[3,224,128]{2,1,0:T(8,128)(2,1)S(1)} %get-tuple-element.51), channel_id=1, source_target_pairs={{0,2},{1,3},{10,8},{11,9},{20,22},{21,23},{30,28},{31,29}} | collective-permute-start | bytes 516104 | tf_op jit(solution)/shard_map/ppermute | solution.py:299
  44.9 8.9 %collective-permute-start.18 = (bf16[3,224,128]{2,1,0:T(8,128)(2,1)S(1)}, bf16[3,224,128]{2,1,0:T(8,128)(2,1)S(1)}, u32[]{:S(2)}, u32[]{:S(2)}) collective-permute-start(bf16[3,224,128]{2,1,0:T(8,128)(2,1)S(1)} %get-tuple-element.52), channel_id=1, source_target_pairs={{0,4},{1,5},{10,14},{11,15},{20,16},{21,17},{30,26},{31,27}} | collective-permute-start | bytes 516104 | tf_op jit(solution)/shard_map/ppermute | solution.py:299
  45.6 10.5 %collective-permute-start.19 = (bf16[3,224,128]{2,1,0:T(8,128)(2,1)S(1)}, bf16[3,224,128]{2,1,0:T(8,128)(2,1)S(1)}, u32[]{:S(2)}, u32[]{:S(2)}) collective-permute-start(bf16[3,224,128]{2,1,0:T(8,128)(2,1)S(1)} %get-tuple-element.53), channel_id=1, source_target_pairs={{0,6},{1,7},{10,12},{11,13},{20,18},{21,19},{30,24},{31,25}} | collective-permute-start | bytes 516104 | tf_op jit(solution)/shard_map/ppermute | solution.py:299
  46.9 17.8 %collective-permute-start.25 = (bf16[32,1792]{1,0:T(8,128)(2,1)S(1)}, bf16[32,1792]{1,0:T(8,128)(2,1)S(1)}, u32[]{:S(2)}, u32[]{:S(2)}) collective-permute-start(bf16[32,1792]{1,0:T(8,128)(2,1)S(1)} %shard_map.56), channel_id=1, source_target_pairs={{0,16},{1,17},{2,18},{3,19},{4,2},{5,3},{6,22},{7,23},{8,10},{9,11... | collective-permute-start | bytes 344072 | tf_op jit(solution)/shard_map/ppermute | solution.py:299
  48.4 16.3 %collective-permute-start.27 = (bf16[32,1792]{1,0:T(8,128)(2,1)S(1)}, bf16[32,1792]{1,0:T(8,128)(2,1)S(1)}, u32[]{:S(2)}, u32[]{:S(2)}) collective-permute-start(bf16[32,1792]{1,0:T(8,128)(2,1)S(1)} %shard_map.58), channel_id=1, source_target_pairs={{0,16},{1,17},{2,18},{3,19},{4,2},{5,3},{6,22},{7,23},{8,10},{9,11... | collective-permute-start | bytes 344072 | tf_op jit(solution)/shard_map/ppermute | solution.py:299
  56.1 19.4 %collective-permute-start.20 = (bf16[3,224,128]{2,1,0:T(8,128)(2,1)S(1)}, bf16[3,224,128]{2,1,0:T(8,128)(2,1)S(1)}, u32[]{:S(2)}, u32[]{:S(2)}) collective-permute-start(bf16[3,224,128]{2,1,0:T(8,128)(2,1)S(1)} %shard_map.53.a_2_), channel_id=1, source_target_pairs={{0,1},{1,0},{2,3},{3,2},{4,5},{5,4},{6,7},{7,6},{8,9},{9,8},{10,11... | collective-permute-start | bytes 516104 | tf_op jit(solution)/shard_map/ppermute | solution.py:299
  64.8 2.8 %collective-permute-start.28 = (bf16[224,128]{1,0:T(8,128)(2,1)S(1)}, bf16[224,128]{1,0:T(8,128)(2,1)S(1)}, u32[]{:S(2)}, u32[]{:S(2)}) collective-permute-start(bf16[224,128]{1,0:T(8,128)(2,1)S(1)} %get-tuple-element.60), channel_id=1, source_target_pairs={{30,28},{31,29}} | collective-permute-start | bytes 172040 | tf_op jit(solution)/shard_map/ppermute | solution.py:299
  65.6 2.0 %collective-permute-start.29 = (bf16[224,128]{1,0:T(8,128)(2,1)S(1)}, bf16[224,128]{1,0:T(8,128)(2,1)S(1)}, u32[]{:S(2)}, u32[]{:S(2)}) collective-permute-start(bf16[224,128]{1,0:T(8,128)(2,1)S(1)} %get-tuple-element.61), channel_id=1, source_target_pairs={{30,26},{31,27}} | collective-permute-start | bytes 172040 | tf_op jit(solution)/shard_map/ppermute | solution.py:299
  66.3 6.8 %collective-permute-start.30 = (bf16[224,128]{1,0:T(8,128)(2,1)S(1)}, bf16[224,128]{1,0:T(8,128)(2,1)S(1)}, u32[]{:S(2)}, u32[]{:S(2)}) collective-permute-start(bf16[224,128]{1,0:T(8,128)(2,1)S(1)} %get-tuple-element.62), channel_id=1, source_target_pairs={{30,24},{31,25}} | collective-permute-start | bytes 172040 | tf_op jit(solution)/shard_map/ppermute | solution.py:299
  73.1 4.1 %collective-permute-start.31 = (bf16[1,224,128]{2,1,0:T(8,128)(2,1)S(1)}, bf16[1,224,128]{2,1,0:T(8,128)(2,1)S(1)}, u32[]{:S(2)}, u32[]{:S(2)}) collective-permute-start(bf16[1,224,128]{2,1,0:T(8,128)(2,1)S(1)} %shard_map.60.a_2_), channel_id=1, source_target_pairs={{0,1},{1,0},{2,3},{3,2},{4,5},{5,4},{6,7},{7,6},{8,9},{9,8},{10,11... | collective-permute-start | bytes 172040 | tf_op jit(solution)/shard_map/ppermute | solution.py:299
  (5 other events, 25.2 us)
